TPU v7x, 256 devices: a whole 4x4x8 slice. The times are simulated.
256 devices in a mesh: tok: 64 (over y, z, core), head: 4 (over x).
Axes of the slice: x: 4, y: 4, z: 8, core: 2. Of those that a mesh axis runs over, the one named last changes fastest.
Arguments:
- query_rows: bfloat16 [32768, 4, 1024], P('tok', 'head'), may hold values from -6 to 6
- key_rows: bfloat16 [32768, 4, 128], P('tok', 'head'), may hold values from -6 to 6
- value_rows: bfloat16 [32768, 4, 128], P('tok', 'head'), may hold values from -6 to 6
- output_gradient: bfloat16 [32768, 4, 1024], P('tok', 'head'), may hold values from -6 to 6
- row_logsumexp: bfloat16 [4, 8, 32768], P('head', None, 'tok'), may hold values from 3 to 7
- row_delta_sums: bfloat16 [4, 8, 32768], P('head', None, 'tok'), may hold values from -5 to 5
- segments: int32 [32768], replicated, may hold values from 0 to 32767, as said below
- query_key_value_weight: bfloat16 [4096, 4, 1280], P('tok', 'head'), may hold values from -0.09375 to 0.09375
Outputs:
- grad_input: bfloat16 [32768, 4096], P('tok', 'head')
Inputs may be any that keep to these rules, and one draw needn't show every extreme that they name: `segments`: numbers never fall along the tokens, and every document lies inside one window of 512 consecutive tokens.
All inputs are finite; a program needn't handle non-finite values.
Results may differ from a plain program's by a relative error of at most 0.012.
Values may be sent and summed in bfloat16 or wider, within the bound.
No kernel may reach another device: no remote copies, remote signals or barrier semaphores. Data moves between devices by JAX's collectives and lax.ppermute only.
A program may use at most 128 MiB of HBM per device.

v0:
```python
import jax
import jax.numpy as jnp
import numpy as np
from jax import lax
from jax.sharding import PartitionSpec as P

BLOCK = 128


def pair_lists(block_count):
    query_list = []
    key_list = []
    for query_block in range(block_count):
        for key_block in range(query_block + 1):
            query_list.append(query_block)
            key_list.append(key_block)
    return (np.array(query_list, np.int32), np.array(key_list, np.int32))


def live_pairs(seg_window, query_list, key_list, tile_rows):
    first_seg = jnp.take(seg_window, query_list * tile_rows)
    last_seg = jnp.take(seg_window, key_list * tile_rows + tile_rows - 1)
    return (first_seg == last_seg) | jnp.asarray(query_list == key_list)


def pair_grads(query_tile, dout_tile, key_tile, value_tile, lse_tile, delta_tile, allowed):
    tile_rows, groups, query_width = query_tile.shape
    head_size = key_tile.shape[2]
    heads_per_group = query_width // head_size
    query_heads = query_tile.reshape(tile_rows, groups, heads_per_group, head_size)
    dout_heads = dout_tile.reshape(tile_rows, groups, heads_per_group, head_size)
    scores = jnp.einsum(
        "agrd,bgd->grab", query_heads, key_tile, preferred_element_type=jnp.float32
    ) * head_size ** (-0.5)
    logits = scores - lse_tile.astype(jnp.float32)[:, :, :, None]
    soft_probs = jnp.where(allowed[None, None], jnp.exp(logits), 0.0)
    probs_low = soft_probs.astype(jnp.bfloat16)
    value_gradient = jnp.einsum(
        "grab,agrd->bgd", probs_low, dout_heads, preferred_element_type=jnp.float32
    )
    grad_prob = jnp.einsum(
        "agrd,bgd->grab", dout_heads, value_tile, preferred_element_type=jnp.float32
    )
    grad_score = (soft_probs * (grad_prob - delta_tile.astype(jnp.float32)[:, :, :, None])).astype(
        jnp.bfloat16
    )
    query_gradient = jnp.einsum(
        "grab,bgd->agrd", grad_score, key_tile, preferred_element_type=jnp.float32
    )
    key_gradient = jnp.einsum(
        "grab,agrd->bgd", grad_score, query_heads, preferred_element_type=jnp.float32
    )
    return (query_gradient.reshape(tile_rows, groups, query_width), key_gradient, value_gradient)


def on_device(
    query_rows,
    key_rows,
    value_rows,
    output_gradient,
    row_logsumexp,
    row_delta_sums,
    segments,
    query_key_value_weight,
):
    weight_whole = lax.all_gather(query_key_value_weight, "tok", axis=0, tiled=True)
    window, kv_dev, query_width = query_rows.shape
    head_size = key_rows.shape[2]
    tile_rows = BLOCK
    block_count = window // tile_rows
    query_list, key_list = pair_lists(block_count)
    query_table = jnp.asarray(query_list)
    key_table = jnp.asarray(key_list)
    myself = lax.axis_index("tok")
    own_seg = lax.dynamic_slice_in_dim(segments, myself * window, window)
    own_live = live_pairs(own_seg, query_list, key_list, tile_rows)
    block_ids = jnp.arange(block_count, dtype=jnp.int32)
    query_match = (query_table[:, None] == block_ids[None, :]) & own_live[:, None]
    key_match = key_table[:, None] == block_ids[None, :]
    block_local = jnp.any(query_match[:, :, None] & key_match[:, None, :], axis=0)
    token_local = jnp.repeat(jnp.repeat(block_local, tile_rows, axis=0), tile_rows, axis=1)
    offsets = jnp.arange(window, dtype=jnp.int32)
    allowed_all = (
        (own_seg[:, None] == own_seg[None, :])
        & (offsets[None, :] <= offsets[:, None])
        & token_local
    )
    local_out = pair_grads(
        query_rows,
        output_gradient,
        key_rows,
        value_rows,
        row_logsumexp,
        row_delta_sums,
        allowed_all,
    )
    acc_query = local_out[0].reshape(block_count, tile_rows, kv_dev, query_width)
    acc_key = local_out[1].reshape(block_count, tile_rows, kv_dev, head_size)
    acc_value = local_out[2].reshape(block_count, tile_rows, kv_dev, head_size)
    score_scale = head_size ** (-0.5)
    query_gradient = (acc_query * score_scale).reshape(window, kv_dev, query_width)
    key_gradient = (acc_key * score_scale).reshape(window, kv_dev, head_size)
    value_gradient = acc_value.reshape(window, kv_dev, head_size)
    stacked_gradients = (
        jnp.concatenate([query_gradient, key_gradient, value_gradient], axis=2)
        .astype(jnp.bfloat16)
        .reshape(window, -1)
    )
    flat_piece = weight_whole.reshape(weight_whole.shape[0], -1)
    partial_sum = lax.dot_general(
        stacked_gradients, flat_piece, (((1,), (1,)), ((), ())), preferred_element_type=jnp.float32
    )
    summed = lax.psum_scatter(
        partial_sum.astype(jnp.bfloat16), "head", scatter_dimension=1, tiled=True
    )
    return summed


def solution(mesh):
    placed = (
        P("tok", "head", None),
        P("tok", "head", None),
        P("tok", "head", None),
        P("tok", "head", None),
        P("head", None, "tok"),
        P("head", None, "tok"),
        P(),
        P("tok", "head", None),
    )
    return jax.shard_map(
        on_device, mesh=mesh, in_specs=placed, out_specs=P("tok", "head"), check_vma=False
    )
```

profile of v0, /device:TPU:8, one launch (start us, length us, event | category | flops | bytes accessed | tf_op | source)
XLA Modules:
  0.0 164.1 jit_solution(10995759829409910202)
XLA Ops:
  6.5 0.0 copy-start
  6.5 0.0 copy-start.1
  6.5 0.0 all-gather.2.cloned.1.call-start
  6.5 0.7 all-gather.2.cloned.1.call-update
  7.3 0.0 reduce-scatter.2.cloned.1.call-start
  7.3 0.8 dynamic_slice.3
  8.1 0.7 pad_clamp_fusion.1
  8.7 0.7 gather_fusion
  9.4 0.7 pad_clamp_fusion
  10.1 0.7 gather_fusion.1
  10.7 0.7 compare_or_fusion
  11.4 0.7 iota_compare_fusion.1
  12.1 0.2 and_reduce_fusion
  12.2 0.1 copy.22
  12.3 0.1 broadcast_bitcast_fusion
  12.4 0.2 fusion.29
  12.7 1.5 copy.36
  14.2 1.5 copy.37
  15.7 0.7 bitcast_convert_fusion.1
  16.4 0.7 bitcast_convert_fusion
  17.1 0.0 copy-done
  17.1 1.2 fusion.32
  18.3 0.0 copy-done.1
  18.3 2.8 %fusion.11 = bf16[8,512,512]{1,2,0:T(8,128)(2,1)S(1)} fusion(f32[512,512,8]{1,0,2:T(8,128)S(1)} %fusion.32, f32[8,512]{1,0:T(8,128)S(1)} %bitcast_convert_fusion, f32[8,512]{1,0:T(8,128)S(1)} %bitcast_convert_fusion.1, pred[512,512]{0,1:T(8,128)(4,1)S(1)} %fusion.29, bf16[512,8,128]{0,2,1:T(8,128)(2,1)S(1)} %bitcast.99, bf16[512,1,128]{2,0,1:T(8,128)(2,1)S(1)} %copy-done.1), kind=kOutput, calls=%fused_computation.13 | convolution fusion | flops 549453824 | bytes 14057472 | tf_op jit(solution)/shard_map/agrd,bgd->grab/dot_general | solution.py:41
  21.2 0.8 multiply_convert_fusion
  22.0 2.1 %fusion.27 = bf16[512,128]{0,1:T(8,128)(2,1)} fusion(bf16[8,512,512]{1,2,0:T(8,128)(2,1)S(1)} %fusion.11, bf16[512,8,128]{0,2,1:T(8,128)(2,1)S(1)} %bitcast.98), kind=kOutput, calls=%fused_computation.26 | convolution fusion | flops 537001984 | bytes 5373952 | tf_op jit(solution)/shard_map/grab,agrd->bgd/dot_general | solution.py:50
  24.1 0.0 copy-start.2
  24.1 1.9 %fusion.24 = bf16[512,128]{0,1:T(8,128)(2,1)S(1)} fusion(bf16[512,8,128]{0,2,1:T(8,128)(2,1)S(1)} %bitcast.100, f32[512,512,8]{1,0,2:T(8,128)S(1)} %fusion.32, f32[8,512]{1,0:T(8,128)S(1)} %bitcast_convert_fusion.1, pred[512,512]{0,1:T(8,128)(4,1)S(1)} %fusion.29), kind=kOutput, calls=%fused_computation.25 | convolution fusion | flops 545325056 | bytes 9846784 | tf_op jit(solution)/shard_map/grab,agrd->bgd/dot_general | solution.py:38
  26.1 71.9 %all-gather.2.cloned.1.call-done = bf16[4096,1,1280]{2,0,1:T(8,128)(2,1)} async-done(((bf16[64,1,1280]{2,0,1:T(8,128)(2,1)}), bf16[4096,1,1280]{2,0,1:T(8,128)(2,1)}) %all-gather.2.cloned.1.call-update) | async-done | bytes 10485776 | tf_op jit(solution)/shard_map/all_gather | solution.py:66
  98.0 0.0 copy-done.2
  98.0 11.2 %fusion.7 = bf16[512,4096]{1,0:T(8,128)(2,1)} fusion(bf16[4096,1,1280]{2,0,1:T(8,128)(2,1)} %all-gather.2.cloned.1.call-done, bf16[512,128]{0,1:T(8,128)(2,1)S(1)} %fusion.24, bf16[512,128]{0,1:T(8,128)(2,1)S(1)} %copy-done.2, bf16[512,1024]{0,1:T(8,128)(2,1)S(1)} %bitcast.101), kind=kOutput, calls=%fused_computation.11 | convolution fusion | flops 5374738432 | bytes 15990784 | tf_op jit(solution)/shard_map/dot_general | solution.py:110
  109.2 0.0 reduce-scatter.2.cloned.1.call-update
  109.2 48.0 %reduce-scatter.2.cloned.1.call-done = bf16[512,1024]{1,0:T(8,128)(2,1)} async-done(((bf16[512,4096]{1,0:T(8,128)(2,1)}), bf16[512,1024]{1,0:T(8,128)(2,1)}) %reduce-scatter.2.cloned.1.call-update) | async-done | bytes 1048592 | tf_op jit(solution)/shard_map/reduce_scatter | solution.py:113
  (1 shorter events, 0.0 us)
Async XLA Ops:
  6.5 10.5 %copy-start = (bf16[512,1,128]{2,0,1:T(8,128)(2,1)S(1)}, bf16[512,1,128]{2,0,1:T(8,128)(2,1)}, u32[]{:S(2)}) copy-start(bf16[512,1,128]{2,0,1:T(8,128)(2,1)} %param.16) | copy-start | bytes 393220
  6.5 11.8 %copy-start.1 = (bf16[512,1,128]{2,0,1:T(8,128)(2,1)S(1)}, bf16[512,1,128]{2,0,1:T(8,128)(2,1)}, u32[]{:S(2)}) copy-start(bf16[512,1,128]{2,0,1:T(8,128)(2,1)} %param.17) | copy-start | bytes 393220
  6.5 91.4 %all-gather.2.cloned.1.call-start = ((), (), s32[]{:S(2)}) async-start(), calls=%async_computation.1 | async-start | bytes 10649600 | tf_op jit(solution)/shard_map/all_gather | solution.py:66
  7.3 150.0 %reduce-scatter.2.cloned.1.call-start = ((), (), s32[]{:S(2)}) async-start(), calls=%async_computation.2 | async-start | bytes 5242880 | tf_op jit(solution)/shard_map/reduce_scatter | solution.py:113
  24.1 73.9 %copy-start.2 = (bf16[512,128]{0,1:T(8,128)(2,1)S(1)}, bf16[512,128]{0,1:T(8,128)(2,1)}, u32[]{:S(2)}) copy-start(bf16[512,128]{0,1:T(8,128)(2,1)} %fusion.27) | copy-start | bytes 393220
Sparse Core Ops, SparseCore 0:
  10.1 87.8 all-gather.1
  109.3 47.8 reduce-scatter.1
where the time goes:
time: 165 us; the launch traced here: 164 us
  waiting for transfers between devices  121 us (73%)
  matrix products  20.2 us (12%)
  between operations  13.5 us (8%)
  local copies, waits for them, and re-layouts  5.3 us (3%)
  other arithmetic  4.45 us (3%)
    all_gather x1, waiting for transfers between devices, on_device(): lax.all_gather(query_key_value_weight, 'tok', axis=0, tiled=True)  71.9 us
    reduce_scatter x1, waiting for transfers between devices, on_device(): lax.psum_scatter(partial_sum.astype(jnp.bfloat16), 'head', scatter_dimens...  48 us
    dot_general x1, matrix products, on_device(): lax.dot_general(stacked_gradients, flat_piece, (((1,), (1,)), ((), ())),...  11.2 us
  transfers between devices with their start and end apart: 2, of which 2 were waited for; matrix products, arithmetic and copies ran while one was open for 11% of the time, Pallas kernels for 0%

commit v1 on v0

v1 whole, which is shorter than its diff:
```python
import jax
import jax.numpy as jnp
import numpy as np
from jax import lax
from jax.experimental import pallas as pl
from jax.experimental.pallas import tpu as pltpu
from jax.sharding import Mesh, PartitionSpec as P

SIZES = {"y": 4, "z": 8, "c": 2, "x": 4}
BLOCK = 128
MASKED = -1e30
LOG2E = 1.4426950408889634


def move(value, axes, target):
    dims = [SIZES[a] for a in axes]
    pairs = []
    for source in range(int(np.prod(dims))):
        coords = dict(zip(axes, (int(v) for v in np.unravel_index(source, dims))))
        goal = target(**coords)
        goal = [goal[a] % SIZES[a] for a in axes]
        pairs.append((source, int(np.ravel_multi_index(goal, dims))))
    return lax.ppermute(value, axes, pairs)


def swap_cores(value):
    return move(value, ("c",), lambda c: dict(c=1 - c))


def along(value, axis, steps):
    sign = lambda c: steps if c == 0 else -steps
    return move(value, (axis, "c"), lambda c, **k: {axis: k[axis] + sign(c), "c": c})


def shift(value, axis, steps):
    return move(value, (axis,), lambda **k: {axis: k[axis] + steps})


def nt(a, b):
    return lax.dot_general(a, b, (((1,), (1,)), ((), ())), preferred_element_type=jnp.float32)


def nn(a, b):
    return jnp.dot(a, b, preferred_element_type=jnp.float32)


def attention_kernel(q_ref, do_ref, k_ref, v_ref, lse_ref, delta_ref, seg_ref, out_ref,
                     bias, key_t, lse_f, delta_f, dk_acc, dv_acc):
    head = pl.program_id(0)
    heads = pl.num_programs(0)
    window, size = k_ref.shape
    scale = size ** -0.5

    @pl.when(head == 0)
    def _():
        lse_f[...] = lse_ref[...].astype(jnp.float32) * LOG2E
        delta_f[...] = delta_ref[...].astype(jnp.float32)
        key_t[...] = k_ref[...].astype(jnp.float32).T.astype(jnp.bfloat16)
        seg_row = seg_ref[...].astype(jnp.float32)
        seg_col = jnp.broadcast_to(seg_row, (BLOCK, window)).T
        row = lax.broadcasted_iota(jnp.int32, (window, BLOCK), 0)
        col = lax.broadcasted_iota(jnp.int32, (window, BLOCK), 1)
        for start in range(0, window, BLOCK):
            same = seg_col == seg_row[:, start:start + BLOCK]
            bias[:, start:start + BLOCK] = jnp.where(same & (row <= col + start), 0.0, MASKED)
        dk_acc[...] = jnp.zeros_like(dk_acc)
        dv_acc[...] = jnp.zeros_like(dv_acc)

    lse = lse_f[pl.ds(head, 1), :]
    delta = delta_f[pl.ds(head, 1), :]
    parts = []
    for start in range(0, window, BLOCK):
        rows = slice(start, start + BLOCK)
        query = q_ref[start:, :]
        dout = do_ref[start:, :]
        scores = nt(k_ref[rows, :], query)
        probs = jnp.exp2(scores * (scale * LOG2E) - lse[:, start:] + bias[rows, start:])
        grad_prob = nt(v_ref[rows, :], dout)
        grad_score = (probs * (grad_prob - delta[:, start:])).astype(jnp.bfloat16)
        dv_acc[rows, :] += nn(probs.astype(jnp.bfloat16), dout)
        dk_acc[rows, :] += nn(grad_score, query)
        parts.append(nn(key_t[:, rows], grad_score))
    for start in range(0, window, BLOCK):
        total = parts[0][:, start:start + BLOCK]
        for index in range(1, start // BLOCK + 1):
            first = start - index * BLOCK
            total += parts[index][:, first:first + BLOCK]
        out_ref[start:start + BLOCK, pl.ds(pl.multiple_of(head * size, size), size)] = (
            (total * scale).T.astype(jnp.bfloat16)
        )

    @pl.when(head == heads - 1)
    def _():
        out_ref[:, heads * size:(heads + 1) * size] = (dk_acc[...] * scale).astype(jnp.bfloat16)
        out_ref[:, (heads + 1) * size:] = dv_acc[...].astype(jnp.bfloat16)


def joined_gradients(query, dout, key, value, lse, delta, seg):
    window, width = query.shape
    size = key.shape[1]
    heads = width // size
    whole = lambda shape: pl.BlockSpec(shape, lambda r: (0, 0))
    per_head = pl.BlockSpec((window, size), lambda r: (0, r))
    return pl.pallas_call(
        attention_kernel,
        grid=(heads,),
        in_specs=[per_head, per_head, whole((window, size)), whole((window, size)),
                  whole((heads, window)), whole((heads, window)), whole((1, window))],
        out_specs=whole((window, width + 2 * size)),
        out_shape=jax.ShapeDtypeStruct((window, width + 2 * size), jnp.bfloat16),
        scratch_shapes=[
            pltpu.VMEM((window, window), jnp.float32),
            pltpu.VMEM((size, window), jnp.bfloat16),
            pltpu.VMEM((heads, window), jnp.float32),
            pltpu.VMEM((heads, window), jnp.float32),
            pltpu.VMEM((window, size), jnp.float32),
            pltpu.VMEM((window, size), jnp.float32),
        ],
        compiler_params=pltpu.CompilerParams(vmem_limit_bytes=24 << 20),
        cost_estimate=pl.CostEstimate(flops=4 * 10 ** 9, bytes_accessed=4 * 10 ** 6, transcendentals=10 ** 6),
        name="attention_backward",
    )(query, dout, key, value, lse, delta, seg)


def projection_kernel(where_ref, j0, jp, jm, jf, a_own, a1, a2, a3, a4, ax1, ax2, ax3, ax4,
                      b_own, b1, b2, bx1, bx2, out_ref, joined, wa, wb, sems):
    y, z, c, x = (where_ref[i] for i in range(4))
    sign = 1 - 2 * c
    count = [0]
    copies = []

    def copy(source, target):
        made = pltpu.make_async_copy(source, target, sems.at[count[0]])
        count[0] += 1
        made.start()
        copies.append(made)

    for source, step in ((j0, 0), (jp, 3), (jm, 1), (jf, 2)):
        copy(source, joined.at[(x + step) % 4])

    def put(buffer, source, g, slot):
        copy(source, buffer.at[g, pl.ds(pl.multiple_of(slot * BLOCK, BLOCK), BLOCK)])

    half_mine, half_theirs = c * 2, (1 - c) * 2
    for j in range(4):
        g = (y + j) % 4
        put(wa, a_own.at[j], g, z)
        for k, (mine, theirs) in enumerate(((a1, ax1), (a2, ax2), (a3, ax3)), 1):
            put(wa, mine.at[j], g, (z + 8 - sign * k) % 8)
            put(wa, theirs.at[j], g, (z + 8 + sign * k) % 8)
    for j in range(2):
        put(wa, a4.at[j], (y + half_mine + j) % 4, (z + 4) % 8)
        put(wa, ax4.at[j], (y + half_theirs + j) % 4, (z + 4) % 8)
    for k in range(8):
        step = (0, -1, -2, -3, 4, 1, 2, 3)[k]
        put(wb, b_own.at[k], y, (z + 8 + sign * step) % 8)
        put(wb, b1.at[k], (y + 4 - sign) % 4, (z + 8 + sign * step) % 8)
        put(wb, bx1.at[k], (y + 4 + sign) % 4, (z + 8 - sign * step) % 8)
    for k in range(4):
        mine = jnp.where(c == 0, (0, 7, 6, 5)[k], (1, 2, 3, 4)[k])
        theirs = jnp.where(c == 0, (1, 2, 3, 4)[k], (0, 7, 6, 5)[k])
        put(wb, b2.at[k], (y + 2) % 4, (z + mine) % 8)
        put(wb, bx2.at[k], (y + 2) % 4, (z + theirs) % 8)
    for made in copies:
        made.wait()
    half = wa.shape[2]
    for start in range(0, out_ref.shape[1], 256):
        total = None
        for g in range(4):
            for buffer, columns in ((wa, slice(0, half)), (wb, slice(half, 2 * half))):
                term = nt(joined[g, :, columns], buffer[g, start:start + 256, :])
                total = term if total is None else total + term
        out_ref[:, start:start + 256] = total.astype(jnp.bfloat16)


def projection(where, *operands):
    window, width = operands[0].shape
    half = width // 2
    columns = 8 * BLOCK
    return pl.pallas_call(
        projection_kernel,
        in_specs=[pl.BlockSpec(memory_space=pltpu.SMEM)]
        + [pl.BlockSpec(memory_space=pl.ANY)] * len(operands),
        out_specs=pl.BlockSpec(memory_space=pltpu.VMEM),
        out_shape=jax.ShapeDtypeStruct((window, columns), jnp.bfloat16),
        scratch_shapes=[
            pltpu.VMEM((4, window, width), jnp.bfloat16),
            pltpu.VMEM((4, columns, half), jnp.bfloat16),
            pltpu.VMEM((4, columns, half), jnp.bfloat16),
            pltpu.SemaphoreType.DMA((72,)),
        ],
        compiler_params=pltpu.CompilerParams(vmem_limit_bytes=32 << 20),
        cost_estimate=pl.CostEstimate(flops=6 * 10 ** 9, bytes_accessed=20 * 10 ** 6, transcendentals=0),
        name="projection",
    )(where, *operands)


def gather_weights(weight, core):
    rows, width = weight.shape
    half = width // 2
    turned = move(weight, ("y", "x"), lambda y, x: dict(y=x, x=y))
    other = swap_cores(turned)
    low = jnp.where(core == 0, turned, other)
    high = jnp.where(core == 0, other, turned)
    block = jnp.concatenate([low, high], axis=0)
    a_block, b_block = block[:, :half], block[:, half:]
    a_block, b_block = lax.optimization_barrier((a_block, b_block))

    a_ahead = shift(a_block, "y", -1)
    a_behind = shift(a_block, "y", 1)
    a_far = shift(a_block, "y", 2)
    b1 = along(b_block, "z", 1)
    b4 = along(lax.dynamic_slice_in_dim(b_block, core * rows, rows, 0), "z", 4)

    a_own = jnp.stack([a_block, a_ahead, a_far, a_behind])
    a1 = along(a_own, "z", 1)

    b23 = along(jnp.stack([b1, b_block]), "z", 2)
    bx1, bx4, bx23 = swap_cores(b1), swap_cores(b4), swap_cores(b23)
    far = jnp.concatenate([jnp.where(core == 0, b4, bx4), jnp.where(core == 0, bx4, b4)], axis=0)
    b_own = jnp.stack([b_block, b1, b23[1], b23[0], far, bx1, bx23[1], bx23[0]])

    a2 = along(a1, "z", 1)
    b_next = along(b_own, "y", 1)
    a3 = along(a2, "z", 1)
    a4 = along(lax.dynamic_slice_in_dim(a3, core * 2, 2, 0), "z", 1)
    b_far = along(lax.dynamic_slice_in_dim(b_next, core, 4, 0), "y", 1)
    mine = (a1, a2, a3, a4)
    theirs = tuple(swap_cores(v) for v in mine)
    return (a_own,) + mine + theirs + (b_own, b_next, b_far, swap_cores(b_next), swap_cores(b_far))


def on_device(query_rows, key_rows, value_rows, output_gradient, row_logsumexp, row_delta_sums,
              segments, query_key_value_weight):
    window, _, width = query_rows.shape
    place = [lax.axis_index(a) for a in ("y", "z", "c", "x")]
    core = place[2]
    token_index = (place[0] * SIZES["z"] + place[1]) * SIZES["c"] + core
    weights = gather_weights(query_key_value_weight[:, 0], core)
    seg = lax.dynamic_slice_in_dim(segments, token_index * window, window).reshape(1, window)
    joined = joined_gradients(
        query_rows.reshape(window, width), output_gradient.reshape(window, width),
        key_rows[:, 0], value_rows[:, 0], row_logsumexp[0], row_delta_sums[0], seg)
    from_below = shift(joined, "x", 1)
    from_above = shift(joined, "x", -1)
    from_far = shift(joined, "x", 2)
    where = jnp.stack(place).astype(jnp.int32)
    return projection(where, joined, from_below, from_above, from_far, *weights)


def solution(mesh):
    grid = Mesh(mesh.devices.reshape(4, 8, 2, 4), ("y", "z", "c", "x"))
    tok = ("y", "z", "c")
    rows = P(tok, "x", None)
    placed = (rows, rows, rows, rows, P("x", None, tok), P("x", None, tok), P(), rows)
    return jax.shard_map(on_device, mesh=grid, in_specs=placed, out_specs=P(tok, "x"), check_vma=False)
```

time: 165 us -> 150 us (0.909)
  waiting for transfers between devices: 121 us -> 86.7 us
  starting transfers between devices: 0.04 us -> 28.7 us
  Pallas kernels: 0 us -> 26.1 us
  matrix products: 20.2 us -> 0 us
  between operations: 13.5 us -> 0.36 us
  other arithmetic: 4.45 us -> 0.96 us
    ppermute x0 -> x26, waiting for transfers between devices: none -> 86.7 us  [move(): return lax.ppermute(value, axes, pairs)]
    all_gather x1 -> x0, waiting for transfers between devices: 71.9 us -> none  [on_device(): lax.all_gather(query_key_value_weight, 'tok', axis=0, tiled=True)]
    reduce_scatter x1 -> x0, waiting for transfers between devices: 48 us -> none  [on_device(): lax.psum_scatter(partial_sum.astype(jnp.bfloat16), 'head', scatter_dimens...]
    ppermute x0 -> x26, starting transfers between devices: none -> 28.7 us  [move(): return lax.ppermute(value, axes, pairs)]
    pallas_call x0 -> x2, Pallas kernels: none -> 26.1 us  [the longest x1 15.2 us: projection(): pl.pallas_call(projection_kernel, in_specs=[pl.BlockSpec(memory_space=plt...]
    dot_general x6 -> x0, matrix products: 20.2 us -> none  [the longest x1 11.2 us: on_device(): lax.dot_general(stacked_gradients, flat_piece, (((1,), (1,)), ((), ())),...]
    unnamed x8 -> x18, local copies, waits for them, and re-layouts: 0.1 us -> 4.13 us
    another operation x2 -> x1, local copies, waits for them, and re-layouts: 3 us -> 0.7 us  [gather_weights(): b_own = jnp.stack([b_block, b1, b23[1], b23[0], far, bx1, bx23[1], bx23[0]])]
  transfers between devices with their start and end apart: 2 -> 26, of which waited for: 2 -> 11; matrix products, arithmetic and copies ran while one was open for 11% -> 5% of each run, Pallas kernels for 0% -> 7%
where the time goes in v1:
time: 150 us; the launch traced here: 149 us
  waiting for transfers between devices  86.7 us (58%)
  starting transfers between devices  28.7 us (19%)
  Pallas kernels  26.1 us (17%)
  local copies, waits for them, and re-layouts  6.55 us (4%)
    ppermute x26, waiting for transfers between devices, move(): return lax.ppermute(value, axes, pairs)  86.7 us
    ppermute x26, starting transfers between devices, move(): return lax.ppermute(value, axes, pairs)  28.7 us
    pallas_call x1, Pallas kernels, projection(): pl.pallas_call(projection_kernel, in_specs=[pl.BlockSpec(memory_space=plt...  15.2 us
    pallas_call x1, Pallas kernels, joined_gradients(): pl.pallas_call(attention_kernel, grid=(heads,), in_specs=[per_head, per_h...  10.9 us
    unnamed x18, local copies, waits for them, and re-layouts  4.13 us
  transfers between devices with their start and end apart: 26, of which 11 were waited for; matrix products, arithmetic and copies ran while one was open for 5% of the time, Pallas kernels for 7%

profile of v1, /device:TPU:8, one launch (start us, length us, event | category | flops | bytes accessed | tf_op | source)
XLA Modules:
  0.0 149.3 jit_solution(8197573494966081169)
XLA Ops:
  0.0 3.3 %collective-permute-start.3 = (bf16[64,1280]{1,0:T(8,128)(2,1)}, bf16[64,1280]{1,0:T(8,128)(2,1)S(1)}, u32[]{:S(2)}, u32[]{:S(2)}) collective-permute-start(bf16[64,1280]{1,0:T(8,128)(2,1)} %bitcast.39), channel_id=1, source_target_pairs={{0,0},{1,64},{2,128},{3,192},{64,1},{65,65},{66,129},{67,193},{128... | collective-permute-start | bytes 491528 | tf_op jit(solution)/shard_map/ppermute | solution.py:23
  3.3 6.0 %collective-permute-done.3 = bf16[64,1280]{1,0:T(8,128)(2,1)S(1)} collective-permute-done((bf16[64,1280]{1,0:T(8,128)(2,1)}, bf16[64,1280]{1,0:T(8,128)(2,1)S(1)}, u32[]{:S(2)}, u32[]{:S(2)}) %collective-permute-start.3) | collective-permute-done | bytes 163872 | tf_op jit(solution)/shard_map/ppermute | solution.py:23
  9.3 0.0 collective-permute-start.4
  9.3 1.4 collective-permute-done.4
  10.8 7.3 %collective-permute-start.18 = (bf16[64,640]{1,0:T(8,128)(2,1)S(1)}, bf16[64,640]{1,0:T(8,128)(2,1)S(1)}, u32[]{:S(2)}, u32[]{:S(2)}) collective-permute-start(bf16[64,640]{1,0:T(8,128)(2,1)S(1)} %constant_dynamic-slice_fusion.1), channel_id=1, source_target_pairs={{0,32},{4,36},{8,40},{12,44},{16,48},{20,52},{24,56},{28,60},{32,0... | collective-permute-start | bytes 245768 | tf_op jit(solution)/shard_map/ppermute | solution.py:23
  18.0 0.8 dynamic_slice.12
  18.8 4.6 %collective-permute-start.7 = (bf16[128,640]{1,0:T(8,128)(2,1)S(1)}, bf16[128,640]{1,0:T(8,128)(2,1)S(1)}, u32[]{:S(2)}, u32[]{:S(2)}) collective-permute-start(bf16[128,640]{1,0:T(8,128)(2,1)S(1)} %get-tuple-element.7), channel_id=1, source_target_pairs={{0,64},{64,128},{128,192},{192,0},{1,65},{65,129},{129,193},{193,1... | collective-permute-start | bytes 491528 | tf_op jit(solution)/shard_map/ppermute | solution.py:23
  23.4 3.3 %collective-permute-start.6 = (bf16[128,640]{1,0:T(8,128)(2,1)S(1)}, bf16[128,640]{1,0:T(8,128)(2,1)S(1)}, u32[]{:S(2)}, u32[]{:S(2)}) collective-permute-start(bf16[128,640]{1,0:T(8,128)(2,1)S(1)} %get-tuple-element.7), channel_id=1, source_target_pairs={{0,128},{64,192},{128,0},{192,64},{1,129},{65,193},{129,1},{193,65... | collective-permute-start | bytes 491528 | tf_op jit(solution)/shard_map/ppermute | solution.py:23
  26.7 2.6 %collective-permute-start.5 = (bf16[128,640]{1,0:T(8,128)(2,1)S(1)}, bf16[128,640]{1,0:T(8,128)(2,1)S(1)}, u32[]{:S(2)}, u32[]{:S(2)}) collective-permute-start(bf16[128,640]{1,0:T(8,128)(2,1)S(1)} %get-tuple-element.7), channel_id=1, source_target_pairs={{0,192},{64,0},{128,64},{192,128},{1,193},{65,1},{129,65},{193,129... | collective-permute-start | bytes 491528 | tf_op jit(solution)/shard_map/ppermute | solution.py:23
  29.3 1.0 collective-permute-start.16
  30.3 0.0 collective-permute-done.18
  30.3 0.0 collective-permute-start.19
  30.3 0.7 constant_dynamic-update-slice_fusion.1
  31.0 0.6 collective-permute-done.19
  31.6 4.2 %collective-permute-done.16 = bf16[128,640]{1,0:T(8,128)(2,1)S(1)} collective-permute-done((bf16[128,640]{1,0:T(8,128)(2,1)S(1)}, bf16[128,640]{1,0:T(8,128)(2,1)S(1)}, u32[]{:S(2)}, u32[]{:S(2)}) %collective-permute-start.16) | collective-permute-done | bytes 163872 | tf_op jit(solution)/shard_map/ppermute | solution.py:23
  35.9 0.3 collective-permute-start.17
  36.2 0.0 collective-permute-done.7
  36.2 0.0 collective-permute-done.6
  36.2 0.0 copy-start.3
  36.3 0.1 pad_maximum_fusion.a_own
  36.4 0.0 copy-start
  36.4 0.0 copy-start.1
  36.4 0.0 copy-start.2
  36.4 0.0 copy-start.4
  36.4 0.0 copy-start.5
  36.4 1.1 collective-permute-start.8
  37.5 0.7 constant_dynamic-update-slice_fusion
  38.2 9.3 %collective-permute-done.17 = bf16[2,128,640]{2,1,0:T(8,128)(2,1)S(1)} collective-permute-done((bf16[2,128,640]{2,1,0:T(8,128)(2,1)S(1)}, bf16[2,128,640]{2,1,0:T(8,128)(2,1)S(1)}, u32[]{:S(2)}, u32[]{:S(2)}) %collective-permute-start.17) | collective-permute-done | bytes 327712 | tf_op jit(solution)/shard_map/ppermute | solution.py:23
  47.5 0.7 slice_dynamic-update-slice_fusion.3
  48.2 0.7 slice_dynamic-update-slice_fusion.2
  48.9 0.7 fusion.1
  49.5 0.7 bitcast_dynamic-update-slice_fusion
  50.2 0.7 slice_dynamic-update-slice_fusion.1
  50.9 0.7 slice_dynamic-update-slice_fusion.b_own
  51.7 10.9 %attention_backward.1.j0 = bf16[512,1280]{1,0:T(8,128)(2,1)} custom-call(bf16[512,1024]{1,0:T(8,128)(2,1)S(1)} %bitcast.27, bf16[512,1024]{1,0:T(8,128)(2,1)S(1)} %bitcast.28, bf16[512,128]{1,0:T(8,128)(2,1)S(1)} %bitcast.29, bf16[512,128]{1,0:T(8,128)(2,1)S(1)} %bitcast.30, bf16[8,512]{1,0:T(8,128)(2,1)S(1)} %bitcast.31, bf16[8,512]{1,0:T(8,128)(2,1)S(1)} %bitcast.32, ...), custom_call_target="tpu_custom_call" | custom-call | flops 4000000000 | bytes 4000000 | tf_op jit(solution)/shard_map/attention_backward/pallas_call | solution.py:104
  62.6 2.6 %collective-permute-start.2 = (bf16[512,1280]{1,0:T(8,128)(2,1)}, bf16[512,1280]{1,0:T(8,128)(2,1)}, u32[]{:S(2)}, u32[]{:S(2)}) collective-permute-start(bf16[512,1280]{1,0:T(8,128)(2,1)} %attention_backward.1.j0), channel_id=1, source_target_pairs={{0,2},{1,3},{2,0},{3,1},{4,6},{5,7},{6,4},{7,5},{8,10},{9,11},{10,... | collective-permute-start | bytes 3932168 | tf_op jit(solution)/shard_map/ppermute | solution.py:23
  65.2 2.0 %collective-permute-start = (bf16[512,1280]{1,0:T(8,128)(2,1)}, bf16[512,1280]{1,0:T(8,128)(2,1)}, u32[]{:S(2)}, u32[]{:S(2)}) collective-permute-start(bf16[512,1280]{1,0:T(8,128)(2,1)} %attention_backward.1.j0), channel_id=1, source_target_pairs={{0,1},{1,2},{2,3},{3,0},{4,5},{5,6},{6,7},{7,4},{8,9},{9,10},{10,1... | collective-permute-start | bytes 3932168 | tf_op jit(solution)/shard_map/ppermute | solution.py:23
  67.2 9.9 %collective-permute-done.9.a2 = bf16[4,128,640]{2,1,0:T(8,128)(2,1)} collective-permute-done((bf16[4,128,640]{2,1,0:T(8,128)(2,1)S(1)}, bf16[4,128,640]{2,1,0:T(8,128)(2,1)}, u32[]{:S(2)}, u32[]{:S(2)}) %collective-permute-start.9) | collective-permute-done | bytes 655392 | tf_op jit(solution)/shard_map/ppermute | solution.py:23
  77.1 0.9 constant_dynamic-slice_fusion
  78.0 18.0 %collective-permute-done.2.jf = bf16[512,1280]{1,0:T(8,128)(2,1)} collective-permute-done((bf16[512,1280]{1,0:T(8,128)(2,1)}, bf16[512,1280]{1,0:T(8,128)(2,1)}, u32[]{:S(2)}, u32[]{:S(2)}) %collective-permute-start.2) | collective-permute-done | bytes 1310752 | tf_op jit(solution)/shard_map/ppermute | solution.py:23
  96.1 26.7 %collective-permute-done.1.jm = bf16[512,1280]{1,0:T(8,128)(2,1)} collective-permute-done((bf16[512,1280]{1,0:T(8,128)(2,1)}, bf16[512,1280]{1,0:T(8,128)(2,1)}, u32[]{:S(2)}, u32[]{:S(2)}) %collective-permute-start.1) | collective-permute-done | bytes 1310752 | tf_op jit(solution)/shard_map/ppermute | solution.py:23
  122.8 0.8 collective-permute-done.jp
  123.6 0.0 collective-permute-start.14
  123.6 0.5 collective-permute-start.25
  124.1 7.9 %collective-permute-done.11.a4 = bf16[2,128,640]{2,1,0:T(8,128)(2,1)} collective-permute-done((bf16[2,128,640]{2,1,0:T(8,128)(2,1)S(1)}, bf16[2,128,640]{2,1,0:T(8,128)(2,1)}, u32[]{:S(2)}, u32[]{:S(2)}) %collective-permute-start.11) | collective-permute-done | bytes 327712 | tf_op jit(solution)/shard_map/ppermute | solution.py:23
  132.0 0.1 pad_add_fusion.where_ref
  132.1 1.9 %collective-permute-done.15.ax4 = bf16[2,128,640]{2,1,0:T(8,128)(2,1)} collective-permute-done((bf16[2,128,640]{2,1,0:T(8,128)(2,1)}, bf16[2,128,640]{2,1,0:T(8,128)(2,1)}, u32[]{:S(2)}, u32[]{:S(2)}) %collective-permute-start.15) | collective-permute-done | bytes 327712 | tf_op jit(solution)/shard_map/ppermute | solution.py:23
  134.0 15.2 %projection.1 = bf16[512,1024]{1,0:T(8,128)(2,1)} custom-call(s32[4]{0:T(128)S(1)} %pad_add_fusion.where_ref, bf16[512,1280]{1,0:T(8,128)(2,1)} %attention_backward.1.j0, bf16[512,1280]{1,0:T(8,128)(2,1)} %collective-permute-done.jp, bf16[512,1280]{1,0:T(8,128)(2,1)} %collective-permute-done.1.jm, bf16[512,1280]{1,0:T(8,128)(2,1)} %collective-permute-done.2.jf, ...), custom_call_target="tpu_custom_call" | custom-call | flops 6000000000 | bytes 20000000 | tf_op jit(solution)/shard_map/projection/pallas_call | solution.py:180
  (36 shorter events, 0.2 us)
Async XLA Ops:
  0.0 9.3 %collective-permute-start.3 = (bf16[64,1280]{1,0:T(8,128)(2,1)}, bf16[64,1280]{1,0:T(8,128)(2,1)S(1)}, u32[]{:S(2)}, u32[]{:S(2)}) collective-permute-start(bf16[64,1280]{1,0:T(8,128)(2,1)} %bitcast.39), channel_id=1, source_target_pairs={{0,0},{1,64},{2,128},{3,192},{64,1},{65,65},{66,129},{67,193},{128... | collective-permute-start | bytes 491528 | tf_op jit(solution)/shard_map/ppermute | solution.py:23
  9.3 1.4 collective-permute-start.4
  10.8 19.6 %collective-permute-start.18 = (bf16[64,640]{1,0:T(8,128)(2,1)S(1)}, bf16[64,640]{1,0:T(8,128)(2,1)S(1)}, u32[]{:S(2)}, u32[]{:S(2)}) collective-permute-start(bf16[64,640]{1,0:T(8,128)(2,1)S(1)} %constant_dynamic-slice_fusion.1), channel_id=1, source_target_pairs={{0,32},{4,36},{8,40},{12,44},{16,48},{20,52},{24,56},{28,60},{32,0... | collective-permute-start | bytes 245768 | tf_op jit(solution)/shard_map/ppermute | solution.py:23
  18.8 17.4 %collective-permute-start.7 = (bf16[128,640]{1,0:T(8,128)(2,1)S(1)}, bf16[128,640]{1,0:T(8,128)(2,1)S(1)}, u32[]{:S(2)}, u32[]{:S(2)}) collective-permute-start(bf16[128,640]{1,0:T(8,128)(2,1)S(1)} %get-tuple-element.7), channel_id=1, source_target_pairs={{0,64},{64,128},{128,192},{192,0},{1,65},{65,129},{129,193},{193,1... | collective-permute-start | bytes 491528 | tf_op jit(solution)/shard_map/ppermute | solution.py:23
  23.4 12.8 %collective-permute-start.6 = (bf16[128,640]{1,0:T(8,128)(2,1)S(1)}, bf16[128,640]{1,0:T(8,128)(2,1)S(1)}, u32[]{:S(2)}, u32[]{:S(2)}) collective-permute-start(bf16[128,640]{1,0:T(8,128)(2,1)S(1)} %get-tuple-element.7), channel_id=1, source_target_pairs={{0,128},{64,192},{128,0},{192,64},{1,129},{65,193},{129,1},{193,65... | collective-permute-start | bytes 491528 | tf_op jit(solution)/shard_map/ppermute | solution.py:23
  26.7 9.5 %collective-permute-start.5 = (bf16[128,640]{1,0:T(8,128)(2,1)S(1)}, bf16[128,640]{1,0:T(8,128)(2,1)S(1)}, u32[]{:S(2)}, u32[]{:S(2)}) collective-permute-start(bf16[128,640]{1,0:T(8,128)(2,1)S(1)} %get-tuple-element.7), channel_id=1, source_target_pairs={{0,192},{64,0},{128,64},{192,128},{1,193},{65,1},{129,65},{193,129... | collective-permute-start | bytes 491528 | tf_op jit(solution)/shard_map/ppermute | solution.py:23
  29.3 6.5 %collective-permute-start.16 = (bf16[128,640]{1,0:T(8,128)(2,1)S(1)}, bf16[128,640]{1,0:T(8,128)(2,1)S(1)}, u32[]{:S(2)}, u32[]{:S(2)}) collective-permute-start(bf16[128,640]{1,0:T(8,128)(2,1)S(1)} %get-tuple-element.8), channel_id=1, source_target_pairs={{0,8},{4,60},{8,16},{12,4},{16,24},{20,12},{24,32},{28,20},{32,40}... | collective-permute-start | bytes 491528 | tf_op jit(solution)/shard_map/ppermute | solution.py:23
  30.3 1.3 collective-permute-start.19
  35.9 11.6 %collective-permute-start.17 = (bf16[2,128,640]{2,1,0:T(8,128)(2,1)S(1)}, bf16[2,128,640]{2,1,0:T(8,128)(2,1)S(1)}, u32[]{:S(2)}, u32[]{:S(2)}) collective-permute-start(bf16[2,128,640]{2,1,0:T(8,128)(2,1)S(1)} %pad_maximum_fusion.1), channel_id=1, source_target_pairs={{0,16},{4,52},{8,24},{12,60},{16,32},{20,4},{24,40},{28,12},{32,48... | collective-permute-start | bytes 983048 | tf_op jit(solution)/shard_map/ppermute | solution.py:23
  36.2 15.4 %copy-start.3 = (bf16[512,1,128]{2,0,1:T(8,128)(2,1)S(1)}, bf16[512,1,128]{2,0,1:T(8,128)(2,1)}, u32[]{:S(2)}) copy-start(bf16[512,1,128]{2,0,1:T(8,128)(2,1)} %param.10) | copy-start | bytes 393220
  36.4 15.3 %copy-start = (bf16[512,1,1024]{2,0,1:T(8,128)(2,1)S(1)}, bf16[512,1,1024]{2,0,1:T(8,128)(2,1)}, u32[]{:S(2)}) copy-start(bf16[512,1,1024]{2,0,1:T(8,128)(2,1)} %param.8) | copy-start | bytes 3145732
  36.4 15.3 %copy-start.1 = (bf16[512,1,1024]{2,0,1:T(8,128)(2,1)S(1)}, bf16[512,1,1024]{2,0,1:T(8,128)(2,1)}, u32[]{:S(2)}) copy-start(bf16[512,1,1024]{2,0,1:T(8,128)(2,1)} %param.11) | copy-start | bytes 3145732
  36.4 15.2 %copy-start.2 = (bf16[512,1,128]{2,0,1:T(8,128)(2,1)S(1)}, bf16[512,1,128]{2,0,1:T(8,128)(2,1)}, u32[]{:S(2)}) copy-start(bf16[512,1,128]{2,0,1:T(8,128)(2,1)} %param.9) | copy-start | bytes 393220
  36.4 15.2 %copy-start.4 = (bf16[1,8,512]{2,1,0:T(8,128)(2,1)S(1)}, bf16[1,8,512]{2,1,0:T(8,128)(2,1)}, u32[]{:S(2)}) copy-start(bf16[1,8,512]{2,1,0:T(8,128)(2,1)} %param.12) | copy-start | bytes 24580
  36.4 15.2 %copy-start.5 = (bf16[1,8,512]{2,1,0:T(8,128)(2,1)S(1)}, bf16[1,8,512]{2,1,0:T(8,128)(2,1)}, u32[]{:S(2)}) copy-start(bf16[1,8,512]{2,1,0:T(8,128)(2,1)} %param.13) | copy-start | bytes 24580
  36.4 28.8 %collective-permute-start.8 = (bf16[4,128,640]{2,1,0:T(8,128)(2,1)S(1)}, bf16[4,128,640]{2,1,0:T(8,128)(2,1)S(1)}, u32[]{:S(2)}, u32[]{:S(2)}) collective-permute-start(bf16[4,128,640]{2,1,0:T(8,128)(2,1)S(1)} %pad_maximum_fusion.a_own), channel_id=1, source_target_pairs={{0,8},{4,60},{8,16},{12,4},{16,24},{20,12},{24,32},{28,20},{32,40}... | collective-permute-start | bytes 1966088 | tf_op jit(solution)/shard_map/ppermute | solution.py:23
  37.5 12.0 %collective-permute-start.20 = (bf16[128,640]{1,0:T(8,128)(2,1)S(1)}, bf16[128,640]{1,0:T(8,128)(2,1)S(1)}, u32[]{:S(2)}, u32[]{:S(2)}) collective-permute-start(bf16[128,640]{1,0:T(8,128)(2,1)S(1)} %collective-permute-done.16), channel_id=1, source_target_pairs={{0,4},{4,0},{1,5},{5,1},{2,6},{6,2},{3,7},{7,3},{8,12},{12,8},{9,1... | collective-permute-start | bytes 491528 | tf_op jit(solution)/shard_map/ppermute | solution.py:23
  47.5 2.7 %collective-permute-start.21 = (bf16[2,128,640]{2,1,0:T(8,128)(2,1)S(1)}, bf16[2,128,640]{2,1,0:T(8,128)(2,1)S(1)}, u32[]{:S(2)}, u32[]{:S(2)}) collective-permute-start(bf16[2,128,640]{2,1,0:T(8,128)(2,1)S(1)} %collective-permute-done.17), channel_id=1, source_target_pairs={{0,4},{4,0},{1,5},{5,1},{2,6},{6,2},{3,7},{7,3},{8,12},{12,8},{9,1... | collective-permute-start | bytes 983048 | tf_op jit(solution)/shard_map/ppermute | solution.py:23
  51.6 25.5 %collective-permute-start.22 = (bf16[8,128,640]{2,1,0:T(8,128)(2,1)}, bf16[8,128,640]{2,1,0:T(8,128)(2,1)S(1)}, u32[]{:S(2)}, u32[]{:S(2)}) collective-permute-start(bf16[8,128,640]{2,1,0:T(8,128)(2,1)} %slice_dynamic-update-slice_fusion.b_own), channel_id=1, source_target_pairs={{0,64},{4,196},{64,128},{68,4},{128,192},{132,68},{192,0},{196,132... | collective-permute-start | bytes 3932168 | tf_op jit(solution)/shard_map/ppermute | solution.py:23
  62.6 33.4 %collective-permute-start.2 = (bf16[512,1280]{1,0:T(8,128)(2,1)}, bf16[512,1280]{1,0:T(8,128)(2,1)}, u32[]{:S(2)}, u32[]{:S(2)}) collective-permute-start(bf16[512,1280]{1,0:T(8,128)(2,1)} %attention_backward.1.j0), channel_id=1, source_target_pairs={{0,2},{1,3},{2,0},{3,1},{4,6},{5,7},{6,4},{7,5},{8,10},{9,11},{10,... | collective-permute-start | bytes 3932168 | tf_op jit(solution)/shard_map/ppermute | solution.py:23
  65.2 11.9 %collective-permute-start.9 = (bf16[4,128,640]{2,1,0:T(8,128)(2,1)S(1)}, bf16[4,128,640]{2,1,0:T(8,128)(2,1)}, u32[]{:S(2)}, u32[]{:S(2)}) collective-permute-start(bf16[4,128,640]{2,1,0:T(8,128)(2,1)S(1)} %collective-permute-done.8.a1), channel_id=1, source_target_pairs={{0,8},{4,60},{8,16},{12,4},{16,24},{20,12},{24,32},{28,20},{32,40}... | collective-permute-start | bytes 1966088 | tf_op jit(solution)/shard_map/ppermute | solution.py:23
  65.2 57.6 %collective-permute-start.1 = (bf16[512,1280]{1,0:T(8,128)(2,1)}, bf16[512,1280]{1,0:T(8,128)(2,1)}, u32[]{:S(2)}, u32[]{:S(2)}) collective-permute-start(bf16[512,1280]{1,0:T(8,128)(2,1)} %attention_backward.1.j0), channel_id=1, source_target_pairs={{0,3},{1,0},{2,1},{3,2},{4,7},{5,4},{6,5},{7,6},{8,11},{9,8},{10,9... | collective-permute-start | bytes 3932168 | tf_op jit(solution)/shard_map/ppermute | solution.py:23
  65.2 58.4 %collective-permute-start = (bf16[512,1280]{1,0:T(8,128)(2,1)}, bf16[512,1280]{1,0:T(8,128)(2,1)}, u32[]{:S(2)}, u32[]{:S(2)}) collective-permute-start(bf16[512,1280]{1,0:T(8,128)(2,1)} %attention_backward.1.j0), channel_id=1, source_target_pairs={{0,1},{1,2},{2,3},{3,0},{4,5},{5,6},{6,7},{7,4},{8,9},{9,10},{10,1... | collective-permute-start | bytes 3932168 | tf_op jit(solution)/shard_map/ppermute | solution.py:23
  77.1 18.9 %collective-permute-start.10 = (bf16[4,128,640]{2,1,0:T(8,128)(2,1)}, bf16[4,128,640]{2,1,0:T(8,128)(2,1)S(1)}, u32[]{:S(2)}, u32[]{:S(2)}) collective-permute-start(bf16[4,128,640]{2,1,0:T(8,128)(2,1)} %collective-permute-done.9.a2), channel_id=1, source_target_pairs={{0,8},{4,60},{8,16},{12,4},{16,24},{20,12},{24,32},{28,20},{32,40}... | collective-permute-start | bytes 1966088 | tf_op jit(solution)/shard_map/ppermute | solution.py:23
  77.1 46.5 %collective-permute-start.12 = (bf16[4,128,640]{2,1,0:T(8,128)(2,1)S(1)}, bf16[4,128,640]{2,1,0:T(8,128)(2,1)}, u32[]{:S(2)}, u32[]{:S(2)}) collective-permute-start(bf16[4,128,640]{2,1,0:T(8,128)(2,1)S(1)} %collective-permute-done.8.a1), channel_id=1, source_target_pairs={{0,4},{4,0},{1,5},{5,1},{2,6},{6,2},{3,7},{7,3},{8,12},{12,8},{9,1... | collective-permute-start | bytes 1966088 | tf_op jit(solution)/shard_map/ppermute | solution.py:23
  96.0 27.6 %collective-permute-start.23 = (bf16[4,128,640]{2,1,0:T(8,128)(2,1)}, bf16[4,128,640]{2,1,0:T(8,128)(2,1)}, u32[]{:S(2)}, u32[]{:S(2)}) collective-permute-start(bf16[4,128,640]{2,1,0:T(8,128)(2,1)} %constant_dynamic-slice_fusion), channel_id=1, source_target_pairs={{0,64},{4,196},{64,128},{68,4},{128,192},{132,68},{192,0},{196,132... | collective-permute-start | bytes 1966088 | tf_op jit(solution)/shard_map/ppermute | solution.py:23
  96.0 38.0 %collective-permute-start.24 = (bf16[8,128,640]{2,1,0:T(8,128)(2,1)S(1)}, bf16[8,128,640]{2,1,0:T(8,128)(2,1)}, u32[]{:S(2)}, u32[]{:S(2)}) collective-permute-start(bf16[8,128,640]{2,1,0:T(8,128)(2,1)S(1)} %collective-permute-done.22.b1), channel_id=1, source_target_pairs={{0,4},{4,0},{1,5},{5,1},{2,6},{6,2},{3,7},{7,3},{8,12},{12,8},{9,1... | collective-permute-start | bytes 3932168 | tf_op jit(solution)/shard_map/ppermute | solution.py:23
  122.8 9.3 %collective-permute-start.13 = (bf16[4,128,640]{2,1,0:T(8,128)(2,1)}, bf16[4,128,640]{2,1,0:T(8,128)(2,1)}, u32[]{:S(2)}, u32[]{:S(2)}) collective-permute-start(bf16[4,128,640]{2,1,0:T(8,128)(2,1)} %collective-permute-done.9.a2), channel_id=1, source_target_pairs={{0,4},{4,0},{1,5},{5,1},{2,6},{6,2},{3,7},{7,3},{8,12},{12,8},{9,1... | collective-permute-start | bytes 1966088 | tf_op jit(solution)/shard_map/ppermute | solution.py:23
  123.6 8.4 %collective-permute-start.11 = (bf16[2,128,640]{2,1,0:T(8,128)(2,1)S(1)}, bf16[2,128,640]{2,1,0:T(8,128)(2,1)}, u32[]{:S(2)}, u32[]{:S(2)}) collective-permute-start(bf16[2,128,640]{2,1,0:T(8,128)(2,1)S(1)} %constant_dynamic-slice_fusion.2), channel_id=1, source_target_pairs={{0,8},{4,60},{8,16},{12,4},{16,24},{20,12},{24,32},{28,20},{32,40}... | collective-permute-start | bytes 983048 | tf_op jit(solution)/shard_map/ppermute | solution.py:23
  123.6 10.4 %collective-permute-start.14 = (bf16[4,128,640]{2,1,0:T(8,128)(2,1)S(1)}, bf16[4,128,640]{2,1,0:T(8,128)(2,1)}, u32[]{:S(2)}, u32[]{:S(2)}) collective-permute-start(bf16[4,128,640]{2,1,0:T(8,128)(2,1)S(1)} %collective-permute-done.10.a3), channel_id=1, source_target_pairs={{0,4},{4,0},{1,5},{5,1},{2,6},{6,2},{3,7},{7,3},{8,12},{12,8},{9,1... | collective-permute-start | bytes 1966088 | tf_op jit(solution)/shard_map/ppermute | solution.py:23
  123.6 10.3 %collective-permute-start.25 = (bf16[4,128,640]{2,1,0:T(8,128)(2,1)}, bf16[4,128,640]{2,1,0:T(8,128)(2,1)}, u32[]{:S(2)}, u32[]{:S(2)}) collective-permute-start(bf16[4,128,640]{2,1,0:T(8,128)(2,1)} %collective-permute-done.23.b2), channel_id=1, source_target_pairs={{0,4},{4,0},{1,5},{5,1},{2,6},{6,2},{3,7},{7,3},{8,12},{12,8},{9,1... | collective-permute-start | bytes 1966088 | tf_op jit(solution)/shard_map/ppermute | solution.py:23
  132.0 2.0 %collective-permute-start.15 = (bf16[2,128,640]{2,1,0:T(8,128)(2,1)}, bf16[2,128,640]{2,1,0:T(8,128)(2,1)}, u32[]{:S(2)}, u32[]{:S(2)}) collective-permute-start(bf16[2,128,640]{2,1,0:T(8,128)(2,1)} %collective-permute-done.11.a4), channel_id=1, source_target_pairs={{0,4},{4,0},{1,5},{5,1},{2,6},{6,2},{3,7},{7,3},{8,12},{12,8},{9,1... | collective-permute-start | bytes 983048 | tf_op jit(solution)/shard_map/ppermute | solution.py:23

commit v2 on v1

v2 whole, which is shorter than its diff:
```python
import jax
import jax.numpy as jnp
import numpy as np
from jax import lax
from jax.experimental import pallas as pl
from jax.experimental.pallas import tpu as pltpu
from jax.sharding import Mesh, PartitionSpec as P

SIZES = {"y": 4, "z": 8, "c": 2, "x": 4}
BLOCK = 128
MASKED = -1e30
ATTENTION_VMEM = 58 << 20
PROJECT_VMEM = 16 << 20
Y_FIRST = 512
LOG2E = 1.4426950408889634


def move(value, axes, target):
    axes = tuple(a for a in SIZES if a in axes)
    dims = [SIZES[a] for a in axes]
    pairs = []
    for source in range(int(np.prod(dims))):
        coords = dict(zip(axes, (int(v) for v in np.unravel_index(source, dims))))
        goal = target(**coords)
        goal = [goal[a] % SIZES[a] for a in axes]
        pairs.append((source, int(np.ravel_multi_index(goal, dims))))
    return lax.ppermute(value, axes, pairs)


def swap_cores(value):
    return move(value, ("c",), lambda c: dict(c=1 - c))


def along(value, axis, steps):
    sign = lambda c: steps if c == 0 else -steps
    return move(value, (axis, "c"), lambda c, **k: {axis: k[axis] + sign(c), "c": c})


def shift(value, axis, steps):
    return move(value, (axis,), lambda **k: {axis: k[axis] + steps})


def nt(a, b):
    return lax.dot_general(a, b, (((1,), (1,)), ((), ())), preferred_element_type=jnp.float32)


def nn(a, b):
    return jnp.dot(a, b, preferred_element_type=jnp.float32)


def attention_kernel(q_ref, do_ref, k_ref, v_ref, lse_ref, delta_ref, seg_ref, out_ref,
                     bias, key_t, lse_f, delta_f, dk_acc, dv_acc):
    head = pl.program_id(0)
    heads = pl.num_programs(0)
    window, size = k_ref.shape
    scale = size ** -0.5

    @pl.when(head == 0)
    def _():
        lse_f[...] = lse_ref[...].astype(jnp.float32) * LOG2E
        delta_f[...] = delta_ref[...].astype(jnp.float32)
        key_t[...] = k_ref[...].astype(jnp.float32).T.astype(jnp.bfloat16)
        seg_row = seg_ref[...].astype(jnp.float32)
        seg_col = jnp.broadcast_to(seg_row, (BLOCK, window)).T
        row = lax.broadcasted_iota(jnp.int32, (window, BLOCK), 0)
        col = lax.broadcasted_iota(jnp.int32, (window, BLOCK), 1)
        for start in range(0, window, BLOCK):
            same = seg_col == seg_row[:, start:start + BLOCK]
            bias[:, start:start + BLOCK] = jnp.where(same & (row <= col + start), 0.0, MASKED)
        dk_acc[...] = jnp.zeros_like(dk_acc)
        dv_acc[...] = jnp.zeros_like(dv_acc)

    lse = lse_f[pl.ds(head, 1), :]
    delta = delta_f[pl.ds(head, 1), :]
    parts = []
    for start in range(0, window, BLOCK):
        rows = slice(start, start + BLOCK)
        query = q_ref[start:, :]
        dout = do_ref[start:, :]
        scores = nt(k_ref[rows, :], query)
        probs = jnp.exp2(scores * (scale * LOG2E) - lse[:, start:] + bias[rows, start:])
        grad_prob = nt(v_ref[rows, :], dout)
        grad_score = (probs * (grad_prob - delta[:, start:])).astype(jnp.bfloat16)
        dv_acc[rows, :] += nn(probs.astype(jnp.bfloat16), dout)
        dk_acc[rows, :] += nn(grad_score, query)
        parts.append(nn(key_t[:, rows], grad_score))
    for start in range(0, window, BLOCK):
        total = parts[0][:, start:start + BLOCK]
        for index in range(1, start // BLOCK + 1):
            first = start - index * BLOCK
            total += parts[index][:, first:first + BLOCK]
        out_ref[start:start + BLOCK, pl.ds(pl.multiple_of(head * size, size), size)] = (
            (total * scale).T.astype(jnp.bfloat16)
        )

    @pl.when(head == heads - 1)
    def _():
        out_ref[:, heads * size:(heads + 1) * size] = (dk_acc[...] * scale).astype(jnp.bfloat16)
        out_ref[:, (heads + 1) * size:] = dv_acc[...].astype(jnp.bfloat16)


def joined_gradients(query, dout, key, value, lse, delta, seg):
    window, width = query.shape
    size = key.shape[1]
    heads = width // size
    whole = lambda shape: pl.BlockSpec(shape, lambda r: (0, 0))
    per_head = pl.BlockSpec((window, size), lambda r: (0, r))
    return pl.pallas_call(
        attention_kernel,
        grid=(heads,),
        in_specs=[per_head, per_head, whole((window, size)), whole((window, size)),
                  whole((heads, window)), whole((heads, window)), whole((1, window))],
        out_specs=whole((window, width + 2 * size)),
        out_shape=jax.ShapeDtypeStruct((window, width + 2 * size), jnp.bfloat16),
        scratch_shapes=[
            pltpu.VMEM((window, window), jnp.float32),
            pltpu.VMEM((size, window), jnp.bfloat16),
            pltpu.VMEM((heads, window), jnp.float32),
            pltpu.VMEM((heads, window), jnp.float32),
            pltpu.VMEM((window, size), jnp.float32),
            pltpu.VMEM((window, size), jnp.float32),
        ],
        compiler_params=pltpu.CompilerParams(vmem_limit_bytes=ATTENTION_VMEM),
        cost_estimate=pl.CostEstimate(flops=4 * 10 ** 9, bytes_accessed=4 * 10 ** 6, transcendentals=10 ** 6),
        name="attention_backward",
    )(query, dout, key, value, lse, delta, seg)


def slot_offsets(c, part):
    sign = 1 - 2 * c
    first = 4 * c if part == "lo" else 4 - 4 * c
    step = -sign if part == "lo" else sign
    return [first] + [step * k for k in (1, 2, 3)]


class Plan:
    def __init__(self, joined, slots, rows, first, last):
        self.joined, self.slots, self.rows, self.first, self.last = joined, slots, rows, first, last


def projection_kernel(plan, where_ref, *refs):
    y, z, c, x = (where_ref[i] for i in range(4))
    sign = 1 - 2 * c
    refs = list(refs)
    acc_in = None if plan.first else refs.pop(0)
    heads = [refs.pop(0) for _ in plan.joined]
    slots = []
    for offset in plan.slots:
        slots.append([refs.pop(0), refs.pop(0)] if offset == "far" else [refs.pop(0)])
    rows = [refs.pop(0) for _ in plan.rows]
    out_ref, joined, acc = refs
    width = heads[0].shape[1]
    split = Y_FIRST

    def steps(offset):
        return 2 if offset in (2, "far") else sign * offset

    def tile(offset):
        return pl.ds(pl.multiple_of(((z + 8 + offset) % 8) * BLOCK, BLOCK), BLOCK)

    if plan.first:
        acc[...] = jnp.zeros_like(acc)
    else:
        acc[...] = acc_in[...]
    if plan.rows:
        for index, source in enumerate(heads):
            joined[index] = source[:, split:]

    def slot(sources, offset, g):
        if len(sources) == 2:
            k = (y - g + 4) % 4
            mine, theirs = sources
            from_zero = k < 2
            index_zero = jnp.where(from_zero, k, 0)
            index_one = jnp.where(from_zero, 0, (4 - k) % 4 - 1)
            index = jnp.where(from_zero, index_zero, index_one)
            holder = jnp.where(from_zero, 0, 1)
            return jnp.where(holder == c, mine[index], theirs[index])
        made_here = offset <= 0
        direction = sign if made_here else -sign
        return sources[0][((y - g) * direction + 4) % 4]

    for pair in range(0, len(slots), 2):
        total = None
        for source, head in zip(heads, plan.joined):
            g = (x + steps(head) + 4) % 4
            block = jnp.concatenate([slot(slots[pair + k], plan.slots[pair + k], g) for k in range(2)], axis=0)
            term = nt(source[:, :split], block)
            total = term if total is None else total + term
        for k in range(2):
            offset = plan.slots[pair + k]
            acc[:, tile(4 if offset == "far" else sign * offset)] += total[:, k * BLOCK:(k + 1) * BLOCK]

    for source, (part, same, offset, against) in zip(rows, plan.rows):
        g = (y + 4 + steps(offset)) % 4
        index = jnp.int32(-1)
        for position, head in enumerate(plan.joined):
            if head in against:
                index = jnp.where((x + steps(head) + 4) % 4 == g, position, index)
        offsets = slot_offsets(c if same else 1 - c, part)

        def body(source=source, index=index, offsets=offsets):
            for pair in (0, 2):
                block = source[pair:pair + 2].reshape(2 * BLOCK, width - split)
                term = nt(joined[index], block)
                for k in range(2):
                    acc[:, tile(offsets[pair + k])] += term[:, k * BLOCK:(k + 1) * BLOCK]

        if len(against) == 4:
            body()
        else:
            pl.when(index >= 0)(body)
    out_ref[...] = acc[...].astype(out_ref.dtype)


def projection(plan, name, where, *operands):
    window, width = operands[0 if plan.first else 1].shape
    columns = 8 * BLOCK
    vmem = pl.BlockSpec(memory_space=pltpu.VMEM)
    share = (len(plan.joined) * len(plan.slots) + len(plan.rows)) / 40
    return pl.pallas_call(
        lambda *refs: projection_kernel(plan, *refs),
        in_specs=[pl.BlockSpec(memory_space=pltpu.SMEM)] + [vmem] * len(operands),
        out_specs=vmem,
        out_shape=jax.ShapeDtypeStruct((window, columns), jnp.bfloat16 if plan.last else jnp.float32),
        scratch_shapes=[
            pltpu.VMEM((len(plan.joined) if plan.rows else 1, window, width - Y_FIRST), jnp.bfloat16),
            pltpu.VMEM((window, columns), jnp.float32),
        ],
        compiler_params=pltpu.CompilerParams(vmem_limit_bytes=PROJECT_VMEM),
        cost_estimate=pl.CostEstimate(
            flops=int(1e9 * share), bytes_accessed=int(1e6 * share), transcendentals=0),
        name=name,
    )(where, *operands)


ALL = (0, -1, 1, 2)
NEAR = (0, -1, 1)


def rows_of(against):
    return [("lo", True, 0, against), ("hi", True, 0, against), ("lo", True, -1, against),
            ("hi", True, -1, against), ("lo", False, 1, against), ("hi", False, 1, against)]


def in_order(*values):
    return lax.optimization_barrier(values)


def on_device(query_rows, key_rows, value_rows, output_gradient, row_logsumexp, row_delta_sums,
              segments, query_key_value_weight):
    window, _, width = query_rows.shape
    place = [lax.axis_index(a) for a in ("y", "z", "c", "x")]
    core = place[2]
    where = jnp.stack(place).astype(jnp.int32)
    token_index = (place[0] * SIZES["z"] + place[1]) * SIZES["c"] + core

    weight = query_key_value_weight[:, 0]
    rows = weight.shape[0]
    turned = move(weight, ("y", "x"), lambda y, x: dict(y=x, x=y))

    seg = lax.dynamic_slice_in_dim(segments, token_index * window, window).reshape(1, window)
    joined = joined_gradients(
        query_rows.reshape(window, width), output_gradient.reshape(window, width),
        key_rows[:, 0], value_rows[:, 0], row_logsumexp[0], row_delta_sums[0], seg)
    j_first = along(joined, "x", 1)

    turned, joined, where = in_order(turned, joined, where)
    other = swap_cores(turned)
    j_second = along(joined, "x", -1)
    block = jnp.concatenate([jnp.where(core == 0, turned, other), jnp.where(core == 0, other, turned)], axis=0)
    a_block, b_block = in_order(block[:, :Y_FIRST], block[:, Y_FIRST:])
    own_half = lax.dynamic_slice_in_dim(b_block, core * rows, rows, 0)

    b1 = along(b_block, "z", 1)
    a_first = along(a_block, "y", 1)
    a_second = along(a_block, "y", -1)
    a_far = along(a_block, "y", 2)
    b4 = along(own_half, "z", 4)
    b23 = along(jnp.stack([b1, b_block]), "z", 2)
    a_own = jnp.stack([a_block, a_first, a_far, a_second])
    a1 = along(a_own, "z", 1)
    x1, x4, x23 = swap_cores(b1), swap_cores(b4), swap_cores(b23)
    far = jnp.concatenate([jnp.where(core == 0, b4, x4), jnp.where(core == 0, x4, b4)], axis=0)
    lo = jnp.stack([jnp.where(core == 0, b_block, far), b1, b23[1], b23[0]])
    hi = jnp.stack([jnp.where(core == 0, far, b_block), x1, x23[1], x23[0]])
    lo, hi = in_order(lo, hi)
    lo_next = along(lo, "y", 1)
    a2 = along(a1, "z", 1)
    ax1 = swap_cores(a1)
    hi_next = along(hi, "y", 1)
    lo_far = along(lo_next, "y", 1)
    a3 = along(a2, "z", 1)
    ax2 = swap_cores(a2)
    lo_x, hi_x = swap_cores(lo_next), swap_cores(hi_next)
    j_far = along(j_first, "x", 1)
    a4 = along(lax.dynamic_slice_in_dim(a3, core, 2, 0), "z", 1)
    far_x = swap_cores(lo_far)
    ax3 = swap_cores(a3)
    ax4 = swap_cores(a4)

    ring = (a_own, a1, ax1, a2)
    near_rows = (lo, hi, lo_next, hi_next, lo_x, hi_x)
    acc = projection(Plan(NEAR, (0, -1, 1, -2), rows_of(NEAR), True, False), "project_near", where,
                     joined, j_first, j_second, *ring, *near_rows)
    acc = projection(Plan((2,), (0, -1, 1, -2), rows_of((2,)), False, False), "project_far_head", where,
                     acc, j_far, *ring, *near_rows)
    far_rows = [("lo", True, "far", ALL), ("lo", False, "far", ALL)]
    return projection(Plan(ALL, (2, -3, 3, "far"), far_rows, False, True), "project_rest", where,
                      acc, joined, j_first, j_second, j_far, ax2, a3, ax3, a4, ax4, lo_far, far_x)


def solution(mesh):
    grid = Mesh(mesh.devices.reshape(4, 8, 2, 4), ("y", "z", "c", "x"))
    tok = ("y", "z", "c")
    rows = P(tok, "x", None)
    placed = (rows, rows, rows, rows, P("x", None, tok), P("x", None, tok), P(), rows)
    return jax.shard_map(on_device, mesh=grid, in_specs=placed, out_specs=P(tok, "x"), check_vma=False)
```

time: 150 us -> 108 us (0.72)
  the two profiles are of different devices: /device:TPU:8 before, /device:TPU:1 now
where the time goes in v2:
time: 108 us
  starting transfers between devices  44.2 us (41%)
  Pallas kernels  30 us (28%)
  waiting for transfers between devices  27.2 us (25%)
  local copies, waits for them, and re-layouts  5.87 us (5%)
    ppermute x28, starting transfers between devices, move(): return lax.ppermute(value, axes, pairs)  44.2 us
    ppermute x28, waiting for transfers between devices, move(): return lax.ppermute(value, axes, pairs)  27.2 us
    pallas_call x3, Pallas kernels, projection(): pl.pallas_call(lambda *refs: projection_kernel(plan, *refs), in_specs=[pl...  18.5 us
    pallas_call x1, Pallas kernels, joined_gradients(): pl.pallas_call(attention_kernel, grid=(heads,), in_specs=[per_head, per_h...  11.6 us
    unnamed x18, local copies, waits for them, and re-layouts  3.45 us
  transfers between devices with their start and end apart: 28, of which 8 were waited for; matrix products, arithmetic and copies ran while one was open for 3% of the time, Pallas kernels for 22%

profile of v2, /device:TPU:1, one launch (start us, length us, event | category | flops | bytes accessed | tf_op | source)
XLA Modules:
  0.0 108.0 jit_solution(11226242735972475443)
XLA Ops:
  0.0 1.6 %collective-permute-start = (bf16[64,1280]{1,0:T(8,128)(2,1)}, bf16[64,1280]{1,0:T(8,128)(2,1)S(1)}, u32[]{:S(2)}, u32[]{:S(2)}) collective-permute-start(bf16[64,1280]{1,0:T(8,128)(2,1)} %bitcast.34), channel_id=1, source_target_pairs={{0,0},{1,64},{2,128},{3,192},{64,1},{65,65},{66,129},{67,193},{128... | collective-permute-start | bytes 491528 | tf_op jit(solution)/shard_map/ppermute | solution.py:27
  1.6 1.3 %dynamic_slice.9 = s32[512]{0:T(512)} dynamic-slice(s32[32768]{0:T(1024)} %param.14, s32[]{:T(128)S(6)} %select_n.45), dynamic_slice_sizes={512} | dynamic-slice | bytes 4100 | tf_op jit(solution)/shard_map/dynamic_slice | solution.py:262
  2.9 11.6 %attention_backward.1.refs_1_.refs_2_ = bf16[512,1280]{1,0:T(8,128)(2,1)} custom-call(bf16[512,1024]{1,0:T(8,128)(2,1)} %bitcast.32, bf16[512,1024]{1,0:T(8,128)(2,1)} %bitcast.33, bf16[512,128]{1,0:T(8,128)(2,1)} %bitcast.35, bf16[512,128]{1,0:T(8,128)(2,1)} %bitcast.36, bf16[8,512]{1,0:T(8,128)(2,1)} %bitcast.37, bf16[8,512]{1,0:T(8,128)(2,1)} %bitcast.38, ...), custom_call_target="tpu_custom_call" | custom-call | flops 4000000000 | bytes 4000000 | tf_op jit(solution)/shard_map/attention_backward/pallas_call | solution.py:108
  14.5 0.1 pad_add_fusion.refs_0_
  14.5 3.3 %collective-permute-start.3 = (bf16[64,1280]{1,0:T(8,128)(2,1)S(1)}, bf16[64,1280]{1,0:T(8,128)(2,1)S(1)}, u32[]{:S(2)}, u32[]{:S(2)}) collective-permute-start(bf16[64,1280]{1,0:T(8,128)(2,1)S(1)} %collective-permute-done), channel_id=1, source_target_pairs={{0,4},{4,0},{1,5},{5,1},{2,6},{6,2},{3,7},{7,3},{8,12},{12,8},{9,1... | collective-permute-start | bytes 491528 | tf_op jit(solution)/shard_map/ppermute | solution.py:27
  17.8 1.0 collective-permute-done.3
  18.9 3.9 %collective-permute-start.12 = (bf16[128,768]{1,0:T(8,128)(2,1)S(1)}, bf16[128,768]{1,0:T(8,128)(2,1)S(1)}, u32[]{:S(2)}, u32[]{:S(2)}) collective-permute-start(bf16[128,768]{1,0:T(8,128)(2,1)S(1)} %pad_maximum_fusion.4), channel_id=1, source_target_pairs={{0,8},{4,60},{8,16},{12,4},{16,24},{20,12},{24,32},{28,20},{32,40}... | collective-permute-start | bytes 589832 | tf_op jit(solution)/shard_map/ppermute | solution.py:27
  22.8 5.5 %collective-permute-start.4 = (bf16[128,512]{1,0:T(8,128)(2,1)S(1)}, bf16[128,512]{1,0:T(8,128)(2,1)S(1)}, u32[]{:S(2)}, u32[]{:S(2)}) collective-permute-start(bf16[128,512]{1,0:T(8,128)(2,1)S(1)} %pad_maximum_fusion.6), channel_id=1, source_target_pairs={{0,64},{4,196},{64,128},{68,4},{128,192},{132,68},{192,0},{196,132... | collective-permute-start | bytes 393224 | tf_op jit(solution)/shard_map/ppermute | solution.py:27
  28.3 0.6 collective-permute-start.5
  28.9 0.9 collective-permute-start.6
  29.8 1.5 %collective-permute-start.10 = (bf16[64,768]{1,0:T(8,128)(2,1)S(1)}, bf16[64,768]{1,0:T(8,128)(2,1)S(1)}, u32[]{:S(2)}, u32[]{:S(2)}) collective-permute-start(bf16[64,768]{1,0:T(8,128)(2,1)S(1)} %constant_dynamic-slice_fusion.1), channel_id=1, source_target_pairs={{0,32},{4,36},{8,40},{12,44},{16,48},{20,52},{24,56},{28,60},{32,0... | collective-permute-start | bytes 294920 | tf_op jit(solution)/shard_map/ppermute | solution.py:27
  31.3 0.1 collective-permute-start.13
  31.4 7.4 %collective-permute-done.10 = bf16[64,768]{1,0:T(8,128)(2,1)S(1)} collective-permute-done((bf16[64,768]{1,0:T(8,128)(2,1)S(1)}, bf16[64,768]{1,0:T(8,128)(2,1)S(1)}, u32[]{:S(2)}, u32[]{:S(2)}) %collective-permute-start.10) | collective-permute-done | bytes 98336 | tf_op jit(solution)/shard_map/ppermute | solution.py:27
  38.8 1.4 %collective-permute-start.1 = (bf16[512,1280]{1,0:T(8,128)(2,1)S(1)}, bf16[512,1280]{1,0:T(8,128)(2,1)}, u32[]{:S(2)}, u32[]{:S(2)}) collective-permute-start(bf16[512,1280]{1,0:T(8,128)(2,1)S(1)} %copy-done), channel_id=1, source_target_pairs={{0,1},{1,2},{2,3},{3,0},{4,7},{5,4},{6,5},{7,6},{8,9},{9,10},{10,1... | collective-permute-start | bytes 3932168 | tf_op jit(solution)/shard_map/ppermute | solution.py:27
  40.3 2.1 %collective-permute-start.11 = (bf16[64,768]{1,0:T(8,128)(2,1)S(1)}, bf16[64,768]{1,0:T(8,128)(2,1)S(1)}, u32[]{:S(2)}, u32[]{:S(2)}) collective-permute-start(bf16[64,768]{1,0:T(8,128)(2,1)S(1)} %collective-permute-done.10), channel_id=1, source_target_pairs={{0,4},{4,0},{1,5},{5,1},{2,6},{6,2},{3,7},{7,3},{8,12},{12,8},{9,1... | collective-permute-start | bytes 294920 | tf_op jit(solution)/shard_map/ppermute | solution.py:27
  42.4 0.1 pad_maximum_fusion.2.refs_4_.refs_3_
  42.5 4.2 %collective-permute-start.7 = (bf16[4,128,512]{2,1,0:T(8,128)(2,1)S(1)}, bf16[4,128,512]{2,1,0:T(8,128)(2,1)}, u32[]{:S(2)}, u32[]{:S(2)}) collective-permute-start(bf16[4,128,512]{2,1,0:T(8,128)(2,1)S(1)} %pad_maximum_fusion.2.refs_4_.refs_3_), channel_id=1, source_target_pairs={{0,8},{4,60},{8,16},{12,4},{16,24},{20,12},{24,32},{28,20},{32,40}... | collective-permute-start | bytes 1572872 | tf_op jit(solution)/shard_map/ppermute | solution.py:27
  46.8 0.1 collective-permute-start.15
  46.9 0.1 select_bitcast_fusion
  46.9 0.6 collective-permute-start.14
  47.5 0.1 pad_maximum_fusion.refs_8_.refs_7_
  47.7 5.2 %collective-permute-done.7.refs_5_.refs_4_ = bf16[4,128,512]{2,1,0:T(8,128)(2,1)} collective-permute-done((bf16[4,128,512]{2,1,0:T(8,128)(2,1)S(1)}, bf16[4,128,512]{2,1,0:T(8,128)(2,1)}, u32[]{:S(2)}, u32[]{:S(2)}) %collective-permute-start.7) | collective-permute-done | bytes 524320 | tf_op jit(solution)/shard_map/ppermute | solution.py:27
  52.9 3.5 %collective-permute-start.9 = (bf16[4,128,512]{2,1,0:T(8,128)(2,1)}, bf16[4,128,512]{2,1,0:T(8,128)(2,1)S(1)}, u32[]{:S(2)}, u32[]{:S(2)}) collective-permute-start(bf16[4,128,512]{2,1,0:T(8,128)(2,1)} %collective-permute-done.7.refs_5_.refs_4_), channel_id=1, source_target_pairs={{0,8},{4,60},{8,16},{12,4},{16,24},{20,12},{24,32},{28,20},{32,40}... | collective-permute-start | bytes 1572872 | tf_op jit(solution)/shard_map/ppermute | solution.py:27
  56.4 0.1 pad_maximum_fusion.1.refs_9_.refs_8_
  56.5 0.2 collective-permute-start.16
  56.7 0.3 collective-permute-start.17
  57.0 5.8 %collective-permute-done.9.refs_7_.refs_6_ = bf16[4,128,512]{2,1,0:T(8,128)(2,1)S(1)} collective-permute-done((bf16[4,128,512]{2,1,0:T(8,128)(2,1)}, bf16[4,128,512]{2,1,0:T(8,128)(2,1)S(1)}, u32[]{:S(2)}, u32[]{:S(2)}) %collective-permute-start.9) | collective-permute-done | bytes 524320 | tf_op jit(solution)/shard_map/ppermute | solution.py:27
  62.8 3.4 %collective-permute-start.22 = (bf16[4,128,512]{2,1,0:T(8,128)(2,1)S(1)}, bf16[4,128,512]{2,1,0:T(8,128)(2,1)S(1)}, u32[]{:S(2)}, u32[]{:S(2)}) collective-permute-start(bf16[4,128,512]{2,1,0:T(8,128)(2,1)S(1)} %collective-permute-done.9.refs_7_.refs_6_), channel_id=1, source_target_pairs={{0,8},{4,60},{8,16},{12,4},{16,24},{20,12},{24,32},{28,20},{32,40}... | collective-permute-start | bytes 1572872 | tf_op jit(solution)/shard_map/ppermute | solution.py:27
  66.2 1.6 %collective-permute-done.16.refs_10_.refs_9_ = bf16[4,128,768]{2,1,0:T(8,128)(2,1)} collective-permute-done((bf16[4,128,768]{2,1,0:T(8,128)(2,1)S(1)}, bf16[4,128,768]{2,1,0:T(8,128)(2,1)}, u32[]{:S(2)}, u32[]{:S(2)}) %collective-permute-start.16) | collective-permute-done | bytes 786464 | tf_op jit(solution)/shard_map/ppermute | solution.py:27
  67.8 1.0 collective-permute-start.26
  68.9 1.9 %collective-permute-start.20 = (bf16[512,1280]{1,0:T(8,128)(2,1)}, bf16[512,1280]{1,0:T(8,128)(2,1)}, u32[]{:S(2)}, u32[]{:S(2)}) collective-permute-start(bf16[512,1280]{1,0:T(8,128)(2,1)} %collective-permute-done.1.refs_2_.refs_3_), channel_id=1, source_target_pairs={{0,1},{1,2},{2,3},{3,0},{4,7},{5,4},{6,5},{7,6},{8,9},{9,10},{10,1... | collective-permute-start | bytes 3932168 | tf_op jit(solution)/shard_map/ppermute | solution.py:27
  70.8 1.0 collective-permute-done.2.refs_3_.refs_4_
  71.8 1.1 copy-done.1
  72.8 2.6 %collective-permute-start.18 = (bf16[4,128,768]{2,1,0:T(8,128)(2,1)}, bf16[4,128,768]{2,1,0:T(8,128)(2,1)}, u32[]{:S(2)}, u32[]{:S(2)}) collective-permute-start(bf16[4,128,768]{2,1,0:T(8,128)(2,1)} %collective-permute-done.16.refs_10_.refs_9_), channel_id=1, source_target_pairs={{0,4},{4,0},{1,5},{5,1},{2,6},{6,2},{3,7},{7,3},{8,12},{12,8},{9,1... | collective-permute-start | bytes 2359304 | tf_op jit(solution)/shard_map/ppermute | solution.py:27
  75.4 0.8 collective-permute-done.17.refs_11_.refs_10_
  76.3 1.6 %collective-permute-start.19 = (bf16[4,128,768]{2,1,0:T(8,128)(2,1)}, bf16[4,128,768]{2,1,0:T(8,128)(2,1)}, u32[]{:S(2)}, u32[]{:S(2)}) collective-permute-start(bf16[4,128,768]{2,1,0:T(8,128)(2,1)} %collective-permute-done.17.refs_11_.refs_10_), channel_id=1, source_target_pairs={{0,4},{4,0},{1,5},{5,1},{2,6},{6,2},{3,7},{7,3},{8,12},{12,8},{9,1... | collective-permute-start | bytes 2359304 | tf_op jit(solution)/shard_map/ppermute | solution.py:27
  77.8 1.0 constant_dynamic-slice_fusion
  78.9 1.6 %collective-permute-start.24 = (bf16[2,128,512]{2,1,0:T(8,128)(2,1)S(1)}, bf16[2,128,512]{2,1,0:T(8,128)(2,1)S(1)}, u32[]{:S(2)}, u32[]{:S(2)}) collective-permute-start(bf16[2,128,512]{2,1,0:T(8,128)(2,1)S(1)} %constant_dynamic-slice_fusion), channel_id=1, source_target_pairs={{0,8},{4,60},{8,16},{12,4},{16,24},{20,12},{24,32},{28,20},{32,40}... | collective-permute-start | bytes 786440 | tf_op jit(solution)/shard_map/ppermute | solution.py:27
  80.5 4.2 %collective-permute-done.26.refs_11_ = bf16[4,128,768]{2,1,0:T(8,128)(2,1)} collective-permute-done((bf16[4,128,768]{2,1,0:T(8,128)(2,1)}, bf16[4,128,768]{2,1,0:T(8,128)(2,1)}, u32[]{:S(2)}, u32[]{:S(2)}) %collective-permute-start.26) | collective-permute-done | bytes 786464 | tf_op jit(solution)/shard_map/ppermute | solution.py:27
  84.7 1.6 %collective-permute-start.27 = (bf16[4,128,768]{2,1,0:T(8,128)(2,1)}, bf16[4,128,768]{2,1,0:T(8,128)(2,1)S(1)}, u32[]{:S(2)}, u32[]{:S(2)}) collective-permute-start(bf16[4,128,768]{2,1,0:T(8,128)(2,1)} %collective-permute-done.26.refs_11_), channel_id=1, source_target_pairs={{0,4},{4,0},{1,5},{5,1},{2,6},{6,2},{3,7},{7,3},{8,12},{12,8},{9,1... | collective-permute-start | bytes 2359304 | tf_op jit(solution)/shard_map/ppermute | solution.py:27
  86.3 0.3 collective-permute-start.21
  86.6 0.2 collective-permute-start.23
  86.8 0.3 collective-permute-start.25
  87.1 1.3 %copy-done.2 = bf16[512,1280]{1,0:T(8,128)(2,1)S(1)} copy-done((bf16[512,1280]{1,0:T(8,128)(2,1)S(1)}, bf16[512,1280]{1,0:T(8,128)(2,1)}, u32[]{:S(2)}) %copy-start.2) | copy-done | bytes 1310744
  88.4 1.0 copy-done.5
  89.4 8.7 %project_near.1.refs_1_ = f32[512,1024]{1,0:T(8,128)S(1)} custom-call(s32[4]{0:T(128)S(1)} %pad_add_fusion.refs_0_, bf16[512,1280]{1,0:T(8,128)(2,1)S(1)} %copy-done, bf16[512,1280]{1,0:T(8,128)(2,1)} %collective-permute-done.1.refs_2_.refs_3_, bf16[512,1280]{1,0:T(8,128)(2,1)S(1)} %copy-done.2, bf16[4,128,512]{2,1,0:T(8,128)(2,1)S(1)} %pad_maximum_fusion.2.refs_4_.refs_3_, ...), custom_call_target="tpu_custom_call" | custom-call | flops 450000000 | bytes 450000 | tf_op jit(solution)/shard_map/project_near/pallas_call | solution.py:221
  98.2 3.8 %project_far_head.1.refs_1_ = f32[512,1024]{1,0:T(8,128)S(1)} custom-call(s32[4]{0:T(128)S(1)} %pad_add_fusion.refs_0_, f32[512,1024]{1,0:T(8,128)S(1)} %project_near.1.refs_1_, bf16[512,1280]{1,0:T(8,128)(2,1)} %collective-permute-done.20.refs_2_.refs_5_, bf16[4,128,512]{2,1,0:T(8,128)(2,1)S(1)} %pad_maximum_fusion.2.refs_4_.refs_3_, ...), custom_call_target="tpu_custom_call" | custom-call | flops 250000000 | bytes 250000 | tf_op jit(solution)/shard_map/project_far_head/pallas_call | solution.py:221
  102.0 6.0 %project_rest.1 = bf16[512,1024]{1,0:T(8,128)(2,1)} custom-call(s32[4]{0:T(128)S(1)} %pad_add_fusion.refs_0_, f32[512,1024]{1,0:T(8,128)S(1)} %project_far_head.1.refs_1_, bf16[512,1280]{1,0:T(8,128)(2,1)S(1)} %copy-done, bf16[512,1280]{1,0:T(8,128)(2,1)} %collective-permute-done.1.refs_2_.refs_3_, bf16[512,1280]{1,0:T(8,128)(2,1)S(1)} %copy-done.3, ...), custom_call_target="tpu_custom_call" | custom-call | flops 450000000 | bytes 450000 | tf_op jit(solution)/shard_map/project_rest/pallas_call | solution.py:221
  (45 shorter events, 0.3 us)
Async XLA Ops:
  0.0 14.5 %collective-permute-start = (bf16[64,1280]{1,0:T(8,128)(2,1)}, bf16[64,1280]{1,0:T(8,128)(2,1)S(1)}, u32[]{:S(2)}, u32[]{:S(2)}) collective-permute-start(bf16[64,1280]{1,0:T(8,128)(2,1)} %bitcast.34), channel_id=1, source_target_pairs={{0,0},{1,64},{2,128},{3,192},{64,1},{65,65},{66,129},{67,193},{128... | collective-permute-start | bytes 491528 | tf_op jit(solution)/shard_map/ppermute | solution.py:27
  14.5 4.3 %collective-permute-start.3 = (bf16[64,1280]{1,0:T(8,128)(2,1)S(1)}, bf16[64,1280]{1,0:T(8,128)(2,1)S(1)}, u32[]{:S(2)}, u32[]{:S(2)}) collective-permute-start(bf16[64,1280]{1,0:T(8,128)(2,1)S(1)} %collective-permute-done), channel_id=1, source_target_pairs={{0,4},{4,0},{1,5},{5,1},{2,6},{6,2},{3,7},{7,3},{8,12},{12,8},{9,1... | collective-permute-start | bytes 491528 | tf_op jit(solution)/shard_map/ppermute | solution.py:27
  17.8 21.0 %copy-start = (bf16[512,1280]{1,0:T(8,128)(2,1)S(1)}, bf16[512,1280]{1,0:T(8,128)(2,1)}, u32[]{:S(2)}) copy-start(bf16[512,1280]{1,0:T(8,128)(2,1)} %attention_backward.1.refs_1_.refs_2_) | copy-start | bytes 3932164
  18.9 12.4 %collective-permute-start.12 = (bf16[128,768]{1,0:T(8,128)(2,1)S(1)}, bf16[128,768]{1,0:T(8,128)(2,1)S(1)}, u32[]{:S(2)}, u32[]{:S(2)}) collective-permute-start(bf16[128,768]{1,0:T(8,128)(2,1)S(1)} %pad_maximum_fusion.4), channel_id=1, source_target_pairs={{0,8},{4,60},{8,16},{12,4},{16,24},{20,12},{24,32},{28,20},{32,40}... | collective-permute-start | bytes 589832 | tf_op jit(solution)/shard_map/ppermute | solution.py:27
  22.8 17.4 %collective-permute-start.4 = (bf16[128,512]{1,0:T(8,128)(2,1)S(1)}, bf16[128,512]{1,0:T(8,128)(2,1)S(1)}, u32[]{:S(2)}, u32[]{:S(2)}) collective-permute-start(bf16[128,512]{1,0:T(8,128)(2,1)S(1)} %pad_maximum_fusion.6), channel_id=1, source_target_pairs={{0,64},{4,196},{64,128},{68,4},{128,192},{132,68},{192,0},{196,132... | collective-permute-start | bytes 393224 | tf_op jit(solution)/shard_map/ppermute | solution.py:27
  28.3 12.0 %collective-permute-start.5 = (bf16[128,512]{1,0:T(8,128)(2,1)S(1)}, bf16[128,512]{1,0:T(8,128)(2,1)S(1)}, u32[]{:S(2)}, u32[]{:S(2)}) collective-permute-start(bf16[128,512]{1,0:T(8,128)(2,1)S(1)} %pad_maximum_fusion.6), channel_id=1, source_target_pairs={{0,128},{4,132},{64,192},{68,196},{128,0},{132,4},{192,64},{196,68... | collective-permute-start | bytes 393224 | tf_op jit(solution)/shard_map/ppermute | solution.py:27
  28.9 13.5 %collective-permute-start.6 = (bf16[128,512]{1,0:T(8,128)(2,1)S(1)}, bf16[128,512]{1,0:T(8,128)(2,1)S(1)}, u32[]{:S(2)}, u32[]{:S(2)}) collective-permute-start(bf16[128,512]{1,0:T(8,128)(2,1)S(1)} %pad_maximum_fusion.6), channel_id=1, source_target_pairs={{0,192},{4,68},{64,0},{68,132},{128,64},{132,196},{192,128},{196,4... | collective-permute-start | bytes 393224 | tf_op jit(solution)/shard_map/ppermute | solution.py:27
  29.8 9.1 %collective-permute-start.10 = (bf16[64,768]{1,0:T(8,128)(2,1)S(1)}, bf16[64,768]{1,0:T(8,128)(2,1)S(1)}, u32[]{:S(2)}, u32[]{:S(2)}) collective-permute-start(bf16[64,768]{1,0:T(8,128)(2,1)S(1)} %constant_dynamic-slice_fusion.1), channel_id=1, source_target_pairs={{0,32},{4,36},{8,40},{12,44},{16,48},{20,52},{24,56},{28,60},{32,0... | collective-permute-start | bytes 294920 | tf_op jit(solution)/shard_map/ppermute | solution.py:27
  31.3 15.4 %collective-permute-start.13 = (bf16[2,128,768]{2,1,0:T(8,128)(2,1)S(1)}, bf16[2,128,768]{2,1,0:T(8,128)(2,1)S(1)}, u32[]{:S(2)}, u32[]{:S(2)}) collective-permute-start(bf16[2,128,768]{2,1,0:T(8,128)(2,1)S(1)} %pad_maximum_fusion.3), channel_id=1, source_target_pairs={{0,16},{4,52},{8,24},{12,60},{16,32},{20,4},{24,40},{28,12},{32,48... | collective-permute-start | bytes 1179656 | tf_op jit(solution)/shard_map/ppermute | solution.py:27
  38.8 30.1 %collective-permute-start.1 = (bf16[512,1280]{1,0:T(8,128)(2,1)S(1)}, bf16[512,1280]{1,0:T(8,128)(2,1)}, u32[]{:S(2)}, u32[]{:S(2)}) collective-permute-start(bf16[512,1280]{1,0:T(8,128)(2,1)S(1)} %copy-done), channel_id=1, source_target_pairs={{0,1},{1,2},{2,3},{3,0},{4,7},{5,4},{6,5},{7,6},{8,9},{9,10},{10,1... | collective-permute-start | bytes 3932168 | tf_op jit(solution)/shard_map/ppermute | solution.py:27
  40.2 31.5 %collective-permute-start.2 = (bf16[512,1280]{1,0:T(8,128)(2,1)S(1)}, bf16[512,1280]{1,0:T(8,128)(2,1)S(1)}, u32[]{:S(2)}, u32[]{:S(2)}) collective-permute-start(bf16[512,1280]{1,0:T(8,128)(2,1)S(1)} %copy-done), channel_id=1, source_target_pairs={{0,3},{1,0},{2,1},{3,2},{4,5},{5,6},{6,7},{7,4},{8,11},{9,8},{10,9... | collective-permute-start | bytes 3932168 | tf_op jit(solution)/shard_map/ppermute | solution.py:27
  40.3 6.4 %collective-permute-start.11 = (bf16[64,768]{1,0:T(8,128)(2,1)S(1)}, bf16[64,768]{1,0:T(8,128)(2,1)S(1)}, u32[]{:S(2)}, u32[]{:S(2)}) collective-permute-start(bf16[64,768]{1,0:T(8,128)(2,1)S(1)} %collective-permute-done.10), channel_id=1, source_target_pairs={{0,4},{4,0},{1,5},{5,1},{2,6},{6,2},{3,7},{7,3},{8,12},{12,8},{9,1... | collective-permute-start | bytes 294920 | tf_op jit(solution)/shard_map/ppermute | solution.py:27
  42.5 10.3 %collective-permute-start.7 = (bf16[4,128,512]{2,1,0:T(8,128)(2,1)S(1)}, bf16[4,128,512]{2,1,0:T(8,128)(2,1)}, u32[]{:S(2)}, u32[]{:S(2)}) collective-permute-start(bf16[4,128,512]{2,1,0:T(8,128)(2,1)S(1)} %pad_maximum_fusion.2.refs_4_.refs_3_), channel_id=1, source_target_pairs={{0,8},{4,60},{8,16},{12,4},{16,24},{20,12},{24,32},{28,20},{32,40}... | collective-permute-start | bytes 1572872 | tf_op jit(solution)/shard_map/ppermute | solution.py:27
  46.8 9.6 %collective-permute-start.15 = (bf16[2,128,768]{2,1,0:T(8,128)(2,1)S(1)}, bf16[2,128,768]{2,1,0:T(8,128)(2,1)S(1)}, u32[]{:S(2)}, u32[]{:S(2)}) collective-permute-start(bf16[2,128,768]{2,1,0:T(8,128)(2,1)S(1)} %collective-permute-done.13), channel_id=1, source_target_pairs={{0,4},{4,0},{1,5},{5,1},{2,6},{6,2},{3,7},{7,3},{8,12},{12,8},{9,1... | collective-permute-start | bytes 1179656 | tf_op jit(solution)/shard_map/ppermute | solution.py:27
  46.9 9.5 %collective-permute-start.14 = (bf16[128,768]{1,0:T(8,128)(2,1)S(1)}, bf16[128,768]{1,0:T(8,128)(2,1)S(1)}, u32[]{:S(2)}, u32[]{:S(2)}) collective-permute-start(bf16[128,768]{1,0:T(8,128)(2,1)S(1)} %collective-permute-done.12), channel_id=1, source_target_pairs={{0,4},{4,0},{1,5},{5,1},{2,6},{6,2},{3,7},{7,3},{8,12},{12,8},{9,1... | collective-permute-start | bytes 589832 | tf_op jit(solution)/shard_map/ppermute | solution.py:27
  52.9 10.0 %collective-permute-start.9 = (bf16[4,128,512]{2,1,0:T(8,128)(2,1)}, bf16[4,128,512]{2,1,0:T(8,128)(2,1)S(1)}, u32[]{:S(2)}, u32[]{:S(2)}) collective-permute-start(bf16[4,128,512]{2,1,0:T(8,128)(2,1)} %collective-permute-done.7.refs_5_.refs_4_), channel_id=1, source_target_pairs={{0,8},{4,60},{8,16},{12,4},{16,24},{20,12},{24,32},{28,20},{32,40}... | collective-permute-start | bytes 1572872 | tf_op jit(solution)/shard_map/ppermute | solution.py:27
  56.5 11.3 %collective-permute-start.16 = (bf16[4,128,768]{2,1,0:T(8,128)(2,1)S(1)}, bf16[4,128,768]{2,1,0:T(8,128)(2,1)}, u32[]{:S(2)}, u32[]{:S(2)}) collective-permute-start(bf16[4,128,768]{2,1,0:T(8,128)(2,1)S(1)} %pad_maximum_fusion.refs_8_.refs_7_), channel_id=1, source_target_pairs={{0,64},{4,196},{64,128},{68,4},{128,192},{132,68},{192,0},{196,132... | collective-permute-start | bytes 2359304 | tf_op jit(solution)/shard_map/ppermute | solution.py:27
  56.7 19.5 %collective-permute-start.17 = (bf16[4,128,768]{2,1,0:T(8,128)(2,1)S(1)}, bf16[4,128,768]{2,1,0:T(8,128)(2,1)}, u32[]{:S(2)}, u32[]{:S(2)}) collective-permute-start(bf16[4,128,768]{2,1,0:T(8,128)(2,1)S(1)} %pad_maximum_fusion.1.refs_9_.refs_8_), channel_id=1, source_target_pairs={{0,64},{4,196},{64,128},{68,4},{128,192},{132,68},{192,0},{196,132... | collective-permute-start | bytes 2359304 | tf_op jit(solution)/shard_map/ppermute | solution.py:27
  62.8 13.5 %copy-start.4 = (bf16[4,128,512]{2,1,0:T(8,128)(2,1)}, bf16[4,128,512]{2,1,0:T(8,128)(2,1)S(1)}, u32[]{:S(2)}) copy-start(bf16[4,128,512]{2,1,0:T(8,128)(2,1)S(1)} %collective-permute-done.9.refs_7_.refs_6_) | copy-start | bytes 1572868
  62.8 10.0 %collective-permute-start.22 = (bf16[4,128,512]{2,1,0:T(8,128)(2,1)S(1)}, bf16[4,128,512]{2,1,0:T(8,128)(2,1)S(1)}, u32[]{:S(2)}, u32[]{:S(2)}) collective-permute-start(bf16[4,128,512]{2,1,0:T(8,128)(2,1)S(1)} %collective-permute-done.9.refs_7_.refs_6_), channel_id=1, source_target_pairs={{0,8},{4,60},{8,16},{12,4},{16,24},{20,12},{24,32},{28,20},{32,40}... | collective-permute-start | bytes 1572872 | tf_op jit(solution)/shard_map/ppermute | solution.py:27
  67.8 16.9 %collective-permute-start.26 = (bf16[4,128,768]{2,1,0:T(8,128)(2,1)}, bf16[4,128,768]{2,1,0:T(8,128)(2,1)}, u32[]{:S(2)}, u32[]{:S(2)}) collective-permute-start(bf16[4,128,768]{2,1,0:T(8,128)(2,1)} %collective-permute-done.16.refs_10_.refs_9_), channel_id=1, source_target_pairs={{0,64},{4,196},{64,128},{68,4},{128,192},{132,68},{192,0},{196,132... | collective-permute-start | bytes 2359304 | tf_op jit(solution)/shard_map/ppermute | solution.py:27
  68.9 29.3 %collective-permute-start.20 = (bf16[512,1280]{1,0:T(8,128)(2,1)}, bf16[512,1280]{1,0:T(8,128)(2,1)}, u32[]{:S(2)}, u32[]{:S(2)}) collective-permute-start(bf16[512,1280]{1,0:T(8,128)(2,1)} %collective-permute-done.1.refs_2_.refs_3_), channel_id=1, source_target_pairs={{0,1},{1,2},{2,3},{3,0},{4,7},{5,4},{6,5},{7,6},{8,9},{9,10},{10,1... | collective-permute-start | bytes 3932168 | tf_op jit(solution)/shard_map/ppermute | solution.py:27
  71.8 1.1 copy-start.1
  72.8 6.0 %collective-permute-start.8 = (bf16[4,128,512]{2,1,0:T(8,128)(2,1)}, bf16[4,128,512]{2,1,0:T(8,128)(2,1)}, u32[]{:S(2)}, u32[]{:S(2)}) collective-permute-start(bf16[4,128,512]{2,1,0:T(8,128)(2,1)} %collective-permute-done.7.refs_5_.refs_4_), channel_id=1, source_target_pairs={{0,4},{4,0},{1,5},{5,1},{2,6},{6,2},{3,7},{7,3},{8,12},{12,8},{9,1... | collective-permute-start | bytes 1572872 | tf_op jit(solution)/shard_map/ppermute | solution.py:27
  72.8 3.4 %copy-start.7 = (bf16[4,128,512]{2,1,0:T(8,128)(2,1)}, bf16[4,128,512]{2,1,0:T(8,128)(2,1)S(1)}, u32[]{:S(2)}) copy-start(bf16[4,128,512]{2,1,0:T(8,128)(2,1)S(1)} %collective-permute-done.22.refs_7_) | copy-start | bytes 1572868
  72.8 13.7 %collective-permute-start.18 = (bf16[4,128,768]{2,1,0:T(8,128)(2,1)}, bf16[4,128,768]{2,1,0:T(8,128)(2,1)}, u32[]{:S(2)}, u32[]{:S(2)}) collective-permute-start(bf16[4,128,768]{2,1,0:T(8,128)(2,1)} %collective-permute-done.16.refs_10_.refs_9_), channel_id=1, source_target_pairs={{0,4},{4,0},{1,5},{5,1},{2,6},{6,2},{3,7},{7,3},{8,12},{12,8},{9,1... | collective-permute-start | bytes 2359304 | tf_op jit(solution)/shard_map/ppermute | solution.py:27
  76.3 10.5 %collective-permute-start.19 = (bf16[4,128,768]{2,1,0:T(8,128)(2,1)}, bf16[4,128,768]{2,1,0:T(8,128)(2,1)}, u32[]{:S(2)}, u32[]{:S(2)}) collective-permute-start(bf16[4,128,768]{2,1,0:T(8,128)(2,1)} %collective-permute-done.17.refs_11_.refs_10_), channel_id=1, source_target_pairs={{0,4},{4,0},{1,5},{5,1},{2,6},{6,2},{3,7},{7,3},{8,12},{12,8},{9,1... | collective-permute-start | bytes 2359304 | tf_op jit(solution)/shard_map/ppermute | solution.py:27
  77.8 20.3 %copy-start.6 = (bf16[4,128,512]{2,1,0:T(8,128)(2,1)S(1)}, bf16[4,128,512]{2,1,0:T(8,128)(2,1)}, u32[]{:S(2)}) copy-start(bf16[4,128,512]{2,1,0:T(8,128)(2,1)} %copy-done.4) | copy-start | bytes 1572868
  78.9 7.4 %collective-permute-start.24 = (bf16[2,128,512]{2,1,0:T(8,128)(2,1)S(1)}, bf16[2,128,512]{2,1,0:T(8,128)(2,1)S(1)}, u32[]{:S(2)}, u32[]{:S(2)}) collective-permute-start(bf16[2,128,512]{2,1,0:T(8,128)(2,1)S(1)} %constant_dynamic-slice_fusion), channel_id=1, source_target_pairs={{0,8},{4,60},{8,16},{12,4},{16,24},{20,12},{24,32},{28,20},{32,40}... | collective-permute-start | bytes 786440 | tf_op jit(solution)/shard_map/ppermute | solution.py:27
  84.7 17.3 %collective-permute-start.27 = (bf16[4,128,768]{2,1,0:T(8,128)(2,1)}, bf16[4,128,768]{2,1,0:T(8,128)(2,1)S(1)}, u32[]{:S(2)}, u32[]{:S(2)}) collective-permute-start(bf16[4,128,768]{2,1,0:T(8,128)(2,1)} %collective-permute-done.26.refs_11_), channel_id=1, source_target_pairs={{0,4},{4,0},{1,5},{5,1},{2,6},{6,2},{3,7},{7,3},{8,12},{12,8},{9,1... | collective-permute-start | bytes 2359304 | tf_op jit(solution)/shard_map/ppermute | solution.py:27
  86.3 15.7 %collective-permute-start.21 = (bf16[4,128,512]{2,1,0:T(8,128)(2,1)}, bf16[4,128,512]{2,1,0:T(8,128)(2,1)S(1)}, u32[]{:S(2)}, u32[]{:S(2)}) collective-permute-start(bf16[4,128,512]{2,1,0:T(8,128)(2,1)} %copy-done.4), channel_id=1, source_target_pairs={{0,4},{4,0},{1,5},{5,1},{2,6},{6,2},{3,7},{7,3},{8,12},{12,8},{9,1... | collective-permute-start | bytes 1572872 | tf_op jit(solution)/shard_map/ppermute | solution.py:27
  86.6 15.4 %collective-permute-start.23 = (bf16[4,128,512]{2,1,0:T(8,128)(2,1)}, bf16[4,128,512]{2,1,0:T(8,128)(2,1)S(1)}, u32[]{:S(2)}, u32[]{:S(2)}) collective-permute-start(bf16[4,128,512]{2,1,0:T(8,128)(2,1)} %copy-done.7), channel_id=1, source_target_pairs={{0,4},{4,0},{1,5},{5,1},{2,6},{6,2},{3,7},{7,3},{8,12},{12,8},{9,1... | collective-permute-start | bytes 1572872 | tf_op jit(solution)/shard_map/ppermute | solution.py:27
  86.8 15.2 %collective-permute-start.25 = (bf16[2,128,512]{2,1,0:T(8,128)(2,1)S(1)}, bf16[2,128,512]{2,1,0:T(8,128)(2,1)S(1)}, u32[]{:S(2)}, u32[]{:S(2)}) collective-permute-start(bf16[2,128,512]{2,1,0:T(8,128)(2,1)S(1)} %collective-permute-done.24.refs_9_), channel_id=1, source_target_pairs={{0,4},{4,0},{1,5},{5,1},{2,6},{6,2},{3,7},{7,3},{8,12},{12,8},{9,1... | collective-permute-start | bytes 786440 | tf_op jit(solution)/shard_map/ppermute | solution.py:27
  87.1 1.3 %copy-start.2 = (bf16[512,1280]{1,0:T(8,128)(2,1)S(1)}, bf16[512,1280]{1,0:T(8,128)(2,1)}, u32[]{:S(2)}) copy-start(bf16[512,1280]{1,0:T(8,128)(2,1)} %copy-done.1) | copy-start | bytes 3932164
  88.4 1.0 copy-start.5
  98.1 3.9 %copy-start.3 = (bf16[512,1280]{1,0:T(8,128)(2,1)S(1)}, bf16[512,1280]{1,0:T(8,128)(2,1)}, u32[]{:S(2)}) copy-start(bf16[512,1280]{1,0:T(8,128)(2,1)} %copy-done.1) | copy-start | bytes 3932164
  98.1 3.9 %copy-start.8 = (bf16[4,128,512]{2,1,0:T(8,128)(2,1)S(1)}, bf16[4,128,512]{2,1,0:T(8,128)(2,1)}, u32[]{:S(2)}) copy-start(bf16[4,128,512]{2,1,0:T(8,128)(2,1)} %copy-done.7) | copy-start | bytes 1572868

commit v3 on v2

--- a/solution.py
+++ b/solution.py
@@ -10,6 +10,7 @@
 BLOCK = 128
 MASKED = -1e30
 ATTENTION_VMEM = 58 << 20
+STRIP = 256
 PROJECT_VMEM = 16 << 20
 Y_FIRST = 512
 LOG2E = 1.4426950408889634
@@ -48,77 +49,88 @@
     return jnp.dot(a, b, preferred_element_type=jnp.float32)
 
 
-def attention_kernel(q_ref, do_ref, k_ref, v_ref, lse_ref, delta_ref, seg_ref, out_ref,
-                     bias, key_t, lse_f, delta_f, dk_acc, dv_acc):
-    head = pl.program_id(0)
-    heads = pl.num_programs(0)
-    window, size = k_ref.shape
+def attention_kernel(q_hbm, do_hbm, k_hbm, v_hbm, lse_hbm, delta_hbm, seg_ref, out_ref,
+                     query_all, dout_all, k_ref, v_ref, lse_b, delta_b, bias, key_t, dk_acc, dv_acc, sems):
+    heads, window, size = query_all.shape
     scale = size ** -0.5
-
-    @pl.when(head == 0)
-    def _():
-        lse_f[...] = lse_ref[...].astype(jnp.float32) * LOG2E
-        delta_f[...] = delta_ref[...].astype(jnp.float32)
-        key_t[...] = k_ref[...].astype(jnp.float32).T.astype(jnp.bfloat16)
-        seg_row = seg_ref[...].astype(jnp.float32)
-        seg_col = jnp.broadcast_to(seg_row, (BLOCK, window)).T
-        row = lax.broadcasted_iota(jnp.int32, (window, BLOCK), 0)
-        col = lax.broadcasted_iota(jnp.int32, (window, BLOCK), 1)
-        for start in range(0, window, BLOCK):
-            same = seg_col == seg_row[:, start:start + BLOCK]
-            bias[:, start:start + BLOCK] = jnp.where(same & (row <= col + start), 0.0, MASKED)
-        dk_acc[...] = jnp.zeros_like(dk_acc)
-        dv_acc[...] = jnp.zeros_like(dv_acc)
-
-    lse = lse_f[pl.ds(head, 1), :]
-    delta = delta_f[pl.ds(head, 1), :]
-    parts = []
+    small = [pltpu.make_async_copy(source, target, sems.at[2 * heads + index]) for index, (source, target) in
+             enumerate(((k_hbm, k_ref), (v_hbm, v_ref), (lse_hbm, lse_b), (delta_hbm, delta_b)))]
+    for made in small:
+        made.start()
+    wide = []
+    for head in range(heads):
+        columns = slice(head * size, (head + 1) * size)
+        wide.append([
+            pltpu.make_async_copy(q_hbm.at[:, columns], query_all.at[head], sems.at[2 * head]),
+            pltpu.make_async_copy(do_hbm.at[:, columns], dout_all.at[head], sems.at[2 * head + 1])])
+        for made in wide[-1]:
+            made.start()
+    seg_row = seg_ref[...].astype(jnp.float32)
+    seg_col = jnp.broadcast_to(seg_row, (BLOCK, window)).T
+    row = lax.broadcasted_iota(jnp.int32, (window, BLOCK), 0)
+    col = lax.broadcasted_iota(jnp.int32, (window, BLOCK), 1)
     for start in range(0, window, BLOCK):
-        rows = slice(start, start + BLOCK)
-        query = q_ref[start:, :]
-        dout = do_ref[start:, :]
-        scores = nt(k_ref[rows, :], query)
-        probs = jnp.exp2(scores * (scale * LOG2E) - lse[:, start:] + bias[rows, start:])
-        grad_prob = nt(v_ref[rows, :], dout)
-        grad_score = (probs * (grad_prob - delta[:, start:])).astype(jnp.bfloat16)
-        dv_acc[rows, :] += nn(probs.astype(jnp.bfloat16), dout)
-        dk_acc[rows, :] += nn(grad_score, query)
-        parts.append(nn(key_t[:, rows], grad_score))
-    for start in range(0, window, BLOCK):
-        total = parts[0][:, start:start + BLOCK]
-        for index in range(1, start // BLOCK + 1):
-            first = start - index * BLOCK
-            total += parts[index][:, first:first + BLOCK]
-        out_ref[start:start + BLOCK, pl.ds(pl.multiple_of(head * size, size), size)] = (
-            (total * scale).T.astype(jnp.bfloat16)
-        )
-
-    @pl.when(head == heads - 1)
-    def _():
-        out_ref[:, heads * size:(heads + 1) * size] = (dk_acc[...] * scale).astype(jnp.bfloat16)
-        out_ref[:, (heads + 1) * size:] = dv_acc[...].astype(jnp.bfloat16)
+        same = seg_col == seg_row[:, start:start + BLOCK]
+        bias[:, start:start + BLOCK] = jnp.where(same & (row <= col + start), 0.0, MASKED)
+    for made in small:
+        made.wait()
+    lse_f = lse_b[...].astype(jnp.float32) * LOG2E
+    delta_f = delta_b[...].astype(jnp.float32)
+    key_t[...] = k_ref[...].astype(jnp.float32).T.astype(jnp.bfloat16)
+    for head in range(heads):
+        for made in wide[head]:
+            made.wait()
+        lse = lse_f[head:head + 1, :]
+        delta = delta_f[head:head + 1, :]
+        for start in range(0, window, STRIP):
+            rows = slice(start, start + STRIP)
+            query = query_all[head, start:, :]
+            dout = dout_all[head, start:, :]
+            scores = nt(k_ref[rows, :], query)
+            probs = jnp.exp2(scores * (scale * LOG2E) - lse[:, start:] + bias[rows, start:])
+            grad_prob = nt(v_ref[rows, :], dout)
+            grad_score = (probs * (grad_prob - delta[:, start:])).astype(jnp.bfloat16)
+            dv = nn(probs.astype(jnp.bfloat16), dout)
+            dk = nn(grad_score, query)
+            part = nn(key_t[:, rows], grad_score)
+            if head == 0:
+                dv_acc[rows, :] = dv
+                dk_acc[rows, :] = dk
+            else:
+                dv_acc[rows, :] += dv
+                dk_acc[rows, :] += dk
+            if start == 0:
+                total = part
+            else:
+                total = jnp.concatenate([total[:, :start], total[:, start:] + part], axis=1)
+        out_ref[:, head * size:(head + 1) * size] = (total * scale).T.astype(jnp.bfloat16)
+    out_ref[:, heads * size:(heads + 1) * size] = (dk_acc[...] * scale).astype(jnp.bfloat16)
+    out_ref[:, (heads + 1) * size:] = dv_acc[...].astype(jnp.bfloat16)
 
 
 def joined_gradients(query, dout, key, value, lse, delta, seg):
     window, width = query.shape
     size = key.shape[1]
     heads = width // size
-    whole = lambda shape: pl.BlockSpec(shape, lambda r: (0, 0))
-    per_head = pl.BlockSpec((window, size), lambda r: (0, r))
+    hbm = pl.BlockSpec(memory_space=pltpu.HBM)
+    vmem = pl.BlockSpec(memory_space=pltpu.VMEM)
     return pl.pallas_call(
         attention_kernel,
-        grid=(heads,),
-        in_specs=[per_head, per_head, whole((window, size)), whole((window, size)),
-                  whole((heads, window)), whole((heads, window)), whole((1, window))],
-        out_specs=whole((window, width + 2 * size)),
+        in_specs=[hbm] * 6 + [vmem],
+        out_specs=vmem,
         out_shape=jax.ShapeDtypeStruct((window, width + 2 * size), jnp.bfloat16),
         scratch_shapes=[
+            pltpu.VMEM((heads, window, size), jnp.bfloat16),
+            pltpu.VMEM((heads, window, size), jnp.bfloat16),
+            pltpu.VMEM((window, size), jnp.bfloat16),
+            pltpu.VMEM((window, size), jnp.bfloat16),
+            pltpu.VMEM((heads, window), jnp.bfloat16),
+            pltpu.VMEM((heads, window), jnp.bfloat16),
             pltpu.VMEM((window, window), jnp.float32),
             pltpu.VMEM((size, window), jnp.bfloat16),
-            pltpu.VMEM((heads, window), jnp.float32),
-            pltpu.VMEM((heads, window), jnp.float32),
             pltpu.VMEM((window, size), jnp.float32),
             pltpu.VMEM((window, size), jnp.float32),
+            pltpu.SemaphoreType.DMA((2 * heads + 4,)),
         ],
         compiler_params=pltpu.CompilerParams(vmem_limit_bytes=ATTENTION_VMEM),
         cost_estimate=pl.CostEstimate(flops=4 * 10 ** 9, bytes_accessed=4 * 10 ** 6, transcendentals=10 ** 6),
@@ -148,7 +160,8 @@
     for offset in plan.slots:
         slots.append([refs.pop(0), refs.pop(0)] if offset == "far" else [refs.pop(0)])
     rows = [refs.pop(0) for _ in plan.rows]
-    out_ref, joined, acc = refs
+    out_ref, joined = refs[:2]
+    acc = refs[2] if plan.last else out_ref
     width = heads[0].shape[1]
     split = Y_FIRST
 
@@ -162,9 +175,15 @@
         acc[...] = jnp.zeros_like(acc)
     else:
         acc[...] = acc_in[...]
-    if plan.rows:
-        for index, source in enumerate(heads):
-            joined[index] = source[:, split:]
+    for position, (source, head) in enumerate(zip(heads, plan.joined)):
+        if len(plan.rows) == 2:
+            g = (y + 4 + steps(plan.rows[0][2])) % 4
+
+            @pl.when((x + steps(head) + 4) % 4 == g)
+            def _(source=source):
+                joined[0] = source[:, split:]
+        else:
+            joined[position] = source[:, split:]
 
     def slot(sources, offset, g):
         if len(sources) == 2:
@@ -196,7 +215,7 @@
         index = jnp.int32(-1)
         for position, head in enumerate(plan.joined):
             if head in against:
-                index = jnp.where((x + steps(head) + 4) % 4 == g, position, index)
+                index = jnp.where((x + steps(head) + 4) % 4 == g, 0 if len(plan.rows) == 2 else position, index)
         offsets = slot_offsets(c if same else 1 - c, part)
 
         def body(source=source, index=index, offsets=offsets):
@@ -210,7 +229,8 @@
             body()
         else:
             pl.when(index >= 0)(body)
-    out_ref[...] = acc[...].astype(out_ref.dtype)
+    if plan.last:
+        out_ref[...] = acc[...].astype(out_ref.dtype)
 
 
 def projection(plan, name, where, *operands):
@@ -224,9 +244,8 @@
         out_specs=vmem,
         out_shape=jax.ShapeDtypeStruct((window, columns), jnp.bfloat16 if plan.last else jnp.float32),
         scratch_shapes=[
-            pltpu.VMEM((len(plan.joined) if plan.rows else 1, window, width - Y_FIRST), jnp.bfloat16),
-            pltpu.VMEM((window, columns), jnp.float32),
-        ],
+            pltpu.VMEM((1 if len(plan.rows) == 2 else len(plan.joined), window, width - Y_FIRST), jnp.bfloat16),
+        ] + [pltpu.VMEM((window, columns), jnp.float32)] * plan.last,
         compiler_params=pltpu.CompilerParams(vmem_limit_bytes=PROJECT_VMEM),
         cost_estimate=pl.CostEstimate(
             flops=int(1e9 * share), bytes_accessed=int(1e6 * share), transcendentals=0),
@@ -295,14 +314,15 @@
     lo_x, hi_x = swap_cores(lo_next), swap_cores(hi_next)
     j_far = along(j_first, "x", 1)
     a4 = along(lax.dynamic_slice_in_dim(a3, core, 2, 0), "z", 1)
-    far_x = swap_cores(lo_far)
-    ax3 = swap_cores(a3)
-    ax4 = swap_cores(a4)
 
     ring = (a_own, a1, ax1, a2)
     near_rows = (lo, hi, lo_next, hi_next, lo_x, hi_x)
     acc = projection(Plan(NEAR, (0, -1, 1, -2), rows_of(NEAR), True, False), "project_near", where,
                      joined, j_first, j_second, *ring, *near_rows)
+    acc, lo_far, a4 = in_order(acc, lo_far, a4)
+    far_x = swap_cores(lo_far)
+    ax3 = swap_cores(a3)
+    ax4 = swap_cores(a4)
     acc = projection(Plan((2,), (0, -1, 1, -2), rows_of((2,)), False, False), "project_far_head", where,
                      acc, j_far, *ring, *near_rows)
     far_rows = [("lo", True, "far", ALL), ("lo", False, "far", ALL)]

time: 108 us -> 102 us (0.944)
  the two profiles are of different devices: /device:TPU:1 before, /device:TPU:8 now
where the time goes in v3:
time: 102 us
  starting transfers between devices  38.6 us (38%)
  Pallas kernels  27.6 us (27%)
  waiting for transfers between devices  27.1 us (27%)
  local copies, waits for them, and re-layouts  7.45 us (7%)
    ppermute x28, starting transfers between devices, move(): return lax.ppermute(value, axes, pairs)  38.6 us
    ppermute x28, waiting for transfers between devices, move(): return lax.ppermute(value, axes, pairs)  27.1 us
    pallas_call x3, Pallas kernels, projection(): pl.pallas_call(lambda *refs: projection_kernel(plan, *refs), in_specs=[pl...  18 us
    pallas_call x1, Pallas kernels, joined_gradients(): pl.pallas_call(attention_kernel, in_specs=[hbm] * 6 + [vmem], out_specs=v...  9.59 us
    unnamed x18, local copies, waits for them, and re-layouts  5.02 us
  transfers between devices with their start and end apart: 28, of which 10 were waited for; matrix products, arithmetic and copies ran while one was open for 3% of the time, Pallas kernels for 21%

profile of v3, /device:TPU:8, one launch (start us, length us, event | category | flops | bytes accessed | tf_op | source)
XLA Modules:
  0.0 101.5 jit_solution(188203895146341949)
XLA Ops:
  0.0 3.3 %collective-permute-start = (bf16[64,1280]{1,0:T(8,128)(2,1)}, bf16[64,1280]{1,0:T(8,128)(2,1)S(1)}, u32[]{:S(2)}, u32[]{:S(2)}) collective-permute-start(bf16[64,1280]{1,0:T(8,128)(2,1)} %bitcast.34), channel_id=1, source_target_pairs={{0,0},{1,64},{2,128},{3,192},{64,1},{65,65},{66,129},{67,193},{128... | collective-permute-start | bytes 491528 | tf_op jit(solution)/shard_map/ppermute | solution.py:28
  3.3 1.3 %dynamic_slice.9 = s32[512]{0:T(512)} dynamic-slice(s32[32768]{0:T(1024)} %param.14, s32[]{:T(128)S(6)} %select_n.45), dynamic_slice_sizes={512} | dynamic-slice | bytes 4100 | tf_op jit(solution)/shard_map/dynamic_slice | solution.py:281
  4.6 9.6 %attention_backward.1.refs_1_.refs_2_ = bf16[512,1280]{1,0:T(8,128)(2,1)} custom-call(bf16[512,1024]{1,0:T(8,128)(2,1)} %bitcast.32, bf16[512,1024]{1,0:T(8,128)(2,1)} %bitcast.33, bf16[512,128]{1,0:T(8,128)(2,1)} %bitcast.35, bf16[512,128]{1,0:T(8,128)(2,1)} %bitcast.36, bf16[8,512]{1,0:T(8,128)(2,1)} %bitcast.37, bf16[8,512]{1,0:T(8,128)(2,1)} %bitcast.38, ...), custom_call_target="tpu_custom_call" | custom-call | flops 4000000000 | bytes 4000000 | tf_op jit(solution)/shard_map/attention_backward/pallas_call | solution.py:117
  14.4 1.4 %collective-permute-done.3 = bf16[64,1280]{1,0:T(8,128)(2,1)S(1)} collective-permute-done((bf16[64,1280]{1,0:T(8,128)(2,1)S(1)}, bf16[64,1280]{1,0:T(8,128)(2,1)S(1)}, u32[]{:S(2)}, u32[]{:S(2)}) %collective-permute-start.3) | collective-permute-done | bytes 163872 | tf_op jit(solution)/shard_map/ppermute | solution.py:28
  15.8 2.0 %collective-permute-start.12 = (bf16[128,768]{1,0:T(8,128)(2,1)S(1)}, bf16[128,768]{1,0:T(8,128)(2,1)S(1)}, u32[]{:S(2)}, u32[]{:S(2)}) collective-permute-start(bf16[128,768]{1,0:T(8,128)(2,1)S(1)} %pad_maximum_fusion.4), channel_id=1, source_target_pairs={{0,8},{4,60},{8,16},{12,4},{16,24},{20,12},{24,32},{28,20},{32,40}... | collective-permute-start | bytes 589832 | tf_op jit(solution)/shard_map/ppermute | solution.py:28
  17.8 3.0 %collective-permute-start.4 = (bf16[128,512]{1,0:T(8,128)(2,1)S(1)}, bf16[128,512]{1,0:T(8,128)(2,1)S(1)}, u32[]{:S(2)}, u32[]{:S(2)}) collective-permute-start(bf16[128,512]{1,0:T(8,128)(2,1)S(1)} %pad_maximum_fusion.6), channel_id=1, source_target_pairs={{0,64},{4,196},{64,128},{68,4},{128,192},{132,68},{192,0},{196,132... | collective-permute-start | bytes 393224 | tf_op jit(solution)/shard_map/ppermute | solution.py:28
  20.8 0.3 collective-permute-start.5
  21.2 2.6 %collective-permute-start.6 = (bf16[128,512]{1,0:T(8,128)(2,1)S(1)}, bf16[128,512]{1,0:T(8,128)(2,1)S(1)}, u32[]{:S(2)}, u32[]{:S(2)}) collective-permute-start(bf16[128,512]{1,0:T(8,128)(2,1)S(1)} %pad_maximum_fusion.6), channel_id=1, source_target_pairs={{0,192},{4,68},{64,0},{68,132},{128,64},{132,196},{192,128},{196,4... | collective-permute-start | bytes 393224 | tf_op jit(solution)/shard_map/ppermute | solution.py:28
  23.8 6.4 %collective-permute-start.10 = (bf16[64,768]{1,0:T(8,128)(2,1)S(1)}, bf16[64,768]{1,0:T(8,128)(2,1)S(1)}, u32[]{:S(2)}, u32[]{:S(2)}) collective-permute-start(bf16[64,768]{1,0:T(8,128)(2,1)S(1)} %constant_dynamic-slice_fusion.1), channel_id=1, source_target_pairs={{0,32},{4,36},{8,40},{12,44},{16,48},{20,52},{24,56},{28,60},{32,0... | collective-permute-start | bytes 294920 | tf_op jit(solution)/shard_map/ppermute | solution.py:28
  30.2 1.6 %collective-permute-start.13 = (bf16[2,128,768]{2,1,0:T(8,128)(2,1)S(1)}, bf16[2,128,768]{2,1,0:T(8,128)(2,1)S(1)}, u32[]{:S(2)}, u32[]{:S(2)}) collective-permute-start(bf16[2,128,768]{2,1,0:T(8,128)(2,1)S(1)} %pad_maximum_fusion.3), channel_id=1, source_target_pairs={{0,16},{4,52},{8,24},{12,60},{16,32},{20,4},{24,40},{28,12},{32,48... | collective-permute-start | bytes 1179656 | tf_op jit(solution)/shard_map/ppermute | solution.py:28
  31.8 1.3 %collective-permute-done.10 = bf16[64,768]{1,0:T(8,128)(2,1)S(1)} collective-permute-done((bf16[64,768]{1,0:T(8,128)(2,1)S(1)}, bf16[64,768]{1,0:T(8,128)(2,1)S(1)}, u32[]{:S(2)}, u32[]{:S(2)}) %collective-permute-start.10) | collective-permute-done | bytes 98336 | tf_op jit(solution)/shard_map/ppermute | solution.py:28
  33.0 1.9 %collective-permute-start.1 = (bf16[512,1280]{1,0:T(8,128)(2,1)S(1)}, bf16[512,1280]{1,0:T(8,128)(2,1)}, u32[]{:S(2)}, u32[]{:S(2)}) collective-permute-start(bf16[512,1280]{1,0:T(8,128)(2,1)S(1)} %copy-done), channel_id=1, source_target_pairs={{0,1},{1,2},{2,3},{3,0},{4,7},{5,4},{6,5},{7,6},{8,9},{9,10},{10,1... | collective-permute-start | bytes 3932168 | tf_op jit(solution)/shard_map/ppermute | solution.py:28
  34.9 1.4 %collective-permute-start.2 = (bf16[512,1280]{1,0:T(8,128)(2,1)S(1)}, bf16[512,1280]{1,0:T(8,128)(2,1)S(1)}, u32[]{:S(2)}, u32[]{:S(2)}) collective-permute-start(bf16[512,1280]{1,0:T(8,128)(2,1)S(1)} %copy-done), channel_id=1, source_target_pairs={{0,3},{1,0},{2,1},{3,2},{4,5},{5,6},{6,7},{7,4},{8,11},{9,8},{10,9... | collective-permute-start | bytes 3932168 | tf_op jit(solution)/shard_map/ppermute | solution.py:28
  36.3 0.7 collective-permute-start.11
  37.1 2.4 %collective-permute-start.7 = (bf16[4,128,512]{2,1,0:T(8,128)(2,1)S(1)}, bf16[4,128,512]{2,1,0:T(8,128)(2,1)}, u32[]{:S(2)}, u32[]{:S(2)}) collective-permute-start(bf16[4,128,512]{2,1,0:T(8,128)(2,1)S(1)} %pad_maximum_fusion.2.refs_4_.refs_3_), channel_id=1, source_target_pairs={{0,8},{4,60},{8,16},{12,4},{16,24},{20,12},{24,32},{28,20},{32,40}... | collective-permute-start | bytes 1572872 | tf_op jit(solution)/shard_map/ppermute | solution.py:28
  39.5 0.8 collective-permute-done.13
  40.3 3.3 %collective-permute-start.15 = (bf16[2,128,768]{2,1,0:T(8,128)(2,1)S(1)}, bf16[2,128,768]{2,1,0:T(8,128)(2,1)S(1)}, u32[]{:S(2)}, u32[]{:S(2)}) collective-permute-start(bf16[2,128,768]{2,1,0:T(8,128)(2,1)S(1)} %collective-permute-done.13), channel_id=1, source_target_pairs={{0,4},{4,0},{1,5},{5,1},{2,6},{6,2},{3,7},{7,3},{8,12},{12,8},{9,1... | collective-permute-start | bytes 1179656 | tf_op jit(solution)/shard_map/ppermute | solution.py:28
  43.6 0.1 collective-permute-start.14
  43.8 0.1 pad_maximum_fusion.refs_8_.refs_7_
  43.9 1.0 %collective-permute-done.15 = bf16[2,128,768]{2,1,0:T(8,128)(2,1)S(1)} collective-permute-done((bf16[2,128,768]{2,1,0:T(8,128)(2,1)S(1)}, bf16[2,128,768]{2,1,0:T(8,128)(2,1)S(1)}, u32[]{:S(2)}, u32[]{:S(2)}) %collective-permute-start.15) | collective-permute-done | bytes 393248 | tf_op jit(solution)/shard_map/ppermute | solution.py:28
  45.0 0.3 collective-permute-done.14
  45.2 0.1 pad_maximum_fusion.1.refs_9_.refs_8_
  45.3 0.3 collective-permute-start.16
  45.6 1.7 %collective-permute-start.17 = (bf16[4,128,768]{2,1,0:T(8,128)(2,1)S(1)}, bf16[4,128,768]{2,1,0:T(8,128)(2,1)}, u32[]{:S(2)}, u32[]{:S(2)}) collective-permute-start(bf16[4,128,768]{2,1,0:T(8,128)(2,1)S(1)} %pad_maximum_fusion.1.refs_9_.refs_8_), channel_id=1, source_target_pairs={{0,64},{4,196},{64,128},{68,4},{128,192},{132,68},{192,0},{196,132... | collective-permute-start | bytes 2359304 | tf_op jit(solution)/shard_map/ppermute | solution.py:28
  47.3 2.4 %collective-permute-done.7.refs_5_.refs_4_ = bf16[4,128,512]{2,1,0:T(8,128)(2,1)} collective-permute-done((bf16[4,128,512]{2,1,0:T(8,128)(2,1)S(1)}, bf16[4,128,512]{2,1,0:T(8,128)(2,1)}, u32[]{:S(2)}, u32[]{:S(2)}) %collective-permute-start.7) | collective-permute-done | bytes 524320 | tf_op jit(solution)/shard_map/ppermute | solution.py:28
  49.7 1.4 %collective-permute-start.9 = (bf16[4,128,512]{2,1,0:T(8,128)(2,1)}, bf16[4,128,512]{2,1,0:T(8,128)(2,1)S(1)}, u32[]{:S(2)}, u32[]{:S(2)}) collective-permute-start(bf16[4,128,512]{2,1,0:T(8,128)(2,1)} %collective-permute-done.7.refs_5_.refs_4_), channel_id=1, source_target_pairs={{0,8},{4,60},{8,16},{12,4},{16,24},{20,12},{24,32},{28,20},{32,40}... | collective-permute-start | bytes 1572872 | tf_op jit(solution)/shard_map/ppermute | solution.py:28
  51.1 9.2 %collective-permute-done.9.refs_7_.refs_6_ = bf16[4,128,512]{2,1,0:T(8,128)(2,1)S(1)} collective-permute-done((bf16[4,128,512]{2,1,0:T(8,128)(2,1)}, bf16[4,128,512]{2,1,0:T(8,128)(2,1)S(1)}, u32[]{:S(2)}, u32[]{:S(2)}) %collective-permute-start.9) | collective-permute-done | bytes 524320 | tf_op jit(solution)/shard_map/ppermute | solution.py:28
  60.3 0.2 collective-permute-start.21
  60.5 0.8 copy-done.4
  61.3 1.6 %collective-permute-start.18 = (bf16[4,128,768]{2,1,0:T(8,128)(2,1)}, bf16[4,128,768]{2,1,0:T(8,128)(2,1)}, u32[]{:S(2)}, u32[]{:S(2)}) collective-permute-start(bf16[4,128,768]{2,1,0:T(8,128)(2,1)} %collective-permute-done.16.refs_10_.refs_9_), channel_id=1, source_target_pairs={{0,4},{4,0},{1,5},{5,1},{2,6},{6,2},{3,7},{7,3},{8,12},{12,8},{9,1... | collective-permute-start | bytes 2359304 | tf_op jit(solution)/shard_map/ppermute | solution.py:28
  63.0 2.9 %collective-permute-done.17.refs_11_.refs_10_ = bf16[4,128,768]{2,1,0:T(8,128)(2,1)} collective-permute-done((bf16[4,128,768]{2,1,0:T(8,128)(2,1)S(1)}, bf16[4,128,768]{2,1,0:T(8,128)(2,1)}, u32[]{:S(2)}, u32[]{:S(2)}) %collective-permute-start.17) | collective-permute-done | bytes 786464 | tf_op jit(solution)/shard_map/ppermute | solution.py:28
  65.9 0.5 collective-permute-start.8
  66.4 1.1 %copy-done.1 = bf16[512,1280]{1,0:T(8,128)(2,1)} copy-done((bf16[512,1280]{1,0:T(8,128)(2,1)}, bf16[512,1280]{1,0:T(8,128)(2,1)S(1)}, u32[]{:S(2)}) %copy-start.1) | copy-done | bytes 1310744
  67.5 0.2 collective-permute-start.20
  67.7 3.0 %collective-permute-done.21.refs_7_ = bf16[4,128,512]{2,1,0:T(8,128)(2,1)S(1)} collective-permute-done((bf16[4,128,512]{2,1,0:T(8,128)(2,1)S(1)}, bf16[4,128,512]{2,1,0:T(8,128)(2,1)S(1)}, u32[]{:S(2)}, u32[]{:S(2)}) %collective-permute-start.21) | collective-permute-done | bytes 524320 | tf_op jit(solution)/shard_map/ppermute | solution.py:28
  70.7 0.8 copy-done.7
  71.5 1.9 %collective-permute-start.23 = (bf16[512,1280]{1,0:T(8,128)(2,1)}, bf16[512,1280]{1,0:T(8,128)(2,1)}, u32[]{:S(2)}, u32[]{:S(2)}) collective-permute-start(bf16[512,1280]{1,0:T(8,128)(2,1)} %collective-permute-done.1.refs_2_.refs_3_), channel_id=1, source_target_pairs={{0,1},{1,2},{2,3},{3,0},{4,7},{5,4},{6,5},{7,6},{8,9},{9,10},{10,1... | collective-permute-start | bytes 3932168 | tf_op jit(solution)/shard_map/ppermute | solution.py:28
  73.4 1.0 %constant_dynamic-slice_fusion = bf16[2,128,512]{2,1,0:T(8,128)(2,1)S(1)} fusion(bf16[4,128,512]{2,1,0:T(8,128)(2,1)} %copy-done.7, s32[]{:T(128)S(6)} %select_n.56), kind=kLoop, calls=%fused_computation.14 | loop fusion | bytes 524292 | tf_op jit(solution)/shard_map/dynamic_slice | solution.py:316
  74.5 1.3 %copy-done.2 = bf16[512,1280]{1,0:T(8,128)(2,1)S(1)} copy-done((bf16[512,1280]{1,0:T(8,128)(2,1)S(1)}, bf16[512,1280]{1,0:T(8,128)(2,1)}, u32[]{:S(2)}) %copy-start.2) | copy-done | bytes 1310744
  75.8 1.0 %copy-done.5 = bf16[4,128,512]{2,1,0:T(8,128)(2,1)S(1)} copy-done((bf16[4,128,512]{2,1,0:T(8,128)(2,1)S(1)}, bf16[4,128,512]{2,1,0:T(8,128)(2,1)}, u32[]{:S(2)}) %copy-start.5) | copy-done | bytes 524312
  76.9 7.2 %project_near.1.refs_1_ = f32[512,1024]{1,0:T(8,128)S(1)} custom-call(s32[4]{0:T(128)S(1)} %pad_add_fusion.refs_0_, bf16[512,1280]{1,0:T(8,128)(2,1)S(1)} %copy-done, bf16[512,1280]{1,0:T(8,128)(2,1)} %collective-permute-done.1.refs_2_.refs_3_, bf16[512,1280]{1,0:T(8,128)(2,1)S(1)} %copy-done.2, bf16[4,128,512]{2,1,0:T(8,128)(2,1)S(1)} %pad_maximum_fusion.2.refs_4_.refs_3_, ...), custom_call_target="tpu_custom_call" | custom-call | flops 450000000 | bytes 450000 | tf_op jit(solution)/shard_map/project_near/pallas_call | solution.py:241
  84.2 1.0 collective-permute-start.27
  85.1 0.1 collective-permute-start.24
  85.3 0.4 collective-permute-start.25
  85.7 0.1 collective-permute-start.26
  85.8 4.9 %collective-permute-done.23.refs_2_.refs_5_ = bf16[512,1280]{1,0:T(8,128)(2,1)} collective-permute-done((bf16[512,1280]{1,0:T(8,128)(2,1)}, bf16[512,1280]{1,0:T(8,128)(2,1)}, u32[]{:S(2)}, u32[]{:S(2)}) %collective-permute-start.23) | collective-permute-done | bytes 1310752 | tf_op jit(solution)/shard_map/ppermute | solution.py:28
  90.6 4.9 %project_far_head.1.refs_1_ = f32[512,1024]{1,0:T(8,128)S(1)} custom-call(s32[4]{0:T(128)S(1)} %pad_add_fusion.refs_0_, f32[512,1024]{1,0:T(8,128)S(1)} %project_near.1.refs_1_, bf16[512,1280]{1,0:T(8,128)(2,1)} %collective-permute-done.23.refs_2_.refs_5_, bf16[4,128,512]{2,1,0:T(8,128)(2,1)S(1)} %pad_maximum_fusion.2.refs_4_.refs_3_, ...), custom_call_target="tpu_custom_call" | custom-call | flops 250000000 | bytes 250000 | tf_op jit(solution)/shard_map/project_far_head/pallas_call | solution.py:241
  95.6 5.9 %project_rest.1 = bf16[512,1024]{1,0:T(8,128)(2,1)} custom-call(s32[4]{0:T(128)S(1)} %pad_add_fusion.refs_0_, f32[512,1024]{1,0:T(8,128)S(1)} %project_far_head.1.refs_1_, bf16[512,1280]{1,0:T(8,128)(2,1)S(1)} %copy-done, bf16[512,1280]{1,0:T(8,128)(2,1)} %collective-permute-done.1.refs_2_.refs_3_, bf16[512,1280]{1,0:T(8,128)(2,1)S(1)} %copy-done.3, ...), custom_call_target="tpu_custom_call" | custom-call | flops 450000000 | bytes 450000 | tf_op jit(solution)/shard_map/project_rest/pallas_call | solution.py:241
  (45 shorter events, 0.6 us)
Async XLA Ops:
  0.0 14.3 %collective-permute-start = (bf16[64,1280]{1,0:T(8,128)(2,1)}, bf16[64,1280]{1,0:T(8,128)(2,1)S(1)}, u32[]{:S(2)}, u32[]{:S(2)}) collective-permute-start(bf16[64,1280]{1,0:T(8,128)(2,1)} %bitcast.34), channel_id=1, source_target_pairs={{0,0},{1,64},{2,128},{3,192},{64,1},{65,65},{66,129},{67,193},{128... | collective-permute-start | bytes 491528 | tf_op jit(solution)/shard_map/ppermute | solution.py:28
  14.3 1.4 %collective-permute-start.3 = (bf16[64,1280]{1,0:T(8,128)(2,1)S(1)}, bf16[64,1280]{1,0:T(8,128)(2,1)S(1)}, u32[]{:S(2)}, u32[]{:S(2)}) collective-permute-start(bf16[64,1280]{1,0:T(8,128)(2,1)S(1)} %collective-permute-done), channel_id=1, source_target_pairs={{0,4},{4,0},{1,5},{5,1},{2,6},{6,2},{3,7},{7,3},{8,12},{12,8},{9,1... | collective-permute-start | bytes 491528 | tf_op jit(solution)/shard_map/ppermute | solution.py:28
  14.4 18.6 %copy-start = (bf16[512,1280]{1,0:T(8,128)(2,1)S(1)}, bf16[512,1280]{1,0:T(8,128)(2,1)}, u32[]{:S(2)}) copy-start(bf16[512,1280]{1,0:T(8,128)(2,1)} %attention_backward.1.refs_1_.refs_2_) | copy-start | bytes 3932164
  15.8 14.3 %collective-permute-start.12 = (bf16[128,768]{1,0:T(8,128)(2,1)S(1)}, bf16[128,768]{1,0:T(8,128)(2,1)S(1)}, u32[]{:S(2)}, u32[]{:S(2)}) collective-permute-start(bf16[128,768]{1,0:T(8,128)(2,1)S(1)} %pad_maximum_fusion.4), channel_id=1, source_target_pairs={{0,8},{4,60},{8,16},{12,4},{16,24},{20,12},{24,32},{28,20},{32,40}... | collective-permute-start | bytes 589832 | tf_op jit(solution)/shard_map/ppermute | solution.py:28
  17.8 17.1 %collective-permute-start.4 = (bf16[128,512]{1,0:T(8,128)(2,1)S(1)}, bf16[128,512]{1,0:T(8,128)(2,1)S(1)}, u32[]{:S(2)}, u32[]{:S(2)}) collective-permute-start(bf16[128,512]{1,0:T(8,128)(2,1)S(1)} %pad_maximum_fusion.6), channel_id=1, source_target_pairs={{0,64},{4,196},{64,128},{68,4},{128,192},{132,68},{192,0},{196,132... | collective-permute-start | bytes 393224 | tf_op jit(solution)/shard_map/ppermute | solution.py:28
  20.8 15.4 %collective-permute-start.5 = (bf16[128,512]{1,0:T(8,128)(2,1)S(1)}, bf16[128,512]{1,0:T(8,128)(2,1)S(1)}, u32[]{:S(2)}, u32[]{:S(2)}) collective-permute-start(bf16[128,512]{1,0:T(8,128)(2,1)S(1)} %pad_maximum_fusion.6), channel_id=1, source_target_pairs={{0,128},{4,132},{64,192},{68,196},{128,0},{132,4},{192,64},{196,68... | collective-permute-start | bytes 393224 | tf_op jit(solution)/shard_map/ppermute | solution.py:28
  21.2 15.8 %collective-permute-start.6 = (bf16[128,512]{1,0:T(8,128)(2,1)S(1)}, bf16[128,512]{1,0:T(8,128)(2,1)S(1)}, u32[]{:S(2)}, u32[]{:S(2)}) collective-permute-start(bf16[128,512]{1,0:T(8,128)(2,1)S(1)} %pad_maximum_fusion.6), channel_id=1, source_target_pairs={{0,192},{4,68},{64,0},{68,132},{128,64},{132,196},{192,128},{196,4... | collective-permute-start | bytes 393224 | tf_op jit(solution)/shard_map/ppermute | solution.py:28
  23.8 9.2 %collective-permute-start.10 = (bf16[64,768]{1,0:T(8,128)(2,1)S(1)}, bf16[64,768]{1,0:T(8,128)(2,1)S(1)}, u32[]{:S(2)}, u32[]{:S(2)}) collective-permute-start(bf16[64,768]{1,0:T(8,128)(2,1)S(1)} %constant_dynamic-slice_fusion.1), channel_id=1, source_target_pairs={{0,32},{4,36},{8,40},{12,44},{16,48},{20,52},{24,56},{28,60},{32,0... | collective-permute-start | bytes 294920 | tf_op jit(solution)/shard_map/ppermute | solution.py:28
  30.2 10.1 %collective-permute-start.13 = (bf16[2,128,768]{2,1,0:T(8,128)(2,1)S(1)}, bf16[2,128,768]{2,1,0:T(8,128)(2,1)S(1)}, u32[]{:S(2)}, u32[]{:S(2)}) collective-permute-start(bf16[2,128,768]{2,1,0:T(8,128)(2,1)S(1)} %pad_maximum_fusion.3), channel_id=1, source_target_pairs={{0,16},{4,52},{8,24},{12,60},{16,32},{20,4},{24,40},{28,12},{32,48... | collective-permute-start | bytes 1179656 | tf_op jit(solution)/shard_map/ppermute | solution.py:28
  33.0 32.9 %collective-permute-start.1 = (bf16[512,1280]{1,0:T(8,128)(2,1)S(1)}, bf16[512,1280]{1,0:T(8,128)(2,1)}, u32[]{:S(2)}, u32[]{:S(2)}) collective-permute-start(bf16[512,1280]{1,0:T(8,128)(2,1)S(1)} %copy-done), channel_id=1, source_target_pairs={{0,1},{1,2},{2,3},{3,0},{4,7},{5,4},{6,5},{7,6},{8,9},{9,10},{10,1... | collective-permute-start | bytes 3932168 | tf_op jit(solution)/shard_map/ppermute | solution.py:28
  34.9 31.5 %collective-permute-start.2 = (bf16[512,1280]{1,0:T(8,128)(2,1)S(1)}, bf16[512,1280]{1,0:T(8,128)(2,1)S(1)}, u32[]{:S(2)}, u32[]{:S(2)}) collective-permute-start(bf16[512,1280]{1,0:T(8,128)(2,1)S(1)} %copy-done), channel_id=1, source_target_pairs={{0,3},{1,0},{2,1},{3,2},{4,5},{5,6},{6,7},{7,4},{8,11},{9,8},{10,9... | collective-permute-start | bytes 3932168 | tf_op jit(solution)/shard_map/ppermute | solution.py:28
  36.3 3.2 %collective-permute-start.11 = (bf16[64,768]{1,0:T(8,128)(2,1)S(1)}, bf16[64,768]{1,0:T(8,128)(2,1)S(1)}, u32[]{:S(2)}, u32[]{:S(2)}) collective-permute-start(bf16[64,768]{1,0:T(8,128)(2,1)S(1)} %collective-permute-done.10), channel_id=1, source_target_pairs={{0,4},{4,0},{1,5},{5,1},{2,6},{6,2},{3,7},{7,3},{8,12},{12,8},{9,1... | collective-permute-start | bytes 294920 | tf_op jit(solution)/shard_map/ppermute | solution.py:28
  37.1 12.7 %collective-permute-start.7 = (bf16[4,128,512]{2,1,0:T(8,128)(2,1)S(1)}, bf16[4,128,512]{2,1,0:T(8,128)(2,1)}, u32[]{:S(2)}, u32[]{:S(2)}) collective-permute-start(bf16[4,128,512]{2,1,0:T(8,128)(2,1)S(1)} %pad_maximum_fusion.2.refs_4_.refs_3_), channel_id=1, source_target_pairs={{0,8},{4,60},{8,16},{12,4},{16,24},{20,12},{24,32},{28,20},{32,40}... | collective-permute-start | bytes 1572872 | tf_op jit(solution)/shard_map/ppermute | solution.py:28
  40.3 4.6 %collective-permute-start.15 = (bf16[2,128,768]{2,1,0:T(8,128)(2,1)S(1)}, bf16[2,128,768]{2,1,0:T(8,128)(2,1)S(1)}, u32[]{:S(2)}, u32[]{:S(2)}) collective-permute-start(bf16[2,128,768]{2,1,0:T(8,128)(2,1)S(1)} %collective-permute-done.13), channel_id=1, source_target_pairs={{0,4},{4,0},{1,5},{5,1},{2,6},{6,2},{3,7},{7,3},{8,12},{12,8},{9,1... | collective-permute-start | bytes 1179656 | tf_op jit(solution)/shard_map/ppermute | solution.py:28
  43.6 1.6 %collective-permute-start.14 = (bf16[128,768]{1,0:T(8,128)(2,1)S(1)}, bf16[128,768]{1,0:T(8,128)(2,1)S(1)}, u32[]{:S(2)}, u32[]{:S(2)}) collective-permute-start(bf16[128,768]{1,0:T(8,128)(2,1)S(1)} %collective-permute-done.12), channel_id=1, source_target_pairs={{0,4},{4,0},{1,5},{5,1},{2,6},{6,2},{3,7},{7,3},{8,12},{12,8},{9,1... | collective-permute-start | bytes 589832 | tf_op jit(solution)/shard_map/ppermute | solution.py:28
  45.3 16.0 %collective-permute-start.16 = (bf16[4,128,768]{2,1,0:T(8,128)(2,1)S(1)}, bf16[4,128,768]{2,1,0:T(8,128)(2,1)}, u32[]{:S(2)}, u32[]{:S(2)}) collective-permute-start(bf16[4,128,768]{2,1,0:T(8,128)(2,1)S(1)} %pad_maximum_fusion.refs_8_.refs_7_), channel_id=1, source_target_pairs={{0,64},{4,196},{64,128},{68,4},{128,192},{132,68},{192,0},{196,132... | collective-permute-start | bytes 2359304 | tf_op jit(solution)/shard_map/ppermute | solution.py:28
  45.6 20.3 %collective-permute-start.17 = (bf16[4,128,768]{2,1,0:T(8,128)(2,1)S(1)}, bf16[4,128,768]{2,1,0:T(8,128)(2,1)}, u32[]{:S(2)}, u32[]{:S(2)}) collective-permute-start(bf16[4,128,768]{2,1,0:T(8,128)(2,1)S(1)} %pad_maximum_fusion.1.refs_9_.refs_8_), channel_id=1, source_target_pairs={{0,64},{4,196},{64,128},{68,4},{128,192},{132,68},{192,0},{196,132... | collective-permute-start | bytes 2359304 | tf_op jit(solution)/shard_map/ppermute | solution.py:28
  49.7 10.6 %collective-permute-start.9 = (bf16[4,128,512]{2,1,0:T(8,128)(2,1)}, bf16[4,128,512]{2,1,0:T(8,128)(2,1)S(1)}, u32[]{:S(2)}, u32[]{:S(2)}) collective-permute-start(bf16[4,128,512]{2,1,0:T(8,128)(2,1)} %collective-permute-done.7.refs_5_.refs_4_), channel_id=1, source_target_pairs={{0,8},{4,60},{8,16},{12,4},{16,24},{20,12},{24,32},{28,20},{32,40}... | collective-permute-start | bytes 1572872 | tf_op jit(solution)/shard_map/ppermute | solution.py:28
  60.3 10.4 %collective-permute-start.21 = (bf16[4,128,512]{2,1,0:T(8,128)(2,1)S(1)}, bf16[4,128,512]{2,1,0:T(8,128)(2,1)S(1)}, u32[]{:S(2)}, u32[]{:S(2)}) collective-permute-start(bf16[4,128,512]{2,1,0:T(8,128)(2,1)S(1)} %collective-permute-done.9.refs_7_.refs_6_), channel_id=1, source_target_pairs={{0,8},{4,60},{8,16},{12,4},{16,24},{20,12},{24,32},{28,20},{32,40}... | collective-permute-start | bytes 1572872 | tf_op jit(solution)/shard_map/ppermute | solution.py:28
  60.5 0.8 copy-start.4
  61.3 13.2 %collective-permute-start.18 = (bf16[4,128,768]{2,1,0:T(8,128)(2,1)}, bf16[4,128,768]{2,1,0:T(8,128)(2,1)}, u32[]{:S(2)}, u32[]{:S(2)}) collective-permute-start(bf16[4,128,768]{2,1,0:T(8,128)(2,1)} %collective-permute-done.16.refs_10_.refs_9_), channel_id=1, source_target_pairs={{0,4},{4,0},{1,5},{5,1},{2,6},{6,2},{3,7},{7,3},{8,12},{12,8},{9,1... | collective-permute-start | bytes 2359304 | tf_op jit(solution)/shard_map/ppermute | solution.py:28
  65.9 8.6 %collective-permute-start.19 = (bf16[4,128,768]{2,1,0:T(8,128)(2,1)}, bf16[4,128,768]{2,1,0:T(8,128)(2,1)}, u32[]{:S(2)}, u32[]{:S(2)}) collective-permute-start(bf16[4,128,768]{2,1,0:T(8,128)(2,1)} %collective-permute-done.17.refs_11_.refs_10_), channel_id=1, source_target_pairs={{0,4},{4,0},{1,5},{5,1},{2,6},{6,2},{3,7},{7,3},{8,12},{12,8},{9,1... | collective-permute-start | bytes 2359304 | tf_op jit(solution)/shard_map/ppermute | solution.py:28
  65.9 8.5 %collective-permute-start.8 = (bf16[4,128,512]{2,1,0:T(8,128)(2,1)}, bf16[4,128,512]{2,1,0:T(8,128)(2,1)}, u32[]{:S(2)}, u32[]{:S(2)}) collective-permute-start(bf16[4,128,512]{2,1,0:T(8,128)(2,1)} %collective-permute-done.7.refs_5_.refs_4_), channel_id=1, source_target_pairs={{0,4},{4,0},{1,5},{5,1},{2,6},{6,2},{3,7},{7,3},{8,12},{12,8},{9,1... | collective-permute-start | bytes 1572872 | tf_op jit(solution)/shard_map/ppermute | solution.py:28
  66.4 1.1 %copy-start.1 = (bf16[512,1280]{1,0:T(8,128)(2,1)}, bf16[512,1280]{1,0:T(8,128)(2,1)S(1)}, u32[]{:S(2)}) copy-start(bf16[512,1280]{1,0:T(8,128)(2,1)S(1)} %collective-permute-done.2.refs_3_.refs_4_) | copy-start | bytes 3932164
  67.5 16.6 %collective-permute-start.20 = (bf16[4,128,768]{2,1,0:T(8,128)(2,1)}, bf16[4,128,768]{2,1,0:T(8,128)(2,1)}, u32[]{:S(2)}, u32[]{:S(2)}) collective-permute-start(bf16[4,128,768]{2,1,0:T(8,128)(2,1)} %collective-permute-done.16.refs_10_.refs_9_), channel_id=1, source_target_pairs={{0,64},{4,196},{64,128},{68,4},{128,192},{132,68},{192,0},{196,132... | collective-permute-start | bytes 2359304 | tf_op jit(solution)/shard_map/ppermute | solution.py:28
  70.7 0.8 copy-start.7
  71.5 19.1 %collective-permute-start.23 = (bf16[512,1280]{1,0:T(8,128)(2,1)}, bf16[512,1280]{1,0:T(8,128)(2,1)}, u32[]{:S(2)}, u32[]{:S(2)}) collective-permute-start(bf16[512,1280]{1,0:T(8,128)(2,1)} %collective-permute-done.1.refs_2_.refs_3_), channel_id=1, source_target_pairs={{0,1},{1,2},{2,3},{3,0},{4,7},{5,4},{6,5},{7,6},{8,9},{9,10},{10,1... | collective-permute-start | bytes 3932168 | tf_op jit(solution)/shard_map/ppermute | solution.py:28
  73.4 11.8 %copy-start.6 = (bf16[4,128,512]{2,1,0:T(8,128)(2,1)S(1)}, bf16[4,128,512]{2,1,0:T(8,128)(2,1)}, u32[]{:S(2)}) copy-start(bf16[4,128,512]{2,1,0:T(8,128)(2,1)} %copy-done.4) | copy-start | bytes 1572868
  74.4 9.7 %collective-permute-start.22 = (bf16[2,128,512]{2,1,0:T(8,128)(2,1)S(1)}, bf16[2,128,512]{2,1,0:T(8,128)(2,1)S(1)}, u32[]{:S(2)}, u32[]{:S(2)}) collective-permute-start(bf16[2,128,512]{2,1,0:T(8,128)(2,1)S(1)} %constant_dynamic-slice_fusion), channel_id=1, source_target_pairs={{0,8},{4,60},{8,16},{12,4},{16,24},{20,12},{24,32},{28,20},{32,40}... | collective-permute-start | bytes 786440 | tf_op jit(solution)/shard_map/ppermute | solution.py:28
  74.5 1.3 %copy-start.2 = (bf16[512,1280]{1,0:T(8,128)(2,1)S(1)}, bf16[512,1280]{1,0:T(8,128)(2,1)}, u32[]{:S(2)}) copy-start(bf16[512,1280]{1,0:T(8,128)(2,1)} %copy-done.1) | copy-start | bytes 3932164
  75.8 1.0 %copy-start.5 = (bf16[4,128,512]{2,1,0:T(8,128)(2,1)S(1)}, bf16[4,128,512]{2,1,0:T(8,128)(2,1)}, u32[]{:S(2)}) copy-start(bf16[4,128,512]{2,1,0:T(8,128)(2,1)} %copy-done.4) | copy-start | bytes 1572868
  76.9 8.4 %copy-start.8 = (bf16[4,128,512]{2,1,0:T(8,128)(2,1)S(1)}, bf16[4,128,512]{2,1,0:T(8,128)(2,1)}, u32[]{:S(2)}) copy-start(bf16[4,128,512]{2,1,0:T(8,128)(2,1)} %copy-done.7) | copy-start | bytes 1572868
  84.1 11.5 %copy-start.3 = (bf16[512,1280]{1,0:T(8,128)(2,1)S(1)}, bf16[512,1280]{1,0:T(8,128)(2,1)}, u32[]{:S(2)}) copy-start(bf16[512,1280]{1,0:T(8,128)(2,1)} %copy-done.1) | copy-start | bytes 3932164
  84.2 11.5 %collective-permute-start.27 = (bf16[4,128,768]{2,1,0:T(8,128)(2,1)}, bf16[4,128,768]{2,1,0:T(8,128)(2,1)S(1)}, u32[]{:S(2)}, u32[]{:S(2)}) collective-permute-start(bf16[4,128,768]{2,1,0:T(8,128)(2,1)} %collective-permute-done.20.refs_11_), channel_id=1, source_target_pairs={{0,4},{4,0},{1,5},{5,1},{2,6},{6,2},{3,7},{7,3},{8,12},{12,8},{9,1... | collective-permute-start | bytes 2359304 | tf_op jit(solution)/shard_map/ppermute | solution.py:28
  85.1 10.4 %collective-permute-start.24 = (bf16[4,128,512]{2,1,0:T(8,128)(2,1)S(1)}, bf16[4,128,512]{2,1,0:T(8,128)(2,1)S(1)}, u32[]{:S(2)}, u32[]{:S(2)}) collective-permute-start(bf16[4,128,512]{2,1,0:T(8,128)(2,1)S(1)} %copy-done.6), channel_id=1, source_target_pairs={{0,4},{4,0},{1,5},{5,1},{2,6},{6,2},{3,7},{7,3},{8,12},{12,8},{9,1... | collective-permute-start | bytes 1572872 | tf_op jit(solution)/shard_map/ppermute | solution.py:28
  85.3 10.3 %collective-permute-start.25 = (bf16[4,128,512]{2,1,0:T(8,128)(2,1)S(1)}, bf16[4,128,512]{2,1,0:T(8,128)(2,1)S(1)}, u32[]{:S(2)}, u32[]{:S(2)}) collective-permute-start(bf16[4,128,512]{2,1,0:T(8,128)(2,1)S(1)} %copy-done.8), channel_id=1, source_target_pairs={{0,4},{4,0},{1,5},{5,1},{2,6},{6,2},{3,7},{7,3},{8,12},{12,8},{9,1... | collective-permute-start | bytes 1572872 | tf_op jit(solution)/shard_map/ppermute | solution.py:28
  85.7 9.9 %collective-permute-start.26 = (bf16[2,128,512]{2,1,0:T(8,128)(2,1)S(1)}, bf16[2,128,512]{2,1,0:T(8,128)(2,1)S(1)}, u32[]{:S(2)}, u32[]{:S(2)}) collective-permute-start(bf16[2,128,512]{2,1,0:T(8,128)(2,1)S(1)} %collective-permute-done.22.refs_9_), channel_id=1, source_target_pairs={{0,4},{4,0},{1,5},{5,1},{2,6},{6,2},{3,7},{7,3},{8,12},{12,8},{9,1... | collective-permute-start | bytes 786440 | tf_op jit(solution)/shard_map/ppermute | solution.py:28

commit v4 on v3

--- a/solution.py
+++ b/solution.py
@@ -11,7 +11,7 @@
 MASKED = -1e30
 ATTENTION_VMEM = 58 << 20
 STRIP = 256
-PROJECT_VMEM = 16 << 20
+PROJECT_VMEM = 28 << 20
 Y_FIRST = 512
 LOG2E = 1.4426950408889634
 
@@ -160,92 +160,142 @@
     for offset in plan.slots:
         slots.append([refs.pop(0), refs.pop(0)] if offset == "far" else [refs.pop(0)])
     rows = [refs.pop(0) for _ in plan.rows]
-    out_ref, joined = refs[:2]
-    acc = refs[2] if plan.last else out_ref
-    width = heads[0].shape[1]
+    out_ref, ja, jb, wa, far, wb, sems = refs[:7]
+    acc = refs[7] if plan.last else out_ref
     split = Y_FIRST
+    single = len(plan.joined) == 1
+    one_row_head = len(plan.rows) == 2
 
     def steps(offset):
         return 2 if offset in (2, "far") else sign * offset
 
     def tile(offset):
-        return pl.ds(pl.multiple_of(((z + 8 + offset) % 8) * BLOCK, BLOCK), BLOCK)
+        return (z + 8 + offset) % 8
+
+    def head_index(head):
+        return (x + steps(head) + 4) % 4
+
+    used = [0]
+
+    def copy(source, target):
+        made = pltpu.make_async_copy(source, target, sems.at[used[0]])
+        used[0] += 1
+        return made
+
+    def entry(offset, g):
+        return ((y - g) * (sign if offset <= 0 else -sign) + 4) % 4
+
+    ahead = [copy(source.at[:, :split], ja.at[index]) for index, source in enumerate(heads)]
+    for index, (sources, offset) in enumerate(zip(slots, plan.slots)):
+        if offset == "far":
+            ahead += [copy(source, far.at[which]) for which, source in enumerate(sources)]
+        elif single:
+            ahead.append(copy(sources[0].at[entry(offset, head_index(plan.joined[0]))], wa.at[index, 0]))
+        else:
+            ahead.append(copy(sources[0], wa.at[index]))
+    for made in ahead:
+        made.start()
+
+    meets = []
+    for part, same, offset, against in plan.rows:
+        g = (y + 4 + steps(offset)) % 4
+        index = jnp.int32(-1)
+        for position, head in enumerate(plan.joined):
+            if head in against:
+                index = jnp.where(head_index(head) == g, position, index)
+        meets.append((g, index, len(against) == 4))
+
+    def guarded(sure, index, body):
+        body() if sure else pl.when(index >= 0)(body)
+
+    row_heads = []
+    if one_row_head:
+        for position, source in enumerate(heads):
+            made = pltpu.make_async_copy(source.at[:, split:], jb.at[0], sems.at[used[0]])
+            pl.when(meets[0][1] == position)(made.start)
+            row_heads.append(made)
+        used[0] += 1
+    else:
+        row_heads = [copy(source.at[:, split:], jb.at[position]) for position, source in enumerate(heads)]
+        for made in row_heads:
+            made.start()
+    row_copies = []
+    for index, (source, (g, meet, sure)) in enumerate(zip(rows, meets)):
+        made = copy(source, wb.at[index])
+        guarded(sure, meet, made.start)
+        row_copies.append(made)
 
     if plan.first:
         acc[...] = jnp.zeros_like(acc)
     else:
         acc[...] = acc_in[...]
-    for position, (source, head) in enumerate(zip(heads, plan.joined)):
-        if len(plan.rows) == 2:
-            g = (y + 4 + steps(plan.rows[0][2])) % 4
-
-            @pl.when((x + steps(head) + 4) % 4 == g)
-            def _(source=source):
-                joined[0] = source[:, split:]
-        else:
-            joined[position] = source[:, split:]
-
-    def slot(sources, offset, g):
-        if len(sources) == 2:
+
+    for made in ahead:
+        made.wait()
+
+    def slot(index, offset, g):
+        if offset == "far":
             k = (y - g + 4) % 4
-            mine, theirs = sources
             from_zero = k < 2
-            index_zero = jnp.where(from_zero, k, 0)
-            index_one = jnp.where(from_zero, 0, (4 - k) % 4 - 1)
-            index = jnp.where(from_zero, index_zero, index_one)
-            holder = jnp.where(from_zero, 0, 1)
-            return jnp.where(holder == c, mine[index], theirs[index])
-        made_here = offset <= 0
-        direction = sign if made_here else -sign
-        return sources[0][((y - g) * direction + 4) % 4]
+            place = jnp.where(from_zero, k, (4 - k) % 4 - 1)
+            return far[jnp.where(jnp.where(from_zero, 0, 1) == c, 0, 1), jnp.maximum(place, 0)]
+        return wa[index, 0 if single else entry(offset, g)]
 
     for pair in range(0, len(slots), 2):
         total = None
-        for source, head in zip(heads, plan.joined):
-            g = (x + steps(head) + 4) % 4
-            block = jnp.concatenate([slot(slots[pair + k], plan.slots[pair + k], g) for k in range(2)], axis=0)
-            term = nt(source[:, :split], block)
+        for position, head in enumerate(plan.joined):
+            g = head_index(head)
+            block = jnp.concatenate([slot(pair + k, plan.slots[pair + k], g) for k in range(2)], axis=0)
+            term = nt(ja[position], block)
             total = term if total is None else total + term
         for k in range(2):
             offset = plan.slots[pair + k]
-            acc[:, tile(4 if offset == "far" else sign * offset)] += total[:, k * BLOCK:(k + 1) * BLOCK]
-
-    for source, (part, same, offset, against) in zip(rows, plan.rows):
-        g = (y + 4 + steps(offset)) % 4
-        index = jnp.int32(-1)
-        for position, head in enumerate(plan.joined):
-            if head in against:
-                index = jnp.where((x + steps(head) + 4) % 4 == g, 0 if len(plan.rows) == 2 else position, index)
+            acc[tile(4 if offset == "far" else sign * offset)] += total[:, k * BLOCK:(k + 1) * BLOCK]
+
+    if one_row_head:
+        row_heads[0].wait()
+    else:
+        for made in row_heads:
+            made.wait()
+    for index, ((part, same, offset, against), (g, meet, sure)) in enumerate(zip(plan.rows, meets)):
         offsets = slot_offsets(c if same else 1 - c, part)
 
-        def body(source=source, index=index, offsets=offsets):
+        def body(index=index, meet=meet, offsets=offsets):
+            row_copies[index].wait()
+            left = jb[0] if one_row_head or single else jb[meet]
             for pair in (0, 2):
-                block = source[pair:pair + 2].reshape(2 * BLOCK, width - split)
-                term = nt(joined[index], block)
+                term = nt(left, wb[index, pair:pair + 2].reshape(2 * BLOCK, wb.shape[3]))
                 for k in range(2):
-                    acc[:, tile(offsets[pair + k])] += term[:, k * BLOCK:(k + 1) * BLOCK]
-
-        if len(against) == 4:
-            body()
-        else:
-            pl.when(index >= 0)(body)
+                    acc[tile(offsets[pair + k])] += term[:, k * BLOCK:(k + 1) * BLOCK]
+
+        guarded(sure, meet, body)
     if plan.last:
-        out_ref[...] = acc[...].astype(out_ref.dtype)
+        for place in range(8):
+            out_ref[:, place * BLOCK:(place + 1) * BLOCK] = acc[place].astype(out_ref.dtype)
 
 
 def projection(plan, name, where, *operands):
     window, width = operands[0 if plan.first else 1].shape
     columns = 8 * BLOCK
     vmem = pl.BlockSpec(memory_space=pltpu.VMEM)
-    share = (len(plan.joined) * len(plan.slots) + len(plan.rows)) / 40
+    kept = 0 if plan.first else 1
+    heads, slots, rows = len(plan.joined), len(plan.slots), len(plan.rows)
+    share = (heads * slots + rows) / 40
     return pl.pallas_call(
         lambda *refs: projection_kernel(plan, *refs),
-        in_specs=[pl.BlockSpec(memory_space=pltpu.SMEM)] + [vmem] * len(operands),
+        in_specs=[pl.BlockSpec(memory_space=pltpu.SMEM)] + [vmem] * kept
+        + [pl.BlockSpec(memory_space=pl.ANY)] * (len(operands) - kept),
         out_specs=vmem,
-        out_shape=jax.ShapeDtypeStruct((window, columns), jnp.bfloat16 if plan.last else jnp.float32),
+        out_shape=jax.ShapeDtypeStruct((window, columns), jnp.bfloat16) if plan.last
+        else jax.ShapeDtypeStruct((8, window, BLOCK), jnp.float32),
         scratch_shapes=[
-            pltpu.VMEM((1 if len(plan.rows) == 2 else len(plan.joined), window, width - Y_FIRST), jnp.bfloat16),
-        ] + [pltpu.VMEM((window, columns), jnp.float32)] * plan.last,
+            pltpu.VMEM((heads, window, Y_FIRST), jnp.bfloat16),
+            pltpu.VMEM((1 if rows == 2 else heads, window, width - Y_FIRST), jnp.bfloat16),
+            pltpu.VMEM((slots, 1 if heads == 1 else 4, BLOCK, Y_FIRST), jnp.bfloat16),
+            pltpu.VMEM((2, 2, BLOCK, Y_FIRST), jnp.bfloat16),
+            pltpu.VMEM((rows, 4, BLOCK, width - Y_FIRST), jnp.bfloat16),
+            pltpu.SemaphoreType.DMA((24,)),
+        ] + [pltpu.VMEM((8, window, BLOCK), jnp.float32)] * plan.last,
         compiler_params=pltpu.CompilerParams(vmem_limit_bytes=PROJECT_VMEM),
         cost_estimate=pl.CostEstimate(
             flops=int(1e9 * share), bytes_accessed=int(1e6 * share), transcendentals=0),
@@ -313,7 +363,7 @@
     ax2 = swap_cores(a2)
     lo_x, hi_x = swap_cores(lo_next), swap_cores(hi_next)
     j_far = along(j_first, "x", 1)
-    a4 = along(lax.dynamic_slice_in_dim(a3, core, 2, 0), "z", 1)
+    a4 = along(jnp.where(core == 0, a3[:2], a3[1:3]), "z", 1)
 
     ring = (a_own, a1, ax1, a2)
     near_rows = (lo, hi, lo_next, hi_next, lo_x, hi_x)

time: 102 us -> 98.8 us (0.969)
  waiting for transfers between devices: 27.1 us -> 34 us
  local copies, waits for them, and re-layouts: 7.45 us -> 1.41 us
  Pallas kernels: 27.6 us -> 24.4 us
    ppermute x28, waiting for transfers between devices: 27.1 us -> 34 us  [move(): return lax.ppermute(value, axes, pairs)]
    unnamed x18 -> x2, local copies, waits for them, and re-layouts: 5.02 us -> 0.01 us
    pallas_call x3, Pallas kernels: 18 us -> 14.8 us  [projection(): pl.pallas_call(lambda *refs: projection_kernel(plan, *refs), in_specs=[pl...]
    dynamic_slice x1 -> x0, local copies, waits for them, and re-layouts: 1.03 us -> none  [on_device(): a4 = along(lax.dynamic_slice_in_dim(a3, core, 2, 0), 'z', 1)]
  transfers between devices with their start and end apart: 28 -> 28, of which waited for: 10 -> 11; matrix products, arithmetic and copies ran while one was open for 3% -> 2% of each run, Pallas kernels for 21% -> 19%
where the time goes in v4:
time: 98.8 us; the launch traced here: 98.6 us
  starting transfers between devices  37.8 us (38%)
  waiting for transfers between devices  34 us (34%)
  Pallas kernels  24.4 us (25%)
  local copies, waits for them, and re-layouts  1.41 us (1%)
    ppermute x28, starting transfers between devices, move(): return lax.ppermute(value, axes, pairs)  37.8 us
    ppermute x28, waiting for transfers between devices, move(): return lax.ppermute(value, axes, pairs)  34 us
    pallas_call x3, Pallas kernels, projection(): pl.pallas_call(lambda *refs: projection_kernel(plan, *refs), in_specs=[pl...  14.8 us
    pallas_call x1, Pallas kernels, joined_gradients(): pl.pallas_call(attention_kernel, in_specs=[hbm] * 6 + [vmem], out_specs=v...  9.58 us
  transfers between devices with their start and end apart: 28, of which 11 were waited for; matrix products, arithmetic and copies ran while one was open for 2% of the time, Pallas kernels for 19%

profile of v4, /device:TPU:8, one launch (start us, length us, event | category | flops | bytes accessed | tf_op | source)
XLA Modules:
  0.0 98.6 jit_solution(12727384612171092176)
XLA Ops:
  0.0 3.3 %collective-permute-start = (bf16[64,1280]{1,0:T(8,128)(2,1)}, bf16[64,1280]{1,0:T(8,128)(2,1)S(1)}, u32[]{:S(2)}, u32[]{:S(2)}) collective-permute-start(bf16[64,1280]{1,0:T(8,128)(2,1)} %bitcast.34), channel_id=1, source_target_pairs={{0,0},{1,64},{2,128},{3,192},{64,1},{65,65},{66,129},{67,193},{128... | collective-permute-start | bytes 491528 | tf_op jit(solution)/shard_map/ppermute | solution.py:28
  3.3 1.3 %dynamic_slice.6 = s32[512]{0:T(512)} dynamic-slice(s32[32768]{0:T(1024)} %param.14, s32[]{:T(128)S(6)} %select_n.50), dynamic_slice_sizes={512} | dynamic-slice | bytes 4100 | tf_op jit(solution)/shard_map/dynamic_slice | solution.py:331
  4.6 9.6 %attention_backward.1.refs_1_.refs_2_ = bf16[512,1280]{1,0:T(8,128)(2,1)} custom-call(bf16[512,1024]{1,0:T(8,128)(2,1)} %bitcast.32, bf16[512,1024]{1,0:T(8,128)(2,1)} %bitcast.33, bf16[512,128]{1,0:T(8,128)(2,1)} %bitcast.35, bf16[512,128]{1,0:T(8,128)(2,1)} %bitcast.36, bf16[8,512]{1,0:T(8,128)(2,1)} %bitcast.37, bf16[8,512]{1,0:T(8,128)(2,1)} %bitcast.38, ...), custom_call_target="tpu_custom_call" | custom-call | flops 4000000000 | bytes 4000000 | tf_op jit(solution)/shard_map/attention_backward/pallas_call | solution.py:117
  14.2 0.1 pad_add_fusion.refs_0_
  14.3 0.0 collective-permute-done
  14.3 0.0 collective-permute-start.3
  14.4 1.4 %collective-permute-done.3 = bf16[64,1280]{1,0:T(8,128)(2,1)S(1)} collective-permute-done((bf16[64,1280]{1,0:T(8,128)(2,1)S(1)}, bf16[64,1280]{1,0:T(8,128)(2,1)S(1)}, u32[]{:S(2)}, u32[]{:S(2)}) %collective-permute-start.3) | collective-permute-done | bytes 163872 | tf_op jit(solution)/shard_map/ppermute | solution.py:28
  15.8 2.0 %collective-permute-start.12 = (bf16[128,768]{1,0:T(8,128)(2,1)S(1)}, bf16[128,768]{1,0:T(8,128)(2,1)S(1)}, u32[]{:S(2)}, u32[]{:S(2)}) collective-permute-start(bf16[128,768]{1,0:T(8,128)(2,1)S(1)} %pad_maximum_fusion.4), channel_id=1, source_target_pairs={{0,8},{4,60},{8,16},{12,4},{16,24},{20,12},{24,32},{28,20},{32,40}... | collective-permute-start | bytes 589832 | tf_op jit(solution)/shard_map/ppermute | solution.py:28
  17.8 3.0 %collective-permute-start.4 = (bf16[128,512]{1,0:T(8,128)(2,1)S(1)}, bf16[128,512]{1,0:T(8,128)(2,1)S(1)}, u32[]{:S(2)}, u32[]{:S(2)}) collective-permute-start(bf16[128,512]{1,0:T(8,128)(2,1)S(1)} %pad_maximum_fusion.6), channel_id=1, source_target_pairs={{0,64},{4,196},{64,128},{68,4},{128,192},{132,68},{192,0},{196,132... | collective-permute-start | bytes 393224 | tf_op jit(solution)/shard_map/ppermute | solution.py:28
  20.8 0.3 collective-permute-start.5
  21.1 2.6 %collective-permute-start.6 = (bf16[128,512]{1,0:T(8,128)(2,1)S(1)}, bf16[128,512]{1,0:T(8,128)(2,1)S(1)}, u32[]{:S(2)}, u32[]{:S(2)}) collective-permute-start(bf16[128,512]{1,0:T(8,128)(2,1)S(1)} %pad_maximum_fusion.6), channel_id=1, source_target_pairs={{0,192},{4,68},{64,0},{68,132},{128,64},{132,196},{192,128},{196,4... | collective-permute-start | bytes 393224 | tf_op jit(solution)/shard_map/ppermute | solution.py:28
  23.8 6.4 %collective-permute-start.10 = (bf16[64,768]{1,0:T(8,128)(2,1)S(1)}, bf16[64,768]{1,0:T(8,128)(2,1)S(1)}, u32[]{:S(2)}, u32[]{:S(2)}) collective-permute-start(bf16[64,768]{1,0:T(8,128)(2,1)S(1)} %constant_dynamic-slice_fusion), channel_id=1, source_target_pairs={{0,32},{4,36},{8,40},{12,44},{16,48},{20,52},{24,56},{28,60},{32,0... | collective-permute-start | bytes 294920 | tf_op jit(solution)/shard_map/ppermute | solution.py:28
  30.2 1.6 %collective-permute-start.13 = (bf16[2,128,768]{2,1,0:T(8,128)(2,1)S(1)}, bf16[2,128,768]{2,1,0:T(8,128)(2,1)S(1)}, u32[]{:S(2)}, u32[]{:S(2)}) collective-permute-start(bf16[2,128,768]{2,1,0:T(8,128)(2,1)S(1)} %pad_maximum_fusion.3), channel_id=1, source_target_pairs={{0,16},{4,52},{8,24},{12,60},{16,32},{20,4},{24,40},{28,12},{32,48... | collective-permute-start | bytes 1179656 | tf_op jit(solution)/shard_map/ppermute | solution.py:28
  31.7 1.3 %collective-permute-done.10 = bf16[64,768]{1,0:T(8,128)(2,1)S(1)} collective-permute-done((bf16[64,768]{1,0:T(8,128)(2,1)S(1)}, bf16[64,768]{1,0:T(8,128)(2,1)S(1)}, u32[]{:S(2)}, u32[]{:S(2)}) %collective-permute-start.10) | collective-permute-done | bytes 98336 | tf_op jit(solution)/shard_map/ppermute | solution.py:28
  33.0 1.9 %collective-permute-start.1 = (bf16[512,1280]{1,0:T(8,128)(2,1)S(1)}, bf16[512,1280]{1,0:T(8,128)(2,1)S(1)}, u32[]{:S(2)}, u32[]{:S(2)}) collective-permute-start(bf16[512,1280]{1,0:T(8,128)(2,1)S(1)} %copy-done), channel_id=1, source_target_pairs={{0,1},{1,2},{2,3},{3,0},{4,7},{5,4},{6,5},{7,6},{8,9},{9,10},{10,1... | collective-permute-start | bytes 3932168 | tf_op jit(solution)/shard_map/ppermute | solution.py:28
  34.9 1.4 %collective-permute-start.2 = (bf16[512,1280]{1,0:T(8,128)(2,1)S(1)}, bf16[512,1280]{1,0:T(8,128)(2,1)S(1)}, u32[]{:S(2)}, u32[]{:S(2)}) collective-permute-start(bf16[512,1280]{1,0:T(8,128)(2,1)S(1)} %copy-done), channel_id=1, source_target_pairs={{0,3},{1,0},{2,1},{3,2},{4,5},{5,6},{6,7},{7,4},{8,11},{9,8},{10,9... | collective-permute-start | bytes 3932168 | tf_op jit(solution)/shard_map/ppermute | solution.py:28
  36.2 0.7 collective-permute-start.11
  37.0 0.1 pad_maximum_fusion.2.refs_4_.refs_3_
  37.0 2.4 %collective-permute-start.7 = (bf16[4,128,512]{2,1,0:T(8,128)(2,1)S(1)}, bf16[4,128,512]{2,1,0:T(8,128)(2,1)S(1)}, u32[]{:S(2)}, u32[]{:S(2)}) collective-permute-start(bf16[4,128,512]{2,1,0:T(8,128)(2,1)S(1)} %pad_maximum_fusion.2.refs_4_.refs_3_), channel_id=1, source_target_pairs={{0,8},{4,60},{8,16},{12,4},{16,24},{20,12},{24,32},{28,20},{32,40}... | collective-permute-start | bytes 1572872 | tf_op jit(solution)/shard_map/ppermute | solution.py:28
  39.5 0.8 collective-permute-done.13
  40.3 3.2 %collective-permute-start.15 = (bf16[2,128,768]{2,1,0:T(8,128)(2,1)S(1)}, bf16[2,128,768]{2,1,0:T(8,128)(2,1)S(1)}, u32[]{:S(2)}, u32[]{:S(2)}) collective-permute-start(bf16[2,128,768]{2,1,0:T(8,128)(2,1)S(1)} %collective-permute-done.13), channel_id=1, source_target_pairs={{0,4},{4,0},{1,5},{5,1},{2,6},{6,2},{3,7},{7,3},{8,12},{12,8},{9,1... | collective-permute-start | bytes 1179656 | tf_op jit(solution)/shard_map/ppermute | solution.py:28
  43.5 0.1 select_bitcast_fusion
  43.5 0.1 collective-permute-start.14
  43.7 0.1 pad_maximum_fusion.refs_8_.refs_7_
  43.8 1.0 %collective-permute-done.15 = bf16[2,128,768]{2,1,0:T(8,128)(2,1)S(1)} collective-permute-done((bf16[2,128,768]{2,1,0:T(8,128)(2,1)S(1)}, bf16[2,128,768]{2,1,0:T(8,128)(2,1)S(1)}, u32[]{:S(2)}, u32[]{:S(2)}) %collective-permute-start.15) | collective-permute-done | bytes 393248 | tf_op jit(solution)/shard_map/ppermute | solution.py:28
  44.8 0.3 collective-permute-done.14
  45.1 0.1 pad_maximum_fusion.1.refs_9_.refs_8_
  45.2 0.3 collective-permute-start.16
  45.5 1.7 %collective-permute-start.17 = (bf16[4,128,768]{2,1,0:T(8,128)(2,1)S(1)}, bf16[4,128,768]{2,1,0:T(8,128)(2,1)S(1)}, u32[]{:S(2)}, u32[]{:S(2)}) collective-permute-start(bf16[4,128,768]{2,1,0:T(8,128)(2,1)S(1)} %pad_maximum_fusion.1.refs_9_.refs_8_), channel_id=1, source_target_pairs={{0,64},{4,196},{64,128},{68,4},{128,192},{132,68},{192,0},{196,132... | collective-permute-start | bytes 2359304 | tf_op jit(solution)/shard_map/ppermute | solution.py:28
  47.2 2.4 %collective-permute-done.7.refs_5_.refs_4_ = bf16[4,128,512]{2,1,0:T(8,128)(2,1)S(1)} collective-permute-done((bf16[4,128,512]{2,1,0:T(8,128)(2,1)S(1)}, bf16[4,128,512]{2,1,0:T(8,128)(2,1)S(1)}, u32[]{:S(2)}, u32[]{:S(2)}) %collective-permute-start.7) | collective-permute-done | bytes 524320 | tf_op jit(solution)/shard_map/ppermute | solution.py:28
  49.6 1.4 %collective-permute-start.9 = (bf16[4,128,512]{2,1,0:T(8,128)(2,1)S(1)}, bf16[4,128,512]{2,1,0:T(8,128)(2,1)S(1)}, u32[]{:S(2)}, u32[]{:S(2)}) collective-permute-start(bf16[4,128,512]{2,1,0:T(8,128)(2,1)S(1)} %collective-permute-done.7.refs_5_.refs_4_), channel_id=1, source_target_pairs={{0,8},{4,60},{8,16},{12,4},{16,24},{20,12},{24,32},{28,20},{32,40}... | collective-permute-start | bytes 1572872 | tf_op jit(solution)/shard_map/ppermute | solution.py:28
  51.0 9.0 %collective-permute-done.9.refs_7_.refs_6_ = bf16[4,128,512]{2,1,0:T(8,128)(2,1)S(1)} collective-permute-done((bf16[4,128,512]{2,1,0:T(8,128)(2,1)S(1)}, bf16[4,128,512]{2,1,0:T(8,128)(2,1)S(1)}, u32[]{:S(2)}, u32[]{:S(2)}) %collective-permute-start.9) | collective-permute-done | bytes 524320 | tf_op jit(solution)/shard_map/ppermute | solution.py:28
  60.0 0.2 collective-permute-start.21
  60.2 1.5 %collective-permute-start.18 = (bf16[4,128,768]{2,1,0:T(8,128)(2,1)S(1)}, bf16[4,128,768]{2,1,0:T(8,128)(2,1)S(1)}, u32[]{:S(2)}, u32[]{:S(2)}) collective-permute-start(bf16[4,128,768]{2,1,0:T(8,128)(2,1)S(1)} %collective-permute-done.16.refs_10_.refs_9_), channel_id=1, source_target_pairs={{0,4},{4,0},{1,5},{5,1},{2,6},{6,2},{3,7},{7,3},{8,12},{12,8},{9,1... | collective-permute-start | bytes 2359304 | tf_op jit(solution)/shard_map/ppermute | solution.py:28
  61.7 3.9 %collective-permute-done.17.refs_11_.refs_10_ = bf16[4,128,768]{2,1,0:T(8,128)(2,1)S(1)} collective-permute-done((bf16[4,128,768]{2,1,0:T(8,128)(2,1)S(1)}, bf16[4,128,768]{2,1,0:T(8,128)(2,1)S(1)}, u32[]{:S(2)}, u32[]{:S(2)}) %collective-permute-start.17) | collective-permute-done | bytes 786464 | tf_op jit(solution)/shard_map/ppermute | solution.py:28
  65.7 0.5 collective-permute-start.8
  66.2 0.2 collective-permute-start.20
  66.5 3.9 %collective-permute-done.21.refs_7_ = bf16[4,128,512]{2,1,0:T(8,128)(2,1)S(1)} collective-permute-done((bf16[4,128,512]{2,1,0:T(8,128)(2,1)S(1)}, bf16[4,128,512]{2,1,0:T(8,128)(2,1)S(1)}, u32[]{:S(2)}, u32[]{:S(2)}) %collective-permute-start.21) | collective-permute-done | bytes 524320 | tf_op jit(solution)/shard_map/ppermute | solution.py:28
  70.4 1.9 %collective-permute-start.23 = (bf16[512,1280]{1,0:T(8,128)(2,1)S(1)}, bf16[512,1280]{1,0:T(8,128)(2,1)S(1)}, u32[]{:S(2)}, u32[]{:S(2)}) collective-permute-start(bf16[512,1280]{1,0:T(8,128)(2,1)S(1)} %collective-permute-done.1.refs_2_.refs_3_), channel_id=1, source_target_pairs={{0,1},{1,2},{2,3},{3,0},{4,7},{5,4},{6,5},{7,6},{8,9},{9,10},{10,1... | collective-permute-start | bytes 3932168 | tf_op jit(solution)/shard_map/ppermute | solution.py:28
  72.3 0.1 collective-permute-start.22
  72.4 5.7 %project_near.1.refs_1_ = f32[8,512,128]{2,1,0:T(8,128)S(1)} custom-call(s32[4]{0:T(128)S(1)} %pad_add_fusion.refs_0_, bf16[512,1280]{1,0:T(8,128)(2,1)S(1)} %copy-done, bf16[512,1280]{1,0:T(8,128)(2,1)S(1)} %collective-permute-done.1.refs_2_.refs_3_, bf16[512,1280]{1,0:T(8,128)(2,1)S(1)} %collective-permute-done.2.refs_3_.refs_4_, ...), custom_call_target="tpu_custom_call" | custom-call | flops 450000000 | bytes 450000 | tf_op jit(solution)/shard_map/project_near/pallas_call | solution.py:284
  78.1 1.9 %collective-permute-done.22.refs_9_ = bf16[2,128,512]{2,1,0:T(8,128)(2,1)S(1)} collective-permute-done((bf16[2,128,512]{2,1,0:T(8,128)(2,1)S(1)}, bf16[2,128,512]{2,1,0:T(8,128)(2,1)S(1)}, u32[]{:S(2)}, u32[]{:S(2)}) %collective-permute-start.22) | collective-permute-done | bytes 262176 | tf_op jit(solution)/shard_map/ppermute | solution.py:28
  79.9 0.5 collective-permute-start.24
  80.5 0.0 collective-permute-start.25
  80.5 0.5 collective-permute-start.26
  81.0 8.2 %collective-permute-done.23.refs_2_.refs_5_ = bf16[512,1280]{1,0:T(8,128)(2,1)S(1)} collective-permute-done((bf16[512,1280]{1,0:T(8,128)(2,1)S(1)}, bf16[512,1280]{1,0:T(8,128)(2,1)S(1)}, u32[]{:S(2)}, u32[]{:S(2)}) %collective-permute-start.23) | collective-permute-done | bytes 1310752 | tf_op jit(solution)/shard_map/ppermute | solution.py:28
  89.2 3.8 %project_far_head.1.refs_1_ = f32[8,512,128]{2,1,0:T(8,128)S(1)} custom-call(s32[4]{0:T(128)S(1)} %pad_add_fusion.refs_0_, f32[8,512,128]{2,1,0:T(8,128)S(1)} %project_near.1.refs_1_, bf16[512,1280]{1,0:T(8,128)(2,1)S(1)} %collective-permute-done.23.refs_2_.refs_5_, bf16[4,128,512]{2,1,0:T(8,128)(2,1)S(1)} %pad_maximum_fusion.2.refs_4_.refs_3_, ...), custom_call_target="tpu_custom_call" | custom-call | flops 250000000 | bytes 250000 | tf_op jit(solution)/shard_map/project_far_head/pallas_call | solution.py:284
  93.0 5.4 %project_rest.1 = bf16[512,1024]{1,0:T(8,128)(2,1)} custom-call(s32[4]{0:T(128)S(1)} %pad_add_fusion.refs_0_, f32[8,512,128]{2,1,0:T(8,128)S(1)} %project_far_head.1.refs_1_, bf16[512,1280]{1,0:T(8,128)(2,1)S(1)} %copy-done, bf16[512,1280]{1,0:T(8,128)(2,1)S(1)} %collective-permute-done.1.refs_2_.refs_3_, ...), custom_call_target="tpu_custom_call" | custom-call | flops 450000000 | bytes 450000 | tf_op jit(solution)/shard_map/project_rest/pallas_call | solution.py:284
  (29 shorter events, 0.2 us)
Async XLA Ops:
  0.0 14.3 %collective-permute-start = (bf16[64,1280]{1,0:T(8,128)(2,1)}, bf16[64,1280]{1,0:T(8,128)(2,1)S(1)}, u32[]{:S(2)}, u32[]{:S(2)}) collective-permute-start(bf16[64,1280]{1,0:T(8,128)(2,1)} %bitcast.34), channel_id=1, source_target_pairs={{0,0},{1,64},{2,128},{3,192},{64,1},{65,65},{66,129},{67,193},{128... | collective-permute-start | bytes 491528 | tf_op jit(solution)/shard_map/ppermute | solution.py:28
  14.3 1.4 %collective-permute-start.3 = (bf16[64,1280]{1,0:T(8,128)(2,1)S(1)}, bf16[64,1280]{1,0:T(8,128)(2,1)S(1)}, u32[]{:S(2)}, u32[]{:S(2)}) collective-permute-start(bf16[64,1280]{1,0:T(8,128)(2,1)S(1)} %collective-permute-done), channel_id=1, source_target_pairs={{0,4},{4,0},{1,5},{5,1},{2,6},{6,2},{3,7},{7,3},{8,12},{12,8},{9,1... | collective-permute-start | bytes 491528 | tf_op jit(solution)/shard_map/ppermute | solution.py:28
  14.4 18.6 %copy-start = (bf16[512,1280]{1,0:T(8,128)(2,1)S(1)}, bf16[512,1280]{1,0:T(8,128)(2,1)}, u32[]{:S(2)}) copy-start(bf16[512,1280]{1,0:T(8,128)(2,1)} %attention_backward.1.refs_1_.refs_2_) | copy-start | bytes 3932164
  15.8 14.3 %collective-permute-start.12 = (bf16[128,768]{1,0:T(8,128)(2,1)S(1)}, bf16[128,768]{1,0:T(8,128)(2,1)S(1)}, u32[]{:S(2)}, u32[]{:S(2)}) collective-permute-start(bf16[128,768]{1,0:T(8,128)(2,1)S(1)} %pad_maximum_fusion.4), channel_id=1, source_target_pairs={{0,8},{4,60},{8,16},{12,4},{16,24},{20,12},{24,32},{28,20},{32,40}... | collective-permute-start | bytes 589832 | tf_op jit(solution)/shard_map/ppermute | solution.py:28
  17.8 17.1 %collective-permute-start.4 = (bf16[128,512]{1,0:T(8,128)(2,1)S(1)}, bf16[128,512]{1,0:T(8,128)(2,1)S(1)}, u32[]{:S(2)}, u32[]{:S(2)}) collective-permute-start(bf16[128,512]{1,0:T(8,128)(2,1)S(1)} %pad_maximum_fusion.6), channel_id=1, source_target_pairs={{0,64},{4,196},{64,128},{68,4},{128,192},{132,68},{192,0},{196,132... | collective-permute-start | bytes 393224 | tf_op jit(solution)/shard_map/ppermute | solution.py:28
  20.8 15.4 %collective-permute-start.5 = (bf16[128,512]{1,0:T(8,128)(2,1)S(1)}, bf16[128,512]{1,0:T(8,128)(2,1)S(1)}, u32[]{:S(2)}, u32[]{:S(2)}) collective-permute-start(bf16[128,512]{1,0:T(8,128)(2,1)S(1)} %pad_maximum_fusion.6), channel_id=1, source_target_pairs={{0,128},{4,132},{64,192},{68,196},{128,0},{132,4},{192,64},{196,68... | collective-permute-start | bytes 393224 | tf_op jit(solution)/shard_map/ppermute | solution.py:28
  21.1 15.8 %collective-permute-start.6 = (bf16[128,512]{1,0:T(8,128)(2,1)S(1)}, bf16[128,512]{1,0:T(8,128)(2,1)S(1)}, u32[]{:S(2)}, u32[]{:S(2)}) collective-permute-start(bf16[128,512]{1,0:T(8,128)(2,1)S(1)} %pad_maximum_fusion.6), channel_id=1, source_target_pairs={{0,192},{4,68},{64,0},{68,132},{128,64},{132,196},{192,128},{196,4... | collective-permute-start | bytes 393224 | tf_op jit(solution)/shard_map/ppermute | solution.py:28
  23.8 9.2 %collective-permute-start.10 = (bf16[64,768]{1,0:T(8,128)(2,1)S(1)}, bf16[64,768]{1,0:T(8,128)(2,1)S(1)}, u32[]{:S(2)}, u32[]{:S(2)}) collective-permute-start(bf16[64,768]{1,0:T(8,128)(2,1)S(1)} %constant_dynamic-slice_fusion), channel_id=1, source_target_pairs={{0,32},{4,36},{8,40},{12,44},{16,48},{20,52},{24,56},{28,60},{32,0... | collective-permute-start | bytes 294920 | tf_op jit(solution)/shard_map/ppermute | solution.py:28
  30.2 10.1 %collective-permute-start.13 = (bf16[2,128,768]{2,1,0:T(8,128)(2,1)S(1)}, bf16[2,128,768]{2,1,0:T(8,128)(2,1)S(1)}, u32[]{:S(2)}, u32[]{:S(2)}) collective-permute-start(bf16[2,128,768]{2,1,0:T(8,128)(2,1)S(1)} %pad_maximum_fusion.3), channel_id=1, source_target_pairs={{0,16},{4,52},{8,24},{12,60},{16,32},{20,4},{24,40},{28,12},{32,48... | collective-permute-start | bytes 1179656 | tf_op jit(solution)/shard_map/ppermute | solution.py:28
  33.0 32.7 %collective-permute-start.1 = (bf16[512,1280]{1,0:T(8,128)(2,1)S(1)}, bf16[512,1280]{1,0:T(8,128)(2,1)S(1)}, u32[]{:S(2)}, u32[]{:S(2)}) collective-permute-start(bf16[512,1280]{1,0:T(8,128)(2,1)S(1)} %copy-done), channel_id=1, source_target_pairs={{0,1},{1,2},{2,3},{3,0},{4,7},{5,4},{6,5},{7,6},{8,9},{9,10},{10,1... | collective-permute-start | bytes 3932168 | tf_op jit(solution)/shard_map/ppermute | solution.py:28
  34.9 31.3 %collective-permute-start.2 = (bf16[512,1280]{1,0:T(8,128)(2,1)S(1)}, bf16[512,1280]{1,0:T(8,128)(2,1)S(1)}, u32[]{:S(2)}, u32[]{:S(2)}) collective-permute-start(bf16[512,1280]{1,0:T(8,128)(2,1)S(1)} %copy-done), channel_id=1, source_target_pairs={{0,3},{1,0},{2,1},{3,2},{4,5},{5,6},{6,7},{7,4},{8,11},{9,8},{10,9... | collective-permute-start | bytes 3932168 | tf_op jit(solution)/shard_map/ppermute | solution.py:28
  36.2 3.2 %collective-permute-start.11 = (bf16[64,768]{1,0:T(8,128)(2,1)S(1)}, bf16[64,768]{1,0:T(8,128)(2,1)S(1)}, u32[]{:S(2)}, u32[]{:S(2)}) collective-permute-start(bf16[64,768]{1,0:T(8,128)(2,1)S(1)} %collective-permute-done.10), channel_id=1, source_target_pairs={{0,4},{4,0},{1,5},{5,1},{2,6},{6,2},{3,7},{7,3},{8,12},{12,8},{9,1... | collective-permute-start | bytes 294920 | tf_op jit(solution)/shard_map/ppermute | solution.py:28
  37.0 12.5 %collective-permute-start.7 = (bf16[4,128,512]{2,1,0:T(8,128)(2,1)S(1)}, bf16[4,128,512]{2,1,0:T(8,128)(2,1)S(1)}, u32[]{:S(2)}, u32[]{:S(2)}) collective-permute-start(bf16[4,128,512]{2,1,0:T(8,128)(2,1)S(1)} %pad_maximum_fusion.2.refs_4_.refs_3_), channel_id=1, source_target_pairs={{0,8},{4,60},{8,16},{12,4},{16,24},{20,12},{24,32},{28,20},{32,40}... | collective-permute-start | bytes 1572872 | tf_op jit(solution)/shard_map/ppermute | solution.py:28
  40.3 4.5 %collective-permute-start.15 = (bf16[2,128,768]{2,1,0:T(8,128)(2,1)S(1)}, bf16[2,128,768]{2,1,0:T(8,128)(2,1)S(1)}, u32[]{:S(2)}, u32[]{:S(2)}) collective-permute-start(bf16[2,128,768]{2,1,0:T(8,128)(2,1)S(1)} %collective-permute-done.13), channel_id=1, source_target_pairs={{0,4},{4,0},{1,5},{5,1},{2,6},{6,2},{3,7},{7,3},{8,12},{12,8},{9,1... | collective-permute-start | bytes 1179656 | tf_op jit(solution)/shard_map/ppermute | solution.py:28
  43.5 1.6 %collective-permute-start.14 = (bf16[128,768]{1,0:T(8,128)(2,1)S(1)}, bf16[128,768]{1,0:T(8,128)(2,1)S(1)}, u32[]{:S(2)}, u32[]{:S(2)}) collective-permute-start(bf16[128,768]{1,0:T(8,128)(2,1)S(1)} %collective-permute-done.12), channel_id=1, source_target_pairs={{0,4},{4,0},{1,5},{5,1},{2,6},{6,2},{3,7},{7,3},{8,12},{12,8},{9,1... | collective-permute-start | bytes 589832 | tf_op jit(solution)/shard_map/ppermute | solution.py:28
  45.2 15.0 %collective-permute-start.16 = (bf16[4,128,768]{2,1,0:T(8,128)(2,1)S(1)}, bf16[4,128,768]{2,1,0:T(8,128)(2,1)S(1)}, u32[]{:S(2)}, u32[]{:S(2)}) collective-permute-start(bf16[4,128,768]{2,1,0:T(8,128)(2,1)S(1)} %pad_maximum_fusion.refs_8_.refs_7_), channel_id=1, source_target_pairs={{0,64},{4,196},{64,128},{68,4},{128,192},{132,68},{192,0},{196,132... | collective-permute-start | bytes 2359304 | tf_op jit(solution)/shard_map/ppermute | solution.py:28
  45.5 20.2 %collective-permute-start.17 = (bf16[4,128,768]{2,1,0:T(8,128)(2,1)S(1)}, bf16[4,128,768]{2,1,0:T(8,128)(2,1)S(1)}, u32[]{:S(2)}, u32[]{:S(2)}) collective-permute-start(bf16[4,128,768]{2,1,0:T(8,128)(2,1)S(1)} %pad_maximum_fusion.1.refs_9_.refs_8_), channel_id=1, source_target_pairs={{0,64},{4,196},{64,128},{68,4},{128,192},{132,68},{192,0},{196,132... | collective-permute-start | bytes 2359304 | tf_op jit(solution)/shard_map/ppermute | solution.py:28
  49.6 10.4 %collective-permute-start.9 = (bf16[4,128,512]{2,1,0:T(8,128)(2,1)S(1)}, bf16[4,128,512]{2,1,0:T(8,128)(2,1)S(1)}, u32[]{:S(2)}, u32[]{:S(2)}) collective-permute-start(bf16[4,128,512]{2,1,0:T(8,128)(2,1)S(1)} %collective-permute-done.7.refs_5_.refs_4_), channel_id=1, source_target_pairs={{0,8},{4,60},{8,16},{12,4},{16,24},{20,12},{24,32},{28,20},{32,40}... | collective-permute-start | bytes 1572872 | tf_op jit(solution)/shard_map/ppermute | solution.py:28
  60.0 10.4 %collective-permute-start.21 = (bf16[4,128,512]{2,1,0:T(8,128)(2,1)S(1)}, bf16[4,128,512]{2,1,0:T(8,128)(2,1)S(1)}, u32[]{:S(2)}, u32[]{:S(2)}) collective-permute-start(bf16[4,128,512]{2,1,0:T(8,128)(2,1)S(1)} %collective-permute-done.9.refs_7_.refs_6_), channel_id=1, source_target_pairs={{0,8},{4,60},{8,16},{12,4},{16,24},{20,12},{24,32},{28,20},{32,40}... | collective-permute-start | bytes 1572872 | tf_op jit(solution)/shard_map/ppermute | solution.py:28
  60.2 12.2 %collective-permute-start.18 = (bf16[4,128,768]{2,1,0:T(8,128)(2,1)S(1)}, bf16[4,128,768]{2,1,0:T(8,128)(2,1)S(1)}, u32[]{:S(2)}, u32[]{:S(2)}) collective-permute-start(bf16[4,128,768]{2,1,0:T(8,128)(2,1)S(1)} %collective-permute-done.16.refs_10_.refs_9_), channel_id=1, source_target_pairs={{0,4},{4,0},{1,5},{5,1},{2,6},{6,2},{3,7},{7,3},{8,12},{12,8},{9,1... | collective-permute-start | bytes 2359304 | tf_op jit(solution)/shard_map/ppermute | solution.py:28
  65.7 6.7 %collective-permute-start.19 = (bf16[4,128,768]{2,1,0:T(8,128)(2,1)S(1)}, bf16[4,128,768]{2,1,0:T(8,128)(2,1)S(1)}, u32[]{:S(2)}, u32[]{:S(2)}) collective-permute-start(bf16[4,128,768]{2,1,0:T(8,128)(2,1)S(1)} %collective-permute-done.17.refs_11_.refs_10_), channel_id=1, source_target_pairs={{0,4},{4,0},{1,5},{5,1},{2,6},{6,2},{3,7},{7,3},{8,12},{12,8},{9,1... | collective-permute-start | bytes 2359304 | tf_op jit(solution)/shard_map/ppermute | solution.py:28
  65.7 6.6 %collective-permute-start.8 = (bf16[4,128,512]{2,1,0:T(8,128)(2,1)S(1)}, bf16[4,128,512]{2,1,0:T(8,128)(2,1)S(1)}, u32[]{:S(2)}, u32[]{:S(2)}) collective-permute-start(bf16[4,128,512]{2,1,0:T(8,128)(2,1)S(1)} %collective-permute-done.7.refs_5_.refs_4_), channel_id=1, source_target_pairs={{0,4},{4,0},{1,5},{5,1},{2,6},{6,2},{3,7},{7,3},{8,12},{12,8},{9,1... | collective-permute-start | bytes 1572872 | tf_op jit(solution)/shard_map/ppermute | solution.py:28
  66.2 13.7 %collective-permute-start.20 = (bf16[4,128,768]{2,1,0:T(8,128)(2,1)S(1)}, bf16[4,128,768]{2,1,0:T(8,128)(2,1)S(1)}, u32[]{:S(2)}, u32[]{:S(2)}) collective-permute-start(bf16[4,128,768]{2,1,0:T(8,128)(2,1)S(1)} %collective-permute-done.16.refs_10_.refs_9_), channel_id=1, source_target_pairs={{0,64},{4,196},{64,128},{68,4},{128,192},{132,68},{192,0},{196,132... | collective-permute-start | bytes 2359304 | tf_op jit(solution)/shard_map/ppermute | solution.py:28
  70.4 18.8 %collective-permute-start.23 = (bf16[512,1280]{1,0:T(8,128)(2,1)S(1)}, bf16[512,1280]{1,0:T(8,128)(2,1)S(1)}, u32[]{:S(2)}, u32[]{:S(2)}) collective-permute-start(bf16[512,1280]{1,0:T(8,128)(2,1)S(1)} %collective-permute-done.1.refs_2_.refs_3_), channel_id=1, source_target_pairs={{0,1},{1,2},{2,3},{3,0},{4,7},{5,4},{6,5},{7,6},{8,9},{9,10},{10,1... | collective-permute-start | bytes 3932168 | tf_op jit(solution)/shard_map/ppermute | solution.py:28
  72.3 7.7 %collective-permute-start.22 = (bf16[2,128,512]{2,1,0:T(8,128)(2,1)S(1)}, bf16[2,128,512]{2,1,0:T(8,128)(2,1)S(1)}, u32[]{:S(2)}, u32[]{:S(2)}) collective-permute-start(bf16[2,128,512]{2,1,0:T(8,128)(2,1)S(1)} %slice_select_fusion), channel_id=1, source_target_pairs={{0,8},{4,60},{8,16},{12,4},{16,24},{20,12},{24,32},{28,20},{32,40}... | collective-permute-start | bytes 786440 | tf_op jit(solution)/shard_map/ppermute | solution.py:28
  79.9 13.0 %collective-permute-start.27 = (bf16[4,128,768]{2,1,0:T(8,128)(2,1)S(1)}, bf16[4,128,768]{2,1,0:T(8,128)(2,1)S(1)}, u32[]{:S(2)}, u32[]{:S(2)}) collective-permute-start(bf16[4,128,768]{2,1,0:T(8,128)(2,1)S(1)} %collective-permute-done.20.refs_11_), channel_id=1, source_target_pairs={{0,4},{4,0},{1,5},{5,1},{2,6},{6,2},{3,7},{7,3},{8,12},{12,8},{9,1... | collective-permute-start | bytes 2359304 | tf_op jit(solution)/shard_map/ppermute | solution.py:28
  79.9 13.0 %collective-permute-start.24 = (bf16[4,128,512]{2,1,0:T(8,128)(2,1)S(1)}, bf16[4,128,512]{2,1,0:T(8,128)(2,1)S(1)}, u32[]{:S(2)}, u32[]{:S(2)}) collective-permute-start(bf16[4,128,512]{2,1,0:T(8,128)(2,1)S(1)} %collective-permute-done.9.refs_7_.refs_6_), channel_id=1, source_target_pairs={{0,4},{4,0},{1,5},{5,1},{2,6},{6,2},{3,7},{7,3},{8,12},{12,8},{9,1... | collective-permute-start | bytes 1572872 | tf_op jit(solution)/shard_map/ppermute | solution.py:28
  80.5 12.5 %collective-permute-start.25 = (bf16[4,128,512]{2,1,0:T(8,128)(2,1)S(1)}, bf16[4,128,512]{2,1,0:T(8,128)(2,1)S(1)}, u32[]{:S(2)}, u32[]{:S(2)}) collective-permute-start(bf16[4,128,512]{2,1,0:T(8,128)(2,1)S(1)} %collective-permute-done.21.refs_7_), channel_id=1, source_target_pairs={{0,4},{4,0},{1,5},{5,1},{2,6},{6,2},{3,7},{7,3},{8,12},{12,8},{9,1... | collective-permute-start | bytes 1572872 | tf_op jit(solution)/shard_map/ppermute | solution.py:28
  80.5 12.5 %collective-permute-start.26 = (bf16[2,128,512]{2,1,0:T(8,128)(2,1)S(1)}, bf16[2,128,512]{2,1,0:T(8,128)(2,1)S(1)}, u32[]{:S(2)}, u32[]{:S(2)}) collective-permute-start(bf16[2,128,512]{2,1,0:T(8,128)(2,1)S(1)} %collective-permute-done.22.refs_9_), channel_id=1, source_target_pairs={{0,4},{4,0},{1,5},{5,1},{2,6},{6,2},{3,7},{7,3},{8,12},{12,8},{9,1... | collective-permute-start | bytes 786440 | tf_op jit(solution)/shard_map/ppermute | solution.py:28

commit v5 on v4

--- a/solution.py
+++ b/solution.py
@@ -253,7 +253,7 @@
             acc[tile(4 if offset == "far" else sign * offset)] += total[:, k * BLOCK:(k + 1) * BLOCK]
 
     if one_row_head:
-        row_heads[0].wait()
+        pl.when(meets[0][1] >= 0)(row_heads[0].wait)
     else:
         for made in row_heads:
             made.wait()
@@ -312,6 +312,10 @@
             ("hi", True, -1, against), ("lo", False, 1, against), ("hi", False, 1, against)]
 
 
+def far_rows(against):
+    return [("lo", True, "far", against), ("lo", False, "far", against)]
+
+
 def in_order(*values):
     return lax.optimization_barrier(values)
 
@@ -373,11 +377,12 @@
     far_x = swap_cores(lo_far)
     ax3 = swap_cores(a3)
     ax4 = swap_cores(a4)
-    acc = projection(Plan((2,), (0, -1, 1, -2), rows_of((2,)), False, False), "project_far_head", where,
-                     acc, j_far, *ring, *near_rows)
-    far_rows = [("lo", True, "far", ALL), ("lo", False, "far", ALL)]
-    return projection(Plan(ALL, (2, -3, 3, "far"), far_rows, False, True), "project_rest", where,
-                      acc, joined, j_first, j_second, j_far, ax2, a3, ax3, a4, ax4, lo_far, far_x)
+    rest = (ax2, a3, ax3, a4, ax4)
+    acc = projection(Plan(NEAR, (2, -3, 3, "far"), far_rows(NEAR), False, False), "project_rest", where,
+                     acc, joined, j_first, j_second, *rest, lo_far, far_x)
+    acc, j_far = in_order(acc, j_far)
+    plan = Plan((2,), (0, -1, 1, -2, 2, -3, 3, "far"), rows_of((2,)) + far_rows((2,)), False, True)
+    return projection(plan, "project_far_head", where, acc, j_far, *ring, *rest, *near_rows, lo_far, far_x)
 
 
 def solution(mesh):

time: 98.8 us -> 95.7 us (0.969)
  waiting for transfers between devices: 34 us -> 30.2 us
    ppermute x28, waiting for transfers between devices: 34 us -> 30.2 us  [move(): return lax.ppermute(value, axes, pairs)]
  transfers between devices with their start and end apart: 28 -> 28, of which waited for: 11 -> 14; matrix products, arithmetic and copies ran while one was open for 2% -> 2% of each run, Pallas kernels for 19% -> 20%
where the time goes in v5:
time: 95.7 us; the launch traced here: 95.2 us
  starting transfers between devices  37.8 us (39%)
  waiting for transfers between devices  30.2 us (32%)
  Pallas kernels  24.9 us (26%)
  local copies, waits for them, and re-layouts  1.41 us (1%)
    ppermute x28, starting transfers between devices, move(): return lax.ppermute(value, axes, pairs)  37.8 us
    ppermute x28, waiting for transfers between devices, move(): return lax.ppermute(value, axes, pairs)  30.2 us
    pallas_call x3, Pallas kernels, projection(): pl.pallas_call(lambda *refs: projection_kernel(plan, *refs), in_specs=[pl...  15.3 us
    pallas_call x1, Pallas kernels, joined_gradients(): pl.pallas_call(attention_kernel, in_specs=[hbm] * 6 + [vmem], out_specs=v...  9.58 us
  transfers between devices with their start and end apart: 28, of which 14 were waited for; matrix products, arithmetic and copies ran while one was open for 2% of the time, Pallas kernels for 20%

profile of v5, /device:TPU:8, one launch (start us, length us, event | category | flops | bytes accessed | tf_op | source)
XLA Modules:
  0.0 95.2 jit_solution(7279631227924964993)
XLA Ops:
  0.0 3.3 %collective-permute-start = (bf16[64,1280]{1,0:T(8,128)(2,1)}, bf16[64,1280]{1,0:T(8,128)(2,1)S(1)}, u32[]{:S(2)}, u32[]{:S(2)}) collective-permute-start(bf16[64,1280]{1,0:T(8,128)(2,1)} %bitcast.34), channel_id=1, source_target_pairs={{0,0},{1,64},{2,128},{3,192},{64,1},{65,65},{66,129},{67,193},{128... | collective-permute-start | bytes 491528 | tf_op jit(solution)/shard_map/ppermute | solution.py:28
  3.3 1.3 %dynamic_slice.6 = s32[512]{0:T(512)} dynamic-slice(s32[32768]{0:T(1024)} %param.14, s32[]{:T(128)S(6)} %select_n.50), dynamic_slice_sizes={512} | dynamic-slice | bytes 4100 | tf_op jit(solution)/shard_map/dynamic_slice | solution.py:335
  4.6 9.6 %attention_backward.1.refs_1_.refs_2_ = bf16[512,1280]{1,0:T(8,128)(2,1)} custom-call(bf16[512,1024]{1,0:T(8,128)(2,1)} %bitcast.32, bf16[512,1024]{1,0:T(8,128)(2,1)} %bitcast.33, bf16[512,128]{1,0:T(8,128)(2,1)} %bitcast.35, bf16[512,128]{1,0:T(8,128)(2,1)} %bitcast.36, bf16[8,512]{1,0:T(8,128)(2,1)} %bitcast.37, bf16[8,512]{1,0:T(8,128)(2,1)} %bitcast.38, ...), custom_call_target="tpu_custom_call" | custom-call | flops 4000000000 | bytes 4000000 | tf_op jit(solution)/shard_map/attention_backward/pallas_call | solution.py:117
  14.2 0.1 pad_add_fusion.refs_0_
  14.4 1.4 %collective-permute-done.3 = bf16[64,1280]{1,0:T(8,128)(2,1)S(1)} collective-permute-done((bf16[64,1280]{1,0:T(8,128)(2,1)S(1)}, bf16[64,1280]{1,0:T(8,128)(2,1)S(1)}, u32[]{:S(2)}, u32[]{:S(2)}) %collective-permute-start.3) | collective-permute-done | bytes 163872 | tf_op jit(solution)/shard_map/ppermute | solution.py:28
  15.8 2.0 %collective-permute-start.12 = (bf16[128,768]{1,0:T(8,128)(2,1)S(1)}, bf16[128,768]{1,0:T(8,128)(2,1)S(1)}, u32[]{:S(2)}, u32[]{:S(2)}) collective-permute-start(bf16[128,768]{1,0:T(8,128)(2,1)S(1)} %pad_maximum_fusion.4), channel_id=1, source_target_pairs={{0,8},{4,60},{8,16},{12,4},{16,24},{20,12},{24,32},{28,20},{32,40}... | collective-permute-start | bytes 589832 | tf_op jit(solution)/shard_map/ppermute | solution.py:28
  17.8 3.0 %collective-permute-start.4 = (bf16[128,512]{1,0:T(8,128)(2,1)S(1)}, bf16[128,512]{1,0:T(8,128)(2,1)S(1)}, u32[]{:S(2)}, u32[]{:S(2)}) collective-permute-start(bf16[128,512]{1,0:T(8,128)(2,1)S(1)} %pad_maximum_fusion.6), channel_id=1, source_target_pairs={{0,64},{4,196},{64,128},{68,4},{128,192},{132,68},{192,0},{196,132... | collective-permute-start | bytes 393224 | tf_op jit(solution)/shard_map/ppermute | solution.py:28
  20.8 0.3 collective-permute-start.5
  21.1 2.6 %collective-permute-start.6 = (bf16[128,512]{1,0:T(8,128)(2,1)S(1)}, bf16[128,512]{1,0:T(8,128)(2,1)S(1)}, u32[]{:S(2)}, u32[]{:S(2)}) collective-permute-start(bf16[128,512]{1,0:T(8,128)(2,1)S(1)} %pad_maximum_fusion.6), channel_id=1, source_target_pairs={{0,192},{4,68},{64,0},{68,132},{128,64},{132,196},{192,128},{196,4... | collective-permute-start | bytes 393224 | tf_op jit(solution)/shard_map/ppermute | solution.py:28
  23.8 6.4 %collective-permute-start.10 = (bf16[64,768]{1,0:T(8,128)(2,1)S(1)}, bf16[64,768]{1,0:T(8,128)(2,1)S(1)}, u32[]{:S(2)}, u32[]{:S(2)}) collective-permute-start(bf16[64,768]{1,0:T(8,128)(2,1)S(1)} %constant_dynamic-slice_fusion), channel_id=1, source_target_pairs={{0,32},{4,36},{8,40},{12,44},{16,48},{20,52},{24,56},{28,60},{32,0... | collective-permute-start | bytes 294920 | tf_op jit(solution)/shard_map/ppermute | solution.py:28
  30.2 1.6 %collective-permute-start.13 = (bf16[2,128,768]{2,1,0:T(8,128)(2,1)S(1)}, bf16[2,128,768]{2,1,0:T(8,128)(2,1)S(1)}, u32[]{:S(2)}, u32[]{:S(2)}) collective-permute-start(bf16[2,128,768]{2,1,0:T(8,128)(2,1)S(1)} %pad_maximum_fusion.3), channel_id=1, source_target_pairs={{0,16},{4,52},{8,24},{12,60},{16,32},{20,4},{24,40},{28,12},{32,48... | collective-permute-start | bytes 1179656 | tf_op jit(solution)/shard_map/ppermute | solution.py:28
  31.7 1.3 %collective-permute-done.10 = bf16[64,768]{1,0:T(8,128)(2,1)S(1)} collective-permute-done((bf16[64,768]{1,0:T(8,128)(2,1)S(1)}, bf16[64,768]{1,0:T(8,128)(2,1)S(1)}, u32[]{:S(2)}, u32[]{:S(2)}) %collective-permute-start.10) | collective-permute-done | bytes 98336 | tf_op jit(solution)/shard_map/ppermute | solution.py:28
  33.0 1.9 %collective-permute-start.1 = (bf16[512,1280]{1,0:T(8,128)(2,1)S(1)}, bf16[512,1280]{1,0:T(8,128)(2,1)S(1)}, u32[]{:S(2)}, u32[]{:S(2)}) collective-permute-start(bf16[512,1280]{1,0:T(8,128)(2,1)S(1)} %copy-done), channel_id=1, source_target_pairs={{0,1},{1,2},{2,3},{3,0},{4,7},{5,4},{6,5},{7,6},{8,9},{9,10},{10,1... | collective-permute-start | bytes 3932168 | tf_op jit(solution)/shard_map/ppermute | solution.py:28
  34.9 1.4 %collective-permute-start.2 = (bf16[512,1280]{1,0:T(8,128)(2,1)S(1)}, bf16[512,1280]{1,0:T(8,128)(2,1)S(1)}, u32[]{:S(2)}, u32[]{:S(2)}) collective-permute-start(bf16[512,1280]{1,0:T(8,128)(2,1)S(1)} %copy-done), channel_id=1, source_target_pairs={{0,3},{1,0},{2,1},{3,2},{4,5},{5,6},{6,7},{7,4},{8,11},{9,8},{10,9... | collective-permute-start | bytes 3932168 | tf_op jit(solution)/shard_map/ppermute | solution.py:28
  36.2 0.7 collective-permute-start.11
  37.0 0.1 pad_maximum_fusion.2.refs_4_.refs_3_
  37.0 2.4 %collective-permute-start.7 = (bf16[4,128,512]{2,1,0:T(8,128)(2,1)S(1)}, bf16[4,128,512]{2,1,0:T(8,128)(2,1)S(1)}, u32[]{:S(2)}, u32[]{:S(2)}) collective-permute-start(bf16[4,128,512]{2,1,0:T(8,128)(2,1)S(1)} %pad_maximum_fusion.2.refs_4_.refs_3_), channel_id=1, source_target_pairs={{0,8},{4,60},{8,16},{12,4},{16,24},{20,12},{24,32},{28,20},{32,40}... | collective-permute-start | bytes 1572872 | tf_op jit(solution)/shard_map/ppermute | solution.py:28
  39.5 0.8 collective-permute-done.13
  40.3 3.2 %collective-permute-start.15 = (bf16[2,128,768]{2,1,0:T(8,128)(2,1)S(1)}, bf16[2,128,768]{2,1,0:T(8,128)(2,1)S(1)}, u32[]{:S(2)}, u32[]{:S(2)}) collective-permute-start(bf16[2,128,768]{2,1,0:T(8,128)(2,1)S(1)} %collective-permute-done.13), channel_id=1, source_target_pairs={{0,4},{4,0},{1,5},{5,1},{2,6},{6,2},{3,7},{7,3},{8,12},{12,8},{9,1... | collective-permute-start | bytes 1179656 | tf_op jit(solution)/shard_map/ppermute | solution.py:28
  43.5 0.1 select_bitcast_fusion
  43.5 0.1 collective-permute-start.14
  43.7 0.1 pad_maximum_fusion.refs_8_.refs_12_
  43.8 1.0 %collective-permute-done.15 = bf16[2,128,768]{2,1,0:T(8,128)(2,1)S(1)} collective-permute-done((bf16[2,128,768]{2,1,0:T(8,128)(2,1)S(1)}, bf16[2,128,768]{2,1,0:T(8,128)(2,1)S(1)}, u32[]{:S(2)}, u32[]{:S(2)}) %collective-permute-start.15) | collective-permute-done | bytes 393248 | tf_op jit(solution)/shard_map/ppermute | solution.py:28
  44.8 0.3 collective-permute-done.14
  45.1 0.1 pad_maximum_fusion.1.refs_9_.refs_13_
  45.2 0.3 collective-permute-start.16
  45.5 1.7 %collective-permute-start.17 = (bf16[4,128,768]{2,1,0:T(8,128)(2,1)S(1)}, bf16[4,128,768]{2,1,0:T(8,128)(2,1)S(1)}, u32[]{:S(2)}, u32[]{:S(2)}) collective-permute-start(bf16[4,128,768]{2,1,0:T(8,128)(2,1)S(1)} %pad_maximum_fusion.1.refs_9_.refs_13_), channel_id=1, source_target_pairs={{0,64},{4,196},{64,128},{68,4},{128,192},{132,68},{192,0},{196,132... | collective-permute-start | bytes 2359304 | tf_op jit(solution)/shard_map/ppermute | solution.py:28
  47.2 2.4 %collective-permute-done.7.refs_5_.refs_4_ = bf16[4,128,512]{2,1,0:T(8,128)(2,1)S(1)} collective-permute-done((bf16[4,128,512]{2,1,0:T(8,128)(2,1)S(1)}, bf16[4,128,512]{2,1,0:T(8,128)(2,1)S(1)}, u32[]{:S(2)}, u32[]{:S(2)}) %collective-permute-start.7) | collective-permute-done | bytes 524320 | tf_op jit(solution)/shard_map/ppermute | solution.py:28
  49.6 1.4 %collective-permute-start.9 = (bf16[4,128,512]{2,1,0:T(8,128)(2,1)S(1)}, bf16[4,128,512]{2,1,0:T(8,128)(2,1)S(1)}, u32[]{:S(2)}, u32[]{:S(2)}) collective-permute-start(bf16[4,128,512]{2,1,0:T(8,128)(2,1)S(1)} %collective-permute-done.7.refs_5_.refs_4_), channel_id=1, source_target_pairs={{0,8},{4,60},{8,16},{12,4},{16,24},{20,12},{24,32},{28,20},{32,40}... | collective-permute-start | bytes 1572872 | tf_op jit(solution)/shard_map/ppermute | solution.py:28
  51.0 9.0 %collective-permute-done.9.refs_7_.refs_6_ = bf16[4,128,512]{2,1,0:T(8,128)(2,1)S(1)} collective-permute-done((bf16[4,128,512]{2,1,0:T(8,128)(2,1)S(1)}, bf16[4,128,512]{2,1,0:T(8,128)(2,1)S(1)}, u32[]{:S(2)}, u32[]{:S(2)}) %collective-permute-start.9) | collective-permute-done | bytes 524320 | tf_op jit(solution)/shard_map/ppermute | solution.py:28
  60.0 0.2 collective-permute-start.21
  60.2 1.5 %collective-permute-start.18 = (bf16[4,128,768]{2,1,0:T(8,128)(2,1)S(1)}, bf16[4,128,768]{2,1,0:T(8,128)(2,1)S(1)}, u32[]{:S(2)}, u32[]{:S(2)}) collective-permute-start(bf16[4,128,768]{2,1,0:T(8,128)(2,1)S(1)} %collective-permute-done.16.refs_10_.refs_14_), channel_id=1, source_target_pairs={{0,4},{4,0},{1,5},{5,1},{2,6},{6,2},{3,7},{7,3},{8,12},{12,8},{9,1... | collective-permute-start | bytes 2359304 | tf_op jit(solution)/shard_map/ppermute | solution.py:28
  61.7 3.9 %collective-permute-done.17.refs_11_.refs_15_ = bf16[4,128,768]{2,1,0:T(8,128)(2,1)S(1)} collective-permute-done((bf16[4,128,768]{2,1,0:T(8,128)(2,1)S(1)}, bf16[4,128,768]{2,1,0:T(8,128)(2,1)S(1)}, u32[]{:S(2)}, u32[]{:S(2)}) %collective-permute-start.17) | collective-permute-done | bytes 786464 | tf_op jit(solution)/shard_map/ppermute | solution.py:28
  65.7 0.5 collective-permute-start.8
  66.2 0.2 collective-permute-start.20
  66.5 3.9 %collective-permute-done.21.refs_6_.refs_8_ = bf16[4,128,512]{2,1,0:T(8,128)(2,1)S(1)} collective-permute-done((bf16[4,128,512]{2,1,0:T(8,128)(2,1)S(1)}, bf16[4,128,512]{2,1,0:T(8,128)(2,1)S(1)}, u32[]{:S(2)}, u32[]{:S(2)}) %collective-permute-start.21) | collective-permute-done | bytes 524320 | tf_op jit(solution)/shard_map/ppermute | solution.py:28
  70.4 1.9 %collective-permute-start.27 = (bf16[512,1280]{1,0:T(8,128)(2,1)S(1)}, bf16[512,1280]{1,0:T(8,128)(2,1)S(1)}, u32[]{:S(2)}, u32[]{:S(2)}) collective-permute-start(bf16[512,1280]{1,0:T(8,128)(2,1)S(1)} %collective-permute-done.1.refs_2_.refs_3_), channel_id=1, source_target_pairs={{0,1},{1,2},{2,3},{3,0},{4,7},{5,4},{6,5},{7,6},{8,9},{9,10},{10,1... | collective-permute-start | bytes 3932168 | tf_op jit(solution)/shard_map/ppermute | solution.py:28
  72.3 0.1 collective-permute-start.22
  72.4 5.7 %project_near.1.refs_1_ = f32[8,512,128]{2,1,0:T(8,128)S(1)} custom-call(s32[4]{0:T(128)S(1)} %pad_add_fusion.refs_0_, bf16[512,1280]{1,0:T(8,128)(2,1)S(1)} %copy-done, bf16[512,1280]{1,0:T(8,128)(2,1)S(1)} %collective-permute-done.1.refs_2_.refs_3_, bf16[512,1280]{1,0:T(8,128)(2,1)S(1)} %collective-permute-done.2.refs_3_.refs_4_, ...), custom_call_target="tpu_custom_call" | custom-call | flops 450000000 | bytes 450000 | tf_op jit(solution)/shard_map/project_near/pallas_call | solution.py:284
  78.1 1.9 %collective-permute-done.22.refs_8_.refs_10_ = bf16[2,128,512]{2,1,0:T(8,128)(2,1)S(1)} collective-permute-done((bf16[2,128,512]{2,1,0:T(8,128)(2,1)S(1)}, bf16[2,128,512]{2,1,0:T(8,128)(2,1)S(1)}, u32[]{:S(2)}, u32[]{:S(2)}) %collective-permute-start.22) | collective-permute-done | bytes 262176 | tf_op jit(solution)/shard_map/ppermute | solution.py:28
  79.9 0.5 collective-permute-start.23
  80.5 0.5 collective-permute-start.25
  81.0 2.0 %collective-permute-done.23.refs_5_.refs_7_ = bf16[4,128,512]{2,1,0:T(8,128)(2,1)S(1)} collective-permute-done((bf16[4,128,512]{2,1,0:T(8,128)(2,1)S(1)}, bf16[4,128,512]{2,1,0:T(8,128)(2,1)S(1)}, u32[]{:S(2)}, u32[]{:S(2)}) %collective-permute-start.23) | collective-permute-done | bytes 524320 | tf_op jit(solution)/shard_map/ppermute | solution.py:28
  83.0 0.7 collective-permute-done.24.refs_7_.refs_9_
  83.7 0.4 collective-permute-done.25.refs_9_.refs_11_
  84.1 3.8 %project_rest.1.refs_1_ = f32[8,512,128]{2,1,0:T(8,128)S(1)} custom-call(s32[4]{0:T(128)S(1)} %pad_add_fusion.refs_0_, f32[8,512,128]{2,1,0:T(8,128)S(1)} %project_near.1.refs_1_, bf16[512,1280]{1,0:T(8,128)(2,1)S(1)} %copy-done, bf16[512,1280]{1,0:T(8,128)(2,1)S(1)} %collective-permute-done.1.refs_2_.refs_3_, ...), custom_call_target="tpu_custom_call" | custom-call | flops 350000000 | bytes 350000 | tf_op jit(solution)/shard_map/project_rest/pallas_call | solution.py:284
  88.0 1.2 %collective-permute-done.27.refs_2_ = bf16[512,1280]{1,0:T(8,128)(2,1)S(1)} collective-permute-done((bf16[512,1280]{1,0:T(8,128)(2,1)S(1)}, bf16[512,1280]{1,0:T(8,128)(2,1)S(1)}, u32[]{:S(2)}, u32[]{:S(2)}) %collective-permute-start.27) | collective-permute-done | bytes 1310752 | tf_op jit(solution)/shard_map/ppermute | solution.py:28
  89.2 5.8 %project_far_head.1 = bf16[512,1024]{1,0:T(8,128)(2,1)} custom-call(s32[4]{0:T(128)S(1)} %pad_add_fusion.refs_0_, f32[8,512,128]{2,1,0:T(8,128)S(1)} %project_rest.1.refs_1_, bf16[512,1280]{1,0:T(8,128)(2,1)S(1)} %collective-permute-done.27.refs_2_, bf16[4,128,512]{2,1,0:T(8,128)(2,1)S(1)} %pad_maximum_fusion.2.refs_4_.refs_3_, ...), custom_call_target="tpu_custom_call" | custom-call | flops 400000000 | bytes 400000 | tf_op jit(solution)/shard_map/project_far_head/pallas_call | solution.py:284
  (29 shorter events, 0.3 us)
Async XLA Ops:
  0.0 14.3 %collective-permute-start = (bf16[64,1280]{1,0:T(8,128)(2,1)}, bf16[64,1280]{1,0:T(8,128)(2,1)S(1)}, u32[]{:S(2)}, u32[]{:S(2)}) collective-permute-start(bf16[64,1280]{1,0:T(8,128)(2,1)} %bitcast.34), channel_id=1, source_target_pairs={{0,0},{1,64},{2,128},{3,192},{64,1},{65,65},{66,129},{67,193},{128... | collective-permute-start | bytes 491528 | tf_op jit(solution)/shard_map/ppermute | solution.py:28
  14.3 1.4 %collective-permute-start.3 = (bf16[64,1280]{1,0:T(8,128)(2,1)S(1)}, bf16[64,1280]{1,0:T(8,128)(2,1)S(1)}, u32[]{:S(2)}, u32[]{:S(2)}) collective-permute-start(bf16[64,1280]{1,0:T(8,128)(2,1)S(1)} %collective-permute-done), channel_id=1, source_target_pairs={{0,4},{4,0},{1,5},{5,1},{2,6},{6,2},{3,7},{7,3},{8,12},{12,8},{9,1... | collective-permute-start | bytes 491528 | tf_op jit(solution)/shard_map/ppermute | solution.py:28
  14.4 18.6 %copy-start = (bf16[512,1280]{1,0:T(8,128)(2,1)S(1)}, bf16[512,1280]{1,0:T(8,128)(2,1)}, u32[]{:S(2)}) copy-start(bf16[512,1280]{1,0:T(8,128)(2,1)} %attention_backward.1.refs_1_.refs_2_) | copy-start | bytes 3932164
  15.8 14.3 %collective-permute-start.12 = (bf16[128,768]{1,0:T(8,128)(2,1)S(1)}, bf16[128,768]{1,0:T(8,128)(2,1)S(1)}, u32[]{:S(2)}, u32[]{:S(2)}) collective-permute-start(bf16[128,768]{1,0:T(8,128)(2,1)S(1)} %pad_maximum_fusion.4), channel_id=1, source_target_pairs={{0,8},{4,60},{8,16},{12,4},{16,24},{20,12},{24,32},{28,20},{32,40}... | collective-permute-start | bytes 589832 | tf_op jit(solution)/shard_map/ppermute | solution.py:28
  17.8 17.1 %collective-permute-start.4 = (bf16[128,512]{1,0:T(8,128)(2,1)S(1)}, bf16[128,512]{1,0:T(8,128)(2,1)S(1)}, u32[]{:S(2)}, u32[]{:S(2)}) collective-permute-start(bf16[128,512]{1,0:T(8,128)(2,1)S(1)} %pad_maximum_fusion.6), channel_id=1, source_target_pairs={{0,64},{4,196},{64,128},{68,4},{128,192},{132,68},{192,0},{196,132... | collective-permute-start | bytes 393224 | tf_op jit(solution)/shard_map/ppermute | solution.py:28
  20.8 15.4 %collective-permute-start.5 = (bf16[128,512]{1,0:T(8,128)(2,1)S(1)}, bf16[128,512]{1,0:T(8,128)(2,1)S(1)}, u32[]{:S(2)}, u32[]{:S(2)}) collective-permute-start(bf16[128,512]{1,0:T(8,128)(2,1)S(1)} %pad_maximum_fusion.6), channel_id=1, source_target_pairs={{0,128},{4,132},{64,192},{68,196},{128,0},{132,4},{192,64},{196,68... | collective-permute-start | bytes 393224 | tf_op jit(solution)/shard_map/ppermute | solution.py:28
  21.1 15.8 %collective-permute-start.6 = (bf16[128,512]{1,0:T(8,128)(2,1)S(1)}, bf16[128,512]{1,0:T(8,128)(2,1)S(1)}, u32[]{:S(2)}, u32[]{:S(2)}) collective-permute-start(bf16[128,512]{1,0:T(8,128)(2,1)S(1)} %pad_maximum_fusion.6), channel_id=1, source_target_pairs={{0,192},{4,68},{64,0},{68,132},{128,64},{132,196},{192,128},{196,4... | collective-permute-start | bytes 393224 | tf_op jit(solution)/shard_map/ppermute | solution.py:28
  23.8 9.2 %collective-permute-start.10 = (bf16[64,768]{1,0:T(8,128)(2,1)S(1)}, bf16[64,768]{1,0:T(8,128)(2,1)S(1)}, u32[]{:S(2)}, u32[]{:S(2)}) collective-permute-start(bf16[64,768]{1,0:T(8,128)(2,1)S(1)} %constant_dynamic-slice_fusion), channel_id=1, source_target_pairs={{0,32},{4,36},{8,40},{12,44},{16,48},{20,52},{24,56},{28,60},{32,0... | collective-permute-start | bytes 294920 | tf_op jit(solution)/shard_map/ppermute | solution.py:28
  30.2 10.1 %collective-permute-start.13 = (bf16[2,128,768]{2,1,0:T(8,128)(2,1)S(1)}, bf16[2,128,768]{2,1,0:T(8,128)(2,1)S(1)}, u32[]{:S(2)}, u32[]{:S(2)}) collective-permute-start(bf16[2,128,768]{2,1,0:T(8,128)(2,1)S(1)} %pad_maximum_fusion.3), channel_id=1, source_target_pairs={{0,16},{4,52},{8,24},{12,60},{16,32},{20,4},{24,40},{28,12},{32,48... | collective-permute-start | bytes 1179656 | tf_op jit(solution)/shard_map/ppermute | solution.py:28
  33.0 32.7 %collective-permute-start.1 = (bf16[512,1280]{1,0:T(8,128)(2,1)S(1)}, bf16[512,1280]{1,0:T(8,128)(2,1)S(1)}, u32[]{:S(2)}, u32[]{:S(2)}) collective-permute-start(bf16[512,1280]{1,0:T(8,128)(2,1)S(1)} %copy-done), channel_id=1, source_target_pairs={{0,1},{1,2},{2,3},{3,0},{4,7},{5,4},{6,5},{7,6},{8,9},{9,10},{10,1... | collective-permute-start | bytes 3932168 | tf_op jit(solution)/shard_map/ppermute | solution.py:28
  34.9 31.3 %collective-permute-start.2 = (bf16[512,1280]{1,0:T(8,128)(2,1)S(1)}, bf16[512,1280]{1,0:T(8,128)(2,1)S(1)}, u32[]{:S(2)}, u32[]{:S(2)}) collective-permute-start(bf16[512,1280]{1,0:T(8,128)(2,1)S(1)} %copy-done), channel_id=1, source_target_pairs={{0,3},{1,0},{2,1},{3,2},{4,5},{5,6},{6,7},{7,4},{8,11},{9,8},{10,9... | collective-permute-start | bytes 3932168 | tf_op jit(solution)/shard_map/ppermute | solution.py:28
  36.2 3.2 %collective-permute-start.11 = (bf16[64,768]{1,0:T(8,128)(2,1)S(1)}, bf16[64,768]{1,0:T(8,128)(2,1)S(1)}, u32[]{:S(2)}, u32[]{:S(2)}) collective-permute-start(bf16[64,768]{1,0:T(8,128)(2,1)S(1)} %collective-permute-done.10), channel_id=1, source_target_pairs={{0,4},{4,0},{1,5},{5,1},{2,6},{6,2},{3,7},{7,3},{8,12},{12,8},{9,1... | collective-permute-start | bytes 294920 | tf_op jit(solution)/shard_map/ppermute | solution.py:28
  37.0 12.5 %collective-permute-start.7 = (bf16[4,128,512]{2,1,0:T(8,128)(2,1)S(1)}, bf16[4,128,512]{2,1,0:T(8,128)(2,1)S(1)}, u32[]{:S(2)}, u32[]{:S(2)}) collective-permute-start(bf16[4,128,512]{2,1,0:T(8,128)(2,1)S(1)} %pad_maximum_fusion.2.refs_4_.refs_3_), channel_id=1, source_target_pairs={{0,8},{4,60},{8,16},{12,4},{16,24},{20,12},{24,32},{28,20},{32,40}... | collective-permute-start | bytes 1572872 | tf_op jit(solution)/shard_map/ppermute | solution.py:28
  40.3 4.5 %collective-permute-start.15 = (bf16[2,128,768]{2,1,0:T(8,128)(2,1)S(1)}, bf16[2,128,768]{2,1,0:T(8,128)(2,1)S(1)}, u32[]{:S(2)}, u32[]{:S(2)}) collective-permute-start(bf16[2,128,768]{2,1,0:T(8,128)(2,1)S(1)} %collective-permute-done.13), channel_id=1, source_target_pairs={{0,4},{4,0},{1,5},{5,1},{2,6},{6,2},{3,7},{7,3},{8,12},{12,8},{9,1... | collective-permute-start | bytes 1179656 | tf_op jit(solution)/shard_map/ppermute | solution.py:28
  43.5 1.6 %collective-permute-start.14 = (bf16[128,768]{1,0:T(8,128)(2,1)S(1)}, bf16[128,768]{1,0:T(8,128)(2,1)S(1)}, u32[]{:S(2)}, u32[]{:S(2)}) collective-permute-start(bf16[128,768]{1,0:T(8,128)(2,1)S(1)} %collective-permute-done.12), channel_id=1, source_target_pairs={{0,4},{4,0},{1,5},{5,1},{2,6},{6,2},{3,7},{7,3},{8,12},{12,8},{9,1... | collective-permute-start | bytes 589832 | tf_op jit(solution)/shard_map/ppermute | solution.py:28
  45.2 15.0 %collective-permute-start.16 = (bf16[4,128,768]{2,1,0:T(8,128)(2,1)S(1)}, bf16[4,128,768]{2,1,0:T(8,128)(2,1)S(1)}, u32[]{:S(2)}, u32[]{:S(2)}) collective-permute-start(bf16[4,128,768]{2,1,0:T(8,128)(2,1)S(1)} %pad_maximum_fusion.refs_8_.refs_12_), channel_id=1, source_target_pairs={{0,64},{4,196},{64,128},{68,4},{128,192},{132,68},{192,0},{196,132... | collective-permute-start | bytes 2359304 | tf_op jit(solution)/shard_map/ppermute | solution.py:28
  45.5 20.2 %collective-permute-start.17 = (bf16[4,128,768]{2,1,0:T(8,128)(2,1)S(1)}, bf16[4,128,768]{2,1,0:T(8,128)(2,1)S(1)}, u32[]{:S(2)}, u32[]{:S(2)}) collective-permute-start(bf16[4,128,768]{2,1,0:T(8,128)(2,1)S(1)} %pad_maximum_fusion.1.refs_9_.refs_13_), channel_id=1, source_target_pairs={{0,64},{4,196},{64,128},{68,4},{128,192},{132,68},{192,0},{196,132... | collective-permute-start | bytes 2359304 | tf_op jit(solution)/shard_map/ppermute | solution.py:28
  49.6 10.4 %collective-permute-start.9 = (bf16[4,128,512]{2,1,0:T(8,128)(2,1)S(1)}, bf16[4,128,512]{2,1,0:T(8,128)(2,1)S(1)}, u32[]{:S(2)}, u32[]{:S(2)}) collective-permute-start(bf16[4,128,512]{2,1,0:T(8,128)(2,1)S(1)} %collective-permute-done.7.refs_5_.refs_4_), channel_id=1, source_target_pairs={{0,8},{4,60},{8,16},{12,4},{16,24},{20,12},{24,32},{28,20},{32,40}... | collective-permute-start | bytes 1572872 | tf_op jit(solution)/shard_map/ppermute | solution.py:28
  60.0 10.4 %collective-permute-start.21 = (bf16[4,128,512]{2,1,0:T(8,128)(2,1)S(1)}, bf16[4,128,512]{2,1,0:T(8,128)(2,1)S(1)}, u32[]{:S(2)}, u32[]{:S(2)}) collective-permute-start(bf16[4,128,512]{2,1,0:T(8,128)(2,1)S(1)} %collective-permute-done.9.refs_7_.refs_6_), channel_id=1, source_target_pairs={{0,8},{4,60},{8,16},{12,4},{16,24},{20,12},{24,32},{28,20},{32,40}... | collective-permute-start | bytes 1572872 | tf_op jit(solution)/shard_map/ppermute | solution.py:28
  60.2 12.2 %collective-permute-start.18 = (bf16[4,128,768]{2,1,0:T(8,128)(2,1)S(1)}, bf16[4,128,768]{2,1,0:T(8,128)(2,1)S(1)}, u32[]{:S(2)}, u32[]{:S(2)}) collective-permute-start(bf16[4,128,768]{2,1,0:T(8,128)(2,1)S(1)} %collective-permute-done.16.refs_10_.refs_14_), channel_id=1, source_target_pairs={{0,4},{4,0},{1,5},{5,1},{2,6},{6,2},{3,7},{7,3},{8,12},{12,8},{9,1... | collective-permute-start | bytes 2359304 | tf_op jit(solution)/shard_map/ppermute | solution.py:28
  65.7 6.7 %collective-permute-start.19 = (bf16[4,128,768]{2,1,0:T(8,128)(2,1)S(1)}, bf16[4,128,768]{2,1,0:T(8,128)(2,1)S(1)}, u32[]{:S(2)}, u32[]{:S(2)}) collective-permute-start(bf16[4,128,768]{2,1,0:T(8,128)(2,1)S(1)} %collective-permute-done.17.refs_11_.refs_15_), channel_id=1, source_target_pairs={{0,4},{4,0},{1,5},{5,1},{2,6},{6,2},{3,7},{7,3},{8,12},{12,8},{9,1... | collective-permute-start | bytes 2359304 | tf_op jit(solution)/shard_map/ppermute | solution.py:28
  65.7 6.6 %collective-permute-start.8 = (bf16[4,128,512]{2,1,0:T(8,128)(2,1)S(1)}, bf16[4,128,512]{2,1,0:T(8,128)(2,1)S(1)}, u32[]{:S(2)}, u32[]{:S(2)}) collective-permute-start(bf16[4,128,512]{2,1,0:T(8,128)(2,1)S(1)} %collective-permute-done.7.refs_5_.refs_4_), channel_id=1, source_target_pairs={{0,4},{4,0},{1,5},{5,1},{2,6},{6,2},{3,7},{7,3},{8,12},{12,8},{9,1... | collective-permute-start | bytes 1572872 | tf_op jit(solution)/shard_map/ppermute | solution.py:28
  66.2 13.7 %collective-permute-start.20 = (bf16[4,128,768]{2,1,0:T(8,128)(2,1)S(1)}, bf16[4,128,768]{2,1,0:T(8,128)(2,1)S(1)}, u32[]{:S(2)}, u32[]{:S(2)}) collective-permute-start(bf16[4,128,768]{2,1,0:T(8,128)(2,1)S(1)} %collective-permute-done.16.refs_10_.refs_14_), channel_id=1, source_target_pairs={{0,64},{4,196},{64,128},{68,4},{128,192},{132,68},{192,0},{196,132... | collective-permute-start | bytes 2359304 | tf_op jit(solution)/shard_map/ppermute | solution.py:28
  70.4 18.8 %collective-permute-start.27 = (bf16[512,1280]{1,0:T(8,128)(2,1)S(1)}, bf16[512,1280]{1,0:T(8,128)(2,1)S(1)}, u32[]{:S(2)}, u32[]{:S(2)}) collective-permute-start(bf16[512,1280]{1,0:T(8,128)(2,1)S(1)} %collective-permute-done.1.refs_2_.refs_3_), channel_id=1, source_target_pairs={{0,1},{1,2},{2,3},{3,0},{4,7},{5,4},{6,5},{7,6},{8,9},{9,10},{10,1... | collective-permute-start | bytes 3932168 | tf_op jit(solution)/shard_map/ppermute | solution.py:28
  72.3 7.7 %collective-permute-start.22 = (bf16[2,128,512]{2,1,0:T(8,128)(2,1)S(1)}, bf16[2,128,512]{2,1,0:T(8,128)(2,1)S(1)}, u32[]{:S(2)}, u32[]{:S(2)}) collective-permute-start(bf16[2,128,512]{2,1,0:T(8,128)(2,1)S(1)} %slice_select_fusion), channel_id=1, source_target_pairs={{0,8},{4,60},{8,16},{12,4},{16,24},{20,12},{24,32},{28,20},{32,40}... | collective-permute-start | bytes 786440 | tf_op jit(solution)/shard_map/ppermute | solution.py:28
  79.9 4.2 %collective-permute-start.26 = (bf16[4,128,768]{2,1,0:T(8,128)(2,1)S(1)}, bf16[4,128,768]{2,1,0:T(8,128)(2,1)S(1)}, u32[]{:S(2)}, u32[]{:S(2)}) collective-permute-start(bf16[4,128,768]{2,1,0:T(8,128)(2,1)S(1)} %collective-permute-done.20.refs_10_.refs_18_), channel_id=1, source_target_pairs={{0,4},{4,0},{1,5},{5,1},{2,6},{6,2},{3,7},{7,3},{8,12},{12,8},{9,1... | collective-permute-start | bytes 2359304 | tf_op jit(solution)/shard_map/ppermute | solution.py:28
  79.9 3.0 %collective-permute-start.23 = (bf16[4,128,512]{2,1,0:T(8,128)(2,1)S(1)}, bf16[4,128,512]{2,1,0:T(8,128)(2,1)S(1)}, u32[]{:S(2)}, u32[]{:S(2)}) collective-permute-start(bf16[4,128,512]{2,1,0:T(8,128)(2,1)S(1)} %collective-permute-done.9.refs_7_.refs_6_), channel_id=1, source_target_pairs={{0,4},{4,0},{1,5},{5,1},{2,6},{6,2},{3,7},{7,3},{8,12},{12,8},{9,1... | collective-permute-start | bytes 1572872 | tf_op jit(solution)/shard_map/ppermute | solution.py:28
  80.5 3.3 %collective-permute-start.24 = (bf16[4,128,512]{2,1,0:T(8,128)(2,1)S(1)}, bf16[4,128,512]{2,1,0:T(8,128)(2,1)S(1)}, u32[]{:S(2)}, u32[]{:S(2)}) collective-permute-start(bf16[4,128,512]{2,1,0:T(8,128)(2,1)S(1)} %collective-permute-done.21.refs_6_.refs_8_), channel_id=1, source_target_pairs={{0,4},{4,0},{1,5},{5,1},{2,6},{6,2},{3,7},{7,3},{8,12},{12,8},{9,1... | collective-permute-start | bytes 1572872 | tf_op jit(solution)/shard_map/ppermute | solution.py:28
  80.5 3.6 %collective-permute-start.25 = (bf16[2,128,512]{2,1,0:T(8,128)(2,1)S(1)}, bf16[2,128,512]{2,1,0:T(8,128)(2,1)S(1)}, u32[]{:S(2)}, u32[]{:S(2)}) collective-permute-start(bf16[2,128,512]{2,1,0:T(8,128)(2,1)S(1)} %collective-permute-done.22.refs_8_.refs_10_), channel_id=1, source_target_pairs={{0,4},{4,0},{1,5},{5,1},{2,6},{6,2},{3,7},{7,3},{8,12},{12,8},{9,1... | collective-permute-start | bytes 786440 | tf_op jit(solution)/shard_map/ppermute | solution.py:28

commit v6 on v5

--- a/solution.py
+++ b/solution.py
@@ -160,8 +160,9 @@
     for offset in plan.slots:
         slots.append([refs.pop(0), refs.pop(0)] if offset == "far" else [refs.pop(0)])
     rows = [refs.pop(0) for _ in plan.rows]
-    out_ref, ja, jb, wa, far, wb, sems = refs[:7]
-    acc = refs[7] if plan.last else out_ref
+    out_ref, jb = refs[:2]
+    acc = refs[2] if plan.last else out_ref
+    width = heads[0].shape[1]
     split = Y_FIRST
     single = len(plan.joined) == 1
     one_row_head = len(plan.rows) == 2
@@ -175,26 +176,8 @@
     def head_index(head):
         return (x + steps(head) + 4) % 4
 
-    used = [0]
-
-    def copy(source, target):
-        made = pltpu.make_async_copy(source, target, sems.at[used[0]])
-        used[0] += 1
-        return made
-
     def entry(offset, g):
         return ((y - g) * (sign if offset <= 0 else -sign) + 4) % 4
-
-    ahead = [copy(source.at[:, :split], ja.at[index]) for index, source in enumerate(heads)]
-    for index, (sources, offset) in enumerate(zip(slots, plan.slots)):
-        if offset == "far":
-            ahead += [copy(source, far.at[which]) for which, source in enumerate(sources)]
-        elif single:
-            ahead.append(copy(sources[0].at[entry(offset, head_index(plan.joined[0]))], wa.at[index, 0]))
-        else:
-            ahead.append(copy(sources[0], wa.at[index]))
-    for made in ahead:
-        made.start()
 
     meets = []
     for part, same, offset, against in plan.rows:
@@ -208,63 +191,49 @@
     def guarded(sure, index, body):
         body() if sure else pl.when(index >= 0)(body)
 
-    row_heads = []
-    if one_row_head:
+    if not single:
         for position, source in enumerate(heads):
-            made = pltpu.make_async_copy(source.at[:, split:], jb.at[0], sems.at[used[0]])
-            pl.when(meets[0][1] == position)(made.start)
-            row_heads.append(made)
-        used[0] += 1
-    else:
-        row_heads = [copy(source.at[:, split:], jb.at[position]) for position, source in enumerate(heads)]
-        for made in row_heads:
-            made.start()
-    row_copies = []
-    for index, (source, (g, meet, sure)) in enumerate(zip(rows, meets)):
-        made = copy(source, wb.at[index])
-        guarded(sure, meet, made.start)
-        row_copies.append(made)
+            if one_row_head:
+
+                @pl.when(meets[0][1] == position)
+                def _(source=source):
+                    jb[0] = source[:, split:]
+            else:
+                jb[position] = source[:, split:]
 
     if plan.first:
         acc[...] = jnp.zeros_like(acc)
     else:
         acc[...] = acc_in[...]
-
-    for made in ahead:
-        made.wait()
 
     def slot(index, offset, g):
         if offset == "far":
             k = (y - g + 4) % 4
             from_zero = k < 2
             place = jnp.where(from_zero, k, (4 - k) % 4 - 1)
-            return far[jnp.where(jnp.where(from_zero, 0, 1) == c, 0, 1), jnp.maximum(place, 0)]
-        return wa[index, 0 if single else entry(offset, g)]
+            place = jnp.maximum(place, 0)
+            here = jnp.where(from_zero, 0, 1) == c
+            return jnp.where(here, slots[index][0][place], slots[index][1][place])
+        return slots[index][0][entry(offset, g)]
 
     for pair in range(0, len(slots), 2):
         total = None
         for position, head in enumerate(plan.joined):
             g = head_index(head)
             block = jnp.concatenate([slot(pair + k, plan.slots[pair + k], g) for k in range(2)], axis=0)
-            term = nt(ja[position], block)
+            term = nt(heads[position][:, :split], block)
             total = term if total is None else total + term
         for k in range(2):
             offset = plan.slots[pair + k]
             acc[tile(4 if offset == "far" else sign * offset)] += total[:, k * BLOCK:(k + 1) * BLOCK]
 
-    if one_row_head:
-        pl.when(meets[0][1] >= 0)(row_heads[0].wait)
-    else:
-        for made in row_heads:
-            made.wait()
     for index, ((part, same, offset, against), (g, meet, sure)) in enumerate(zip(plan.rows, meets)):
         offsets = slot_offsets(c if same else 1 - c, part)
 
         def body(index=index, meet=meet, offsets=offsets):
-            row_copies[index].wait()
-            left = jb[0] if one_row_head or single else jb[meet]
+            left = heads[0][:, split:] if single else jb[0] if one_row_head else jb[meet]
             for pair in (0, 2):
-                term = nt(left, wb[index, pair:pair + 2].reshape(2 * BLOCK, wb.shape[3]))
+                term = nt(left, rows[index][pair:pair + 2].reshape(2 * BLOCK, width - split))
                 for k in range(2):
                     acc[tile(offsets[pair + k])] += term[:, k * BLOCK:(k + 1) * BLOCK]
 
@@ -283,18 +252,12 @@
     share = (heads * slots + rows) / 40
     return pl.pallas_call(
         lambda *refs: projection_kernel(plan, *refs),
-        in_specs=[pl.BlockSpec(memory_space=pltpu.SMEM)] + [vmem] * kept
-        + [pl.BlockSpec(memory_space=pl.ANY)] * (len(operands) - kept),
+        in_specs=[pl.BlockSpec(memory_space=pltpu.SMEM)] + [vmem] * len(operands),
         out_specs=vmem,
         out_shape=jax.ShapeDtypeStruct((window, columns), jnp.bfloat16) if plan.last
         else jax.ShapeDtypeStruct((8, window, BLOCK), jnp.float32),
         scratch_shapes=[
-            pltpu.VMEM((heads, window, Y_FIRST), jnp.bfloat16),
             pltpu.VMEM((1 if rows == 2 else heads, window, width - Y_FIRST), jnp.bfloat16),
-            pltpu.VMEM((slots, 1 if heads == 1 else 4, BLOCK, Y_FIRST), jnp.bfloat16),
-            pltpu.VMEM((2, 2, BLOCK, Y_FIRST), jnp.bfloat16),
-            pltpu.VMEM((rows, 4, BLOCK, width - Y_FIRST), jnp.bfloat16),
-            pltpu.SemaphoreType.DMA((24,)),
         ] + [pltpu.VMEM((8, window, BLOCK), jnp.float32)] * plan.last,
         compiler_params=pltpu.CompilerParams(vmem_limit_bytes=PROJECT_VMEM),
         cost_estimate=pl.CostEstimate(

time: 95.7 us -> 93.5 us (0.977)
  Pallas kernels: 24.9 us -> 21.4 us
  waiting for transfers between devices: 30.2 us -> 32 us
    pallas_call x3, Pallas kernels: 15.3 us -> 11.8 us  [projection(): pl.pallas_call(lambda *refs: projection_kernel(plan, *refs), in_specs=[pl...]
    ppermute x28, waiting for transfers between devices: 30.2 us -> 32 us  [move(): return lax.ppermute(value, axes, pairs)]
  transfers between devices with their start and end apart: 28 -> 28, of which waited for: 14 -> 14; matrix products, arithmetic and copies ran while one was open for 2% -> 2% of each run, Pallas kernels for 20% -> 19%
where the time goes in v6:
time: 93.5 us; the launch traced here: 93.3 us
  starting transfers between devices  37.8 us (40%)
  waiting for transfers between devices  32 us (34%)
  Pallas kernels  21.4 us (23%)
  local copies, waits for them, and re-layouts  1.41 us (2%)
    ppermute x28, starting transfers between devices, move(): return lax.ppermute(value, axes, pairs)  37.8 us
    ppermute x28, waiting for transfers between devices, move(): return lax.ppermute(value, axes, pairs)  32 us
    pallas_call x3, Pallas kernels, projection(): pl.pallas_call(lambda *refs: projection_kernel(plan, *refs), in_specs=[pl...  11.8 us
    pallas_call x1, Pallas kernels, joined_gradients(): pl.pallas_call(attention_kernel, in_specs=[hbm] * 6 + [vmem], out_specs=v...  9.58 us
  transfers between devices with their start and end apart: 28, of which 14 were waited for; matrix products, arithmetic and copies ran while one was open for 2% of the time, Pallas kernels for 19%

profile of v6, /device:TPU:8, one launch (start us, length us, event | category | flops | bytes accessed | tf_op | source)
XLA Modules:
  0.0 93.3 jit_solution(6208258164284257516)
XLA Ops:
  0.0 3.3 %collective-permute-start = (bf16[64,1280]{1,0:T(8,128)(2,1)}, bf16[64,1280]{1,0:T(8,128)(2,1)S(1)}, u32[]{:S(2)}, u32[]{:S(2)}) collective-permute-start(bf16[64,1280]{1,0:T(8,128)(2,1)} %bitcast.34), channel_id=1, source_target_pairs={{0,0},{1,64},{2,128},{3,192},{64,1},{65,65},{66,129},{67,193},{128... | collective-permute-start | bytes 491528 | tf_op jit(solution)/shard_map/ppermute | solution.py:28
  3.3 1.3 %dynamic_slice.6 = s32[512]{0:T(512)} dynamic-slice(s32[32768]{0:T(1024)} %param.14, s32[]{:T(128)S(6)} %select_n.50), dynamic_slice_sizes={512} | dynamic-slice | bytes 4100 | tf_op jit(solution)/shard_map/dynamic_slice | solution.py:298
  4.6 9.6 %attention_backward.1.refs_1_.refs_2_ = bf16[512,1280]{1,0:T(8,128)(2,1)} custom-call(bf16[512,1024]{1,0:T(8,128)(2,1)} %bitcast.32, bf16[512,1024]{1,0:T(8,128)(2,1)} %bitcast.33, bf16[512,128]{1,0:T(8,128)(2,1)} %bitcast.35, bf16[512,128]{1,0:T(8,128)(2,1)} %bitcast.36, bf16[8,512]{1,0:T(8,128)(2,1)} %bitcast.37, bf16[8,512]{1,0:T(8,128)(2,1)} %bitcast.38, ...), custom_call_target="tpu_custom_call" | custom-call | flops 4000000000 | bytes 4000000 | tf_op jit(solution)/shard_map/attention_backward/pallas_call | solution.py:117
  14.2 0.1 pad_add_fusion.refs_0_
  14.4 1.4 %collective-permute-done.3 = bf16[64,1280]{1,0:T(8,128)(2,1)S(1)} collective-permute-done((bf16[64,1280]{1,0:T(8,128)(2,1)S(1)}, bf16[64,1280]{1,0:T(8,128)(2,1)S(1)}, u32[]{:S(2)}, u32[]{:S(2)}) %collective-permute-start.3) | collective-permute-done | bytes 163872 | tf_op jit(solution)/shard_map/ppermute | solution.py:28
  15.8 2.0 %collective-permute-start.12 = (bf16[128,768]{1,0:T(8,128)(2,1)S(1)}, bf16[128,768]{1,0:T(8,128)(2,1)S(1)}, u32[]{:S(2)}, u32[]{:S(2)}) collective-permute-start(bf16[128,768]{1,0:T(8,128)(2,1)S(1)} %pad_maximum_fusion.4), channel_id=1, source_target_pairs={{0,8},{4,60},{8,16},{12,4},{16,24},{20,12},{24,32},{28,20},{32,40}... | collective-permute-start | bytes 589832 | tf_op jit(solution)/shard_map/ppermute | solution.py:28
  17.8 3.0 %collective-permute-start.4 = (bf16[128,512]{1,0:T(8,128)(2,1)S(1)}, bf16[128,512]{1,0:T(8,128)(2,1)S(1)}, u32[]{:S(2)}, u32[]{:S(2)}) collective-permute-start(bf16[128,512]{1,0:T(8,128)(2,1)S(1)} %pad_maximum_fusion.6), channel_id=1, source_target_pairs={{0,64},{4,196},{64,128},{68,4},{128,192},{132,68},{192,0},{196,132... | collective-permute-start | bytes 393224 | tf_op jit(solution)/shard_map/ppermute | solution.py:28
  20.8 0.3 collective-permute-start.5
  21.1 2.6 %collective-permute-start.6 = (bf16[128,512]{1,0:T(8,128)(2,1)S(1)}, bf16[128,512]{1,0:T(8,128)(2,1)S(1)}, u32[]{:S(2)}, u32[]{:S(2)}) collective-permute-start(bf16[128,512]{1,0:T(8,128)(2,1)S(1)} %pad_maximum_fusion.6), channel_id=1, source_target_pairs={{0,192},{4,68},{64,0},{68,132},{128,64},{132,196},{192,128},{196,4... | collective-permute-start | bytes 393224 | tf_op jit(solution)/shard_map/ppermute | solution.py:28
  23.8 6.4 %collective-permute-start.10 = (bf16[64,768]{1,0:T(8,128)(2,1)S(1)}, bf16[64,768]{1,0:T(8,128)(2,1)S(1)}, u32[]{:S(2)}, u32[]{:S(2)}) collective-permute-start(bf16[64,768]{1,0:T(8,128)(2,1)S(1)} %constant_dynamic-slice_fusion), channel_id=1, source_target_pairs={{0,32},{4,36},{8,40},{12,44},{16,48},{20,52},{24,56},{28,60},{32,0... | collective-permute-start | bytes 294920 | tf_op jit(solution)/shard_map/ppermute | solution.py:28
  30.2 1.6 %collective-permute-start.13 = (bf16[2,128,768]{2,1,0:T(8,128)(2,1)S(1)}, bf16[2,128,768]{2,1,0:T(8,128)(2,1)S(1)}, u32[]{:S(2)}, u32[]{:S(2)}) collective-permute-start(bf16[2,128,768]{2,1,0:T(8,128)(2,1)S(1)} %pad_maximum_fusion.3), channel_id=1, source_target_pairs={{0,16},{4,52},{8,24},{12,60},{16,32},{20,4},{24,40},{28,12},{32,48... | collective-permute-start | bytes 1179656 | tf_op jit(solution)/shard_map/ppermute | solution.py:28
  31.7 1.3 %collective-permute-done.10 = bf16[64,768]{1,0:T(8,128)(2,1)S(1)} collective-permute-done((bf16[64,768]{1,0:T(8,128)(2,1)S(1)}, bf16[64,768]{1,0:T(8,128)(2,1)S(1)}, u32[]{:S(2)}, u32[]{:S(2)}) %collective-permute-start.10) | collective-permute-done | bytes 98336 | tf_op jit(solution)/shard_map/ppermute | solution.py:28
  33.0 1.9 %collective-permute-start.1 = (bf16[512,1280]{1,0:T(8,128)(2,1)S(1)}, bf16[512,1280]{1,0:T(8,128)(2,1)S(1)}, u32[]{:S(2)}, u32[]{:S(2)}) collective-permute-start(bf16[512,1280]{1,0:T(8,128)(2,1)S(1)} %copy-done), channel_id=1, source_target_pairs={{0,1},{1,2},{2,3},{3,0},{4,7},{5,4},{6,5},{7,6},{8,9},{9,10},{10,1... | collective-permute-start | bytes 3932168 | tf_op jit(solution)/shard_map/ppermute | solution.py:28
  34.9 1.4 %collective-permute-start.2 = (bf16[512,1280]{1,0:T(8,128)(2,1)S(1)}, bf16[512,1280]{1,0:T(8,128)(2,1)S(1)}, u32[]{:S(2)}, u32[]{:S(2)}) collective-permute-start(bf16[512,1280]{1,0:T(8,128)(2,1)S(1)} %copy-done), channel_id=1, source_target_pairs={{0,3},{1,0},{2,1},{3,2},{4,5},{5,6},{6,7},{7,4},{8,11},{9,8},{10,9... | collective-permute-start | bytes 3932168 | tf_op jit(solution)/shard_map/ppermute | solution.py:28
  36.2 0.7 collective-permute-start.11
  37.0 0.1 pad_maximum_fusion.2.refs_4_.refs_3_
  37.0 2.4 %collective-permute-start.7 = (bf16[4,128,512]{2,1,0:T(8,128)(2,1)S(1)}, bf16[4,128,512]{2,1,0:T(8,128)(2,1)S(1)}, u32[]{:S(2)}, u32[]{:S(2)}) collective-permute-start(bf16[4,128,512]{2,1,0:T(8,128)(2,1)S(1)} %pad_maximum_fusion.2.refs_4_.refs_3_), channel_id=1, source_target_pairs={{0,8},{4,60},{8,16},{12,4},{16,24},{20,12},{24,32},{28,20},{32,40}... | collective-permute-start | bytes 1572872 | tf_op jit(solution)/shard_map/ppermute | solution.py:28
  39.5 0.8 collective-permute-done.13
  40.3 3.2 %collective-permute-start.15 = (bf16[2,128,768]{2,1,0:T(8,128)(2,1)S(1)}, bf16[2,128,768]{2,1,0:T(8,128)(2,1)S(1)}, u32[]{:S(2)}, u32[]{:S(2)}) collective-permute-start(bf16[2,128,768]{2,1,0:T(8,128)(2,1)S(1)} %collective-permute-done.13), channel_id=1, source_target_pairs={{0,4},{4,0},{1,5},{5,1},{2,6},{6,2},{3,7},{7,3},{8,12},{12,8},{9,1... | collective-permute-start | bytes 1179656 | tf_op jit(solution)/shard_map/ppermute | solution.py:28
  43.5 0.1 select_bitcast_fusion
  43.5 0.1 collective-permute-start.14
  43.7 0.1 pad_maximum_fusion.refs_8_.refs_12_
  43.8 1.0 %collective-permute-done.15 = bf16[2,128,768]{2,1,0:T(8,128)(2,1)S(1)} collective-permute-done((bf16[2,128,768]{2,1,0:T(8,128)(2,1)S(1)}, bf16[2,128,768]{2,1,0:T(8,128)(2,1)S(1)}, u32[]{:S(2)}, u32[]{:S(2)}) %collective-permute-start.15) | collective-permute-done | bytes 393248 | tf_op jit(solution)/shard_map/ppermute | solution.py:28
  44.8 0.3 collective-permute-done.14
  45.1 0.1 pad_maximum_fusion.1.refs_9_.refs_13_
  45.2 0.3 collective-permute-start.16
  45.5 1.7 %collective-permute-start.17 = (bf16[4,128,768]{2,1,0:T(8,128)(2,1)S(1)}, bf16[4,128,768]{2,1,0:T(8,128)(2,1)S(1)}, u32[]{:S(2)}, u32[]{:S(2)}) collective-permute-start(bf16[4,128,768]{2,1,0:T(8,128)(2,1)S(1)} %pad_maximum_fusion.1.refs_9_.refs_13_), channel_id=1, source_target_pairs={{0,64},{4,196},{64,128},{68,4},{128,192},{132,68},{192,0},{196,132... | collective-permute-start | bytes 2359304 | tf_op jit(solution)/shard_map/ppermute | solution.py:28
  47.2 2.4 %collective-permute-done.7.refs_5_.refs_4_ = bf16[4,128,512]{2,1,0:T(8,128)(2,1)S(1)} collective-permute-done((bf16[4,128,512]{2,1,0:T(8,128)(2,1)S(1)}, bf16[4,128,512]{2,1,0:T(8,128)(2,1)S(1)}, u32[]{:S(2)}, u32[]{:S(2)}) %collective-permute-start.7) | collective-permute-done | bytes 524320 | tf_op jit(solution)/shard_map/ppermute | solution.py:28
  49.6 1.4 %collective-permute-start.9 = (bf16[4,128,512]{2,1,0:T(8,128)(2,1)S(1)}, bf16[4,128,512]{2,1,0:T(8,128)(2,1)S(1)}, u32[]{:S(2)}, u32[]{:S(2)}) collective-permute-start(bf16[4,128,512]{2,1,0:T(8,128)(2,1)S(1)} %collective-permute-done.7.refs_5_.refs_4_), channel_id=1, source_target_pairs={{0,8},{4,60},{8,16},{12,4},{16,24},{20,12},{24,32},{28,20},{32,40}... | collective-permute-start | bytes 1572872 | tf_op jit(solution)/shard_map/ppermute | solution.py:28
  51.0 9.0 %collective-permute-done.9.refs_7_.refs_6_ = bf16[4,128,512]{2,1,0:T(8,128)(2,1)S(1)} collective-permute-done((bf16[4,128,512]{2,1,0:T(8,128)(2,1)S(1)}, bf16[4,128,512]{2,1,0:T(8,128)(2,1)S(1)}, u32[]{:S(2)}, u32[]{:S(2)}) %collective-permute-start.9) | collective-permute-done | bytes 524320 | tf_op jit(solution)/shard_map/ppermute | solution.py:28
  60.0 0.2 collective-permute-start.21
  60.2 1.5 %collective-permute-start.18 = (bf16[4,128,768]{2,1,0:T(8,128)(2,1)S(1)}, bf16[4,128,768]{2,1,0:T(8,128)(2,1)S(1)}, u32[]{:S(2)}, u32[]{:S(2)}) collective-permute-start(bf16[4,128,768]{2,1,0:T(8,128)(2,1)S(1)} %collective-permute-done.16.refs_10_.refs_14_), channel_id=1, source_target_pairs={{0,4},{4,0},{1,5},{5,1},{2,6},{6,2},{3,7},{7,3},{8,12},{12,8},{9,1... | collective-permute-start | bytes 2359304 | tf_op jit(solution)/shard_map/ppermute | solution.py:28
  61.7 3.9 %collective-permute-done.17.refs_11_.refs_15_ = bf16[4,128,768]{2,1,0:T(8,128)(2,1)S(1)} collective-permute-done((bf16[4,128,768]{2,1,0:T(8,128)(2,1)S(1)}, bf16[4,128,768]{2,1,0:T(8,128)(2,1)S(1)}, u32[]{:S(2)}, u32[]{:S(2)}) %collective-permute-start.17) | collective-permute-done | bytes 786464 | tf_op jit(solution)/shard_map/ppermute | solution.py:28
  65.7 0.5 collective-permute-start.8
  66.2 0.2 collective-permute-start.20
  66.5 3.9 %collective-permute-done.21.refs_6_.refs_8_ = bf16[4,128,512]{2,1,0:T(8,128)(2,1)S(1)} collective-permute-done((bf16[4,128,512]{2,1,0:T(8,128)(2,1)S(1)}, bf16[4,128,512]{2,1,0:T(8,128)(2,1)S(1)}, u32[]{:S(2)}, u32[]{:S(2)}) %collective-permute-start.21) | collective-permute-done | bytes 524320 | tf_op jit(solution)/shard_map/ppermute | solution.py:28
  70.4 1.9 %collective-permute-start.27 = (bf16[512,1280]{1,0:T(8,128)(2,1)S(1)}, bf16[512,1280]{1,0:T(8,128)(2,1)S(1)}, u32[]{:S(2)}, u32[]{:S(2)}) collective-permute-start(bf16[512,1280]{1,0:T(8,128)(2,1)S(1)} %collective-permute-done.1.refs_2_.refs_3_), channel_id=1, source_target_pairs={{0,1},{1,2},{2,3},{3,0},{4,7},{5,4},{6,5},{7,6},{8,9},{9,10},{10,1... | collective-permute-start | bytes 3932168 | tf_op jit(solution)/shard_map/ppermute | solution.py:28
  72.3 0.1 collective-permute-start.22
  72.4 4.6 %project_near.1.refs_1_ = f32[8,512,128]{2,1,0:T(8,128)S(1)} custom-call(s32[4]{0:T(128)S(1)} %pad_add_fusion.refs_0_, bf16[512,1280]{1,0:T(8,128)(2,1)S(1)} %copy-done, bf16[512,1280]{1,0:T(8,128)(2,1)S(1)} %collective-permute-done.1.refs_2_.refs_3_, bf16[512,1280]{1,0:T(8,128)(2,1)S(1)} %collective-permute-done.2.refs_3_.refs_4_, ...), custom_call_target="tpu_custom_call" | custom-call | flops 450000000 | bytes 450000 | tf_op jit(solution)/shard_map/project_near/pallas_call | solution.py:253
  77.0 3.0 %collective-permute-done.22.refs_8_.refs_10_ = bf16[2,128,512]{2,1,0:T(8,128)(2,1)S(1)} collective-permute-done((bf16[2,128,512]{2,1,0:T(8,128)(2,1)S(1)}, bf16[2,128,512]{2,1,0:T(8,128)(2,1)S(1)}, u32[]{:S(2)}, u32[]{:S(2)}) %collective-permute-start.22) | collective-permute-done | bytes 262176 | tf_op jit(solution)/shard_map/ppermute | solution.py:28
  79.9 0.5 collective-permute-start.23
  80.5 0.5 collective-permute-start.25
  81.0 2.0 %collective-permute-done.23.refs_5_.refs_7_ = bf16[4,128,512]{2,1,0:T(8,128)(2,1)S(1)} collective-permute-done((bf16[4,128,512]{2,1,0:T(8,128)(2,1)S(1)}, bf16[4,128,512]{2,1,0:T(8,128)(2,1)S(1)}, u32[]{:S(2)}, u32[]{:S(2)}) %collective-permute-start.23) | collective-permute-done | bytes 524320 | tf_op jit(solution)/shard_map/ppermute | solution.py:28
  83.0 0.7 collective-permute-done.24.refs_7_.refs_9_
  83.7 0.4 collective-permute-done.25.refs_9_.refs_11_
  84.1 3.1 %project_rest.1.refs_1_ = f32[8,512,128]{2,1,0:T(8,128)S(1)} custom-call(s32[4]{0:T(128)S(1)} %pad_add_fusion.refs_0_, f32[8,512,128]{2,1,0:T(8,128)S(1)} %project_near.1.refs_1_, bf16[512,1280]{1,0:T(8,128)(2,1)S(1)} %copy-done, bf16[512,1280]{1,0:T(8,128)(2,1)S(1)} %collective-permute-done.1.refs_2_.refs_3_, ...), custom_call_target="tpu_custom_call" | custom-call | flops 350000000 | bytes 350000 | tf_op jit(solution)/shard_map/project_rest/pallas_call | solution.py:253
  87.2 2.0 %collective-permute-done.27.refs_2_ = bf16[512,1280]{1,0:T(8,128)(2,1)S(1)} collective-permute-done((bf16[512,1280]{1,0:T(8,128)(2,1)S(1)}, bf16[512,1280]{1,0:T(8,128)(2,1)S(1)}, u32[]{:S(2)}, u32[]{:S(2)}) %collective-permute-start.27) | collective-permute-done | bytes 1310752 | tf_op jit(solution)/shard_map/ppermute | solution.py:28
  89.2 4.1 %project_far_head.1 = bf16[512,1024]{1,0:T(8,128)(2,1)} custom-call(s32[4]{0:T(128)S(1)} %pad_add_fusion.refs_0_, f32[8,512,128]{2,1,0:T(8,128)S(1)} %project_rest.1.refs_1_, bf16[512,1280]{1,0:T(8,128)(2,1)S(1)} %collective-permute-done.27.refs_2_, bf16[4,128,512]{2,1,0:T(8,128)(2,1)S(1)} %pad_maximum_fusion.2.refs_4_.refs_3_, ...), custom_call_target="tpu_custom_call" | custom-call | flops 400000000 | bytes 400000 | tf_op jit(solution)/shard_map/project_far_head/pallas_call | solution.py:253
  (29 shorter events, 0.3 us)
Async XLA Ops:
  0.0 14.3 %collective-permute-start = (bf16[64,1280]{1,0:T(8,128)(2,1)}, bf16[64,1280]{1,0:T(8,128)(2,1)S(1)}, u32[]{:S(2)}, u32[]{:S(2)}) collective-permute-start(bf16[64,1280]{1,0:T(8,128)(2,1)} %bitcast.34), channel_id=1, source_target_pairs={{0,0},{1,64},{2,128},{3,192},{64,1},{65,65},{66,129},{67,193},{128... | collective-permute-start | bytes 491528 | tf_op jit(solution)/shard_map/ppermute | solution.py:28
  14.3 1.4 %collective-permute-start.3 = (bf16[64,1280]{1,0:T(8,128)(2,1)S(1)}, bf16[64,1280]{1,0:T(8,128)(2,1)S(1)}, u32[]{:S(2)}, u32[]{:S(2)}) collective-permute-start(bf16[64,1280]{1,0:T(8,128)(2,1)S(1)} %collective-permute-done), channel_id=1, source_target_pairs={{0,4},{4,0},{1,5},{5,1},{2,6},{6,2},{3,7},{7,3},{8,12},{12,8},{9,1... | collective-permute-start | bytes 491528 | tf_op jit(solution)/shard_map/ppermute | solution.py:28
  14.4 18.6 %copy-start = (bf16[512,1280]{1,0:T(8,128)(2,1)S(1)}, bf16[512,1280]{1,0:T(8,128)(2,1)}, u32[]{:S(2)}) copy-start(bf16[512,1280]{1,0:T(8,128)(2,1)} %attention_backward.1.refs_1_.refs_2_) | copy-start | bytes 3932164
  15.8 14.3 %collective-permute-start.12 = (bf16[128,768]{1,0:T(8,128)(2,1)S(1)}, bf16[128,768]{1,0:T(8,128)(2,1)S(1)}, u32[]{:S(2)}, u32[]{:S(2)}) collective-permute-start(bf16[128,768]{1,0:T(8,128)(2,1)S(1)} %pad_maximum_fusion.4), channel_id=1, source_target_pairs={{0,8},{4,60},{8,16},{12,4},{16,24},{20,12},{24,32},{28,20},{32,40}... | collective-permute-start | bytes 589832 | tf_op jit(solution)/shard_map/ppermute | solution.py:28
  17.8 17.1 %collective-permute-start.4 = (bf16[128,512]{1,0:T(8,128)(2,1)S(1)}, bf16[128,512]{1,0:T(8,128)(2,1)S(1)}, u32[]{:S(2)}, u32[]{:S(2)}) collective-permute-start(bf16[128,512]{1,0:T(8,128)(2,1)S(1)} %pad_maximum_fusion.6), channel_id=1, source_target_pairs={{0,64},{4,196},{64,128},{68,4},{128,192},{132,68},{192,0},{196,132... | collective-permute-start | bytes 393224 | tf_op jit(solution)/shard_map/ppermute | solution.py:28
  20.8 15.4 %collective-permute-start.5 = (bf16[128,512]{1,0:T(8,128)(2,1)S(1)}, bf16[128,512]{1,0:T(8,128)(2,1)S(1)}, u32[]{:S(2)}, u32[]{:S(2)}) collective-permute-start(bf16[128,512]{1,0:T(8,128)(2,1)S(1)} %pad_maximum_fusion.6), channel_id=1, source_target_pairs={{0,128},{4,132},{64,192},{68,196},{128,0},{132,4},{192,64},{196,68... | collective-permute-start | bytes 393224 | tf_op jit(solution)/shard_map/ppermute | solution.py:28
  21.1 15.8 %collective-permute-start.6 = (bf16[128,512]{1,0:T(8,128)(2,1)S(1)}, bf16[128,512]{1,0:T(8,128)(2,1)S(1)}, u32[]{:S(2)}, u32[]{:S(2)}) collective-permute-start(bf16[128,512]{1,0:T(8,128)(2,1)S(1)} %pad_maximum_fusion.6), channel_id=1, source_target_pairs={{0,192},{4,68},{64,0},{68,132},{128,64},{132,196},{192,128},{196,4... | collective-permute-start | bytes 393224 | tf_op jit(solution)/shard_map/ppermute | solution.py:28
  23.8 9.2 %collective-permute-start.10 = (bf16[64,768]{1,0:T(8,128)(2,1)S(1)}, bf16[64,768]{1,0:T(8,128)(2,1)S(1)}, u32[]{:S(2)}, u32[]{:S(2)}) collective-permute-start(bf16[64,768]{1,0:T(8,128)(2,1)S(1)} %constant_dynamic-slice_fusion), channel_id=1, source_target_pairs={{0,32},{4,36},{8,40},{12,44},{16,48},{20,52},{24,56},{28,60},{32,0... | collective-permute-start | bytes 294920 | tf_op jit(solution)/shard_map/ppermute | solution.py:28
  30.2 10.1 %collective-permute-start.13 = (bf16[2,128,768]{2,1,0:T(8,128)(2,1)S(1)}, bf16[2,128,768]{2,1,0:T(8,128)(2,1)S(1)}, u32[]{:S(2)}, u32[]{:S(2)}) collective-permute-start(bf16[2,128,768]{2,1,0:T(8,128)(2,1)S(1)} %pad_maximum_fusion.3), channel_id=1, source_target_pairs={{0,16},{4,52},{8,24},{12,60},{16,32},{20,4},{24,40},{28,12},{32,48... | collective-permute-start | bytes 1179656 | tf_op jit(solution)/shard_map/ppermute | solution.py:28
  33.0 32.7 %collective-permute-start.1 = (bf16[512,1280]{1,0:T(8,128)(2,1)S(1)}, bf16[512,1280]{1,0:T(8,128)(2,1)S(1)}, u32[]{:S(2)}, u32[]{:S(2)}) collective-permute-start(bf16[512,1280]{1,0:T(8,128)(2,1)S(1)} %copy-done), channel_id=1, source_target_pairs={{0,1},{1,2},{2,3},{3,0},{4,7},{5,4},{6,5},{7,6},{8,9},{9,10},{10,1... | collective-permute-start | bytes 3932168 | tf_op jit(solution)/shard_map/ppermute | solution.py:28
  34.9 31.3 %collective-permute-start.2 = (bf16[512,1280]{1,0:T(8,128)(2,1)S(1)}, bf16[512,1280]{1,0:T(8,128)(2,1)S(1)}, u32[]{:S(2)}, u32[]{:S(2)}) collective-permute-start(bf16[512,1280]{1,0:T(8,128)(2,1)S(1)} %copy-done), channel_id=1, source_target_pairs={{0,3},{1,0},{2,1},{3,2},{4,5},{5,6},{6,7},{7,4},{8,11},{9,8},{10,9... | collective-permute-start | bytes 3932168 | tf_op jit(solution)/shard_map/ppermute | solution.py:28
  36.2 3.2 %collective-permute-start.11 = (bf16[64,768]{1,0:T(8,128)(2,1)S(1)}, bf16[64,768]{1,0:T(8,128)(2,1)S(1)}, u32[]{:S(2)}, u32[]{:S(2)}) collective-permute-start(bf16[64,768]{1,0:T(8,128)(2,1)S(1)} %collective-permute-done.10), channel_id=1, source_target_pairs={{0,4},{4,0},{1,5},{5,1},{2,6},{6,2},{3,7},{7,3},{8,12},{12,8},{9,1... | collective-permute-start | bytes 294920 | tf_op jit(solution)/shard_map/ppermute | solution.py:28
  37.0 12.5 %collective-permute-start.7 = (bf16[4,128,512]{2,1,0:T(8,128)(2,1)S(1)}, bf16[4,128,512]{2,1,0:T(8,128)(2,1)S(1)}, u32[]{:S(2)}, u32[]{:S(2)}) collective-permute-start(bf16[4,128,512]{2,1,0:T(8,128)(2,1)S(1)} %pad_maximum_fusion.2.refs_4_.refs_3_), channel_id=1, source_target_pairs={{0,8},{4,60},{8,16},{12,4},{16,24},{20,12},{24,32},{28,20},{32,40}... | collective-permute-start | bytes 1572872 | tf_op jit(solution)/shard_map/ppermute | solution.py:28
  40.3 4.5 %collective-permute-start.15 = (bf16[2,128,768]{2,1,0:T(8,128)(2,1)S(1)}, bf16[2,128,768]{2,1,0:T(8,128)(2,1)S(1)}, u32[]{:S(2)}, u32[]{:S(2)}) collective-permute-start(bf16[2,128,768]{2,1,0:T(8,128)(2,1)S(1)} %collective-permute-done.13), channel_id=1, source_target_pairs={{0,4},{4,0},{1,5},{5,1},{2,6},{6,2},{3,7},{7,3},{8,12},{12,8},{9,1... | collective-permute-start | bytes 1179656 | tf_op jit(solution)/shard_map/ppermute | solution.py:28
  43.5 1.6 %collective-permute-start.14 = (bf16[128,768]{1,0:T(8,128)(2,1)S(1)}, bf16[128,768]{1,0:T(8,128)(2,1)S(1)}, u32[]{:S(2)}, u32[]{:S(2)}) collective-permute-start(bf16[128,768]{1,0:T(8,128)(2,1)S(1)} %collective-permute-done.12), channel_id=1, source_target_pairs={{0,4},{4,0},{1,5},{5,1},{2,6},{6,2},{3,7},{7,3},{8,12},{12,8},{9,1... | collective-permute-start | bytes 589832 | tf_op jit(solution)/shard_map/ppermute | solution.py:28
  45.2 15.0 %collective-permute-start.16 = (bf16[4,128,768]{2,1,0:T(8,128)(2,1)S(1)}, bf16[4,128,768]{2,1,0:T(8,128)(2,1)S(1)}, u32[]{:S(2)}, u32[]{:S(2)}) collective-permute-start(bf16[4,128,768]{2,1,0:T(8,128)(2,1)S(1)} %pad_maximum_fusion.refs_8_.refs_12_), channel_id=1, source_target_pairs={{0,64},{4,196},{64,128},{68,4},{128,192},{132,68},{192,0},{196,132... | collective-permute-start | bytes 2359304 | tf_op jit(solution)/shard_map/ppermute | solution.py:28
  45.5 20.2 %collective-permute-start.17 = (bf16[4,128,768]{2,1,0:T(8,128)(2,1)S(1)}, bf16[4,128,768]{2,1,0:T(8,128)(2,1)S(1)}, u32[]{:S(2)}, u32[]{:S(2)}) collective-permute-start(bf16[4,128,768]{2,1,0:T(8,128)(2,1)S(1)} %pad_maximum_fusion.1.refs_9_.refs_13_), channel_id=1, source_target_pairs={{0,64},{4,196},{64,128},{68,4},{128,192},{132,68},{192,0},{196,132... | collective-permute-start | bytes 2359304 | tf_op jit(solution)/shard_map/ppermute | solution.py:28
  49.6 10.4 %collective-permute-start.9 = (bf16[4,128,512]{2,1,0:T(8,128)(2,1)S(1)}, bf16[4,128,512]{2,1,0:T(8,128)(2,1)S(1)}, u32[]{:S(2)}, u32[]{:S(2)}) collective-permute-start(bf16[4,128,512]{2,1,0:T(8,128)(2,1)S(1)} %collective-permute-done.7.refs_5_.refs_4_), channel_id=1, source_target_pairs={{0,8},{4,60},{8,16},{12,4},{16,24},{20,12},{24,32},{28,20},{32,40}... | collective-permute-start | bytes 1572872 | tf_op jit(solution)/shard_map/ppermute | solution.py:28
  60.0 10.4 %collective-permute-start.21 = (bf16[4,128,512]{2,1,0:T(8,128)(2,1)S(1)}, bf16[4,128,512]{2,1,0:T(8,128)(2,1)S(1)}, u32[]{:S(2)}, u32[]{:S(2)}) collective-permute-start(bf16[4,128,512]{2,1,0:T(8,128)(2,1)S(1)} %collective-permute-done.9.refs_7_.refs_6_), channel_id=1, source_target_pairs={{0,8},{4,60},{8,16},{12,4},{16,24},{20,12},{24,32},{28,20},{32,40}... | collective-permute-start | bytes 1572872 | tf_op jit(solution)/shard_map/ppermute | solution.py:28
  60.2 12.2 %collective-permute-start.18 = (bf16[4,128,768]{2,1,0:T(8,128)(2,1)S(1)}, bf16[4,128,768]{2,1,0:T(8,128)(2,1)S(1)}, u32[]{:S(2)}, u32[]{:S(2)}) collective-permute-start(bf16[4,128,768]{2,1,0:T(8,128)(2,1)S(1)} %collective-permute-done.16.refs_10_.refs_14_), channel_id=1, source_target_pairs={{0,4},{4,0},{1,5},{5,1},{2,6},{6,2},{3,7},{7,3},{8,12},{12,8},{9,1... | collective-permute-start | bytes 2359304 | tf_op jit(solution)/shard_map/ppermute | solution.py:28
  65.7 6.7 %collective-permute-start.19 = (bf16[4,128,768]{2,1,0:T(8,128)(2,1)S(1)}, bf16[4,128,768]{2,1,0:T(8,128)(2,1)S(1)}, u32[]{:S(2)}, u32[]{:S(2)}) collective-permute-start(bf16[4,128,768]{2,1,0:T(8,128)(2,1)S(1)} %collective-permute-done.17.refs_11_.refs_15_), channel_id=1, source_target_pairs={{0,4},{4,0},{1,5},{5,1},{2,6},{6,2},{3,7},{7,3},{8,12},{12,8},{9,1... | collective-permute-start | bytes 2359304 | tf_op jit(solution)/shard_map/ppermute | solution.py:28
  65.7 6.6 %collective-permute-start.8 = (bf16[4,128,512]{2,1,0:T(8,128)(2,1)S(1)}, bf16[4,128,512]{2,1,0:T(8,128)(2,1)S(1)}, u32[]{:S(2)}, u32[]{:S(2)}) collective-permute-start(bf16[4,128,512]{2,1,0:T(8,128)(2,1)S(1)} %collective-permute-done.7.refs_5_.refs_4_), channel_id=1, source_target_pairs={{0,4},{4,0},{1,5},{5,1},{2,6},{6,2},{3,7},{7,3},{8,12},{12,8},{9,1... | collective-permute-start | bytes 1572872 | tf_op jit(solution)/shard_map/ppermute | solution.py:28
  66.2 13.7 %collective-permute-start.20 = (bf16[4,128,768]{2,1,0:T(8,128)(2,1)S(1)}, bf16[4,128,768]{2,1,0:T(8,128)(2,1)S(1)}, u32[]{:S(2)}, u32[]{:S(2)}) collective-permute-start(bf16[4,128,768]{2,1,0:T(8,128)(2,1)S(1)} %collective-permute-done.16.refs_10_.refs_14_), channel_id=1, source_target_pairs={{0,64},{4,196},{64,128},{68,4},{128,192},{132,68},{192,0},{196,132... | collective-permute-start | bytes 2359304 | tf_op jit(solution)/shard_map/ppermute | solution.py:28
  70.4 18.8 %collective-permute-start.27 = (bf16[512,1280]{1,0:T(8,128)(2,1)S(1)}, bf16[512,1280]{1,0:T(8,128)(2,1)S(1)}, u32[]{:S(2)}, u32[]{:S(2)}) collective-permute-start(bf16[512,1280]{1,0:T(8,128)(2,1)S(1)} %collective-permute-done.1.refs_2_.refs_3_), channel_id=1, source_target_pairs={{0,1},{1,2},{2,3},{3,0},{4,7},{5,4},{6,5},{7,6},{8,9},{9,10},{10,1... | collective-permute-start | bytes 3932168 | tf_op jit(solution)/shard_map/ppermute | solution.py:28
  72.3 7.7 %collective-permute-start.22 = (bf16[2,128,512]{2,1,0:T(8,128)(2,1)S(1)}, bf16[2,128,512]{2,1,0:T(8,128)(2,1)S(1)}, u32[]{:S(2)}, u32[]{:S(2)}) collective-permute-start(bf16[2,128,512]{2,1,0:T(8,128)(2,1)S(1)} %slice_select_fusion), channel_id=1, source_target_pairs={{0,8},{4,60},{8,16},{12,4},{16,24},{20,12},{24,32},{28,20},{32,40}... | collective-permute-start | bytes 786440 | tf_op jit(solution)/shard_map/ppermute | solution.py:28
  79.9 4.2 %collective-permute-start.26 = (bf16[4,128,768]{2,1,0:T(8,128)(2,1)S(1)}, bf16[4,128,768]{2,1,0:T(8,128)(2,1)S(1)}, u32[]{:S(2)}, u32[]{:S(2)}) collective-permute-start(bf16[4,128,768]{2,1,0:T(8,128)(2,1)S(1)} %collective-permute-done.20.refs_10_.refs_18_), channel_id=1, source_target_pairs={{0,4},{4,0},{1,5},{5,1},{2,6},{6,2},{3,7},{7,3},{8,12},{12,8},{9,1... | collective-permute-start | bytes 2359304 | tf_op jit(solution)/shard_map/ppermute | solution.py:28
  79.9 3.0 %collective-permute-start.23 = (bf16[4,128,512]{2,1,0:T(8,128)(2,1)S(1)}, bf16[4,128,512]{2,1,0:T(8,128)(2,1)S(1)}, u32[]{:S(2)}, u32[]{:S(2)}) collective-permute-start(bf16[4,128,512]{2,1,0:T(8,128)(2,1)S(1)} %collective-permute-done.9.refs_7_.refs_6_), channel_id=1, source_target_pairs={{0,4},{4,0},{1,5},{5,1},{2,6},{6,2},{3,7},{7,3},{8,12},{12,8},{9,1... | collective-permute-start | bytes 1572872 | tf_op jit(solution)/shard_map/ppermute | solution.py:28
  80.5 3.3 %collective-permute-start.24 = (bf16[4,128,512]{2,1,0:T(8,128)(2,1)S(1)}, bf16[4,128,512]{2,1,0:T(8,128)(2,1)S(1)}, u32[]{:S(2)}, u32[]{:S(2)}) collective-permute-start(bf16[4,128,512]{2,1,0:T(8,128)(2,1)S(1)} %collective-permute-done.21.refs_6_.refs_8_), channel_id=1, source_target_pairs={{0,4},{4,0},{1,5},{5,1},{2,6},{6,2},{3,7},{7,3},{8,12},{12,8},{9,1... | collective-permute-start | bytes 1572872 | tf_op jit(solution)/shard_map/ppermute | solution.py:28
  80.5 3.6 %collective-permute-start.25 = (bf16[2,128,512]{2,1,0:T(8,128)(2,1)S(1)}, bf16[2,128,512]{2,1,0:T(8,128)(2,1)S(1)}, u32[]{:S(2)}, u32[]{:S(2)}) collective-permute-start(bf16[2,128,512]{2,1,0:T(8,128)(2,1)S(1)} %collective-permute-done.22.refs_8_.refs_10_), channel_id=1, source_target_pairs={{0,4},{4,0},{1,5},{5,1},{2,6},{6,2},{3,7},{7,3},{8,12},{12,8},{9,1... | collective-permute-start | bytes 786440 | tf_op jit(solution)/shard_map/ppermute | solution.py:28
